TPU v7x, 512 devices: a whole 4x8x8 slice. The times are simulated.
512 devices in a mesh: row: 16 (over x, y_hi), col: 32 (over z, y_lo, core).
Axes of the slice: x: 4, y: 8 (y_hi: 4, y_lo: 2; y = y_hi * 2 + y_lo), z: 8, core: 2. Of those that a mesh axis runs over, the one named last changes fastest.
Arguments:
- left_factor: float32 [8192, 512], P(('row', 'col')), may hold values from -0.0625 to 0.0625
- left_cotangent: float32 [8192, 512], P(('row', 'col')), may hold values from -80 to 80
- right_factor: float32 [24576, 512], P(('col', 'row')), may hold values from -0.0390625 to 0.0390625
- right_cotangent: float32 [24576, 512], P(('col', 'row')), may hold values from -80 to 80
- singular: float32 [512], replicated, may hold values from 0.5 to 2, as said below
- singular_cotangent: float32 [512], replicated, may hold values from -384 to 384
Outputs:
- matrix_cotangent: float32 [8192, 24576], P('row', 'col')
Inputs may be any that keep to these rules, and one draw needn't show every extreme that they name: `singular`: strictly decreasing; consecutive values differ by at least 0.75 / 512.
All inputs are finite; a program needn't handle non-finite values.
Results may differ from a plain program's by a relative error of at most 0.0003.
Values sent between devices are 32-bit elements; how exact they have to be, the bound alone decides.
No kernel may reach another device: no remote copies, remote signals or barrier semaphores. Data moves between devices by JAX's collectives and lax.ppermute only.
A program may use at most 64 MiB of HBM per device.

v0:
```python
import jax
import jax.numpy as jnp
from jax import lax
from jax.sharding import PartitionSpec as P


def linear_core(gram_left, gram_right, singular):
    squares = singular * singular
    spread = squares[None, :] - squares[:, None]
    size_k = singular.shape[0]
    diagonal = jnp.eye(size_k, dtype=jnp.bool_)
    divided = jnp.where(
        diagonal, jnp.float32(0.0), 1.0 / jnp.where(diagonal, jnp.float32(1.0), spread)
    )
    inverse = 1.0 / singular
    core = divided * (gram_left - gram_left.T) * singular[None, :]
    core = core + singular[:, None] * (divided * (gram_right - gram_right.T))
    return core - gram_left * inverse[None, :] - inverse[:, None] * gram_right.T


def local(left_factor, left_cotangent, right_factor, right_cotangent, singular, singular_cotangent):
    highest = lax.Precision.HIGHEST
    dims = (((1,), (1,)), ((), ()))
    inverse = 1.0 / singular
    right_whole, right_cot_whole = (
        lax.all_gather(right_factor, "row", axis=0, tiled=True),
        lax.all_gather(right_cotangent, "row", axis=0, tiled=True),
    )
    scaled_right = right_cot_whole * inverse[None, :]
    local_left = jnp.dot(
        left_factor.T, left_cotangent, precision=highest, preferred_element_type=jnp.float32
    )
    local_right = jnp.dot(
        right_factor.T, right_cotangent, precision=highest, preferred_element_type=jnp.float32
    )
    gram_left, gram_right = lax.psum((local_left, local_right), ("row", "col"))
    core = linear_core(gram_left, gram_right, singular)
    core = core + jnp.diag(singular_cotangent)
    panel = (
        jnp.dot(left_factor, core, precision=highest, preferred_element_type=jnp.float32)
        + left_cotangent * inverse[None, :]
    )
    pieces = lax.all_gather((panel, left_factor), "col", axis=0, tiled=True)
    result = lax.dot_general(
        pieces[0], right_whole, dims, precision=highest, preferred_element_type=jnp.float32
    )
    return result + lax.dot_general(
        pieces[1], scaled_right, dims, precision=highest, preferred_element_type=jnp.float32
    )


def solution(mesh):
    placed = (
        P(("row", "col"), None),
        P(("row", "col"), None),
        P(("col", "row"), None),
        P(("col", "row"), None),
        P(),
        P(),
    )
    return jax.shard_map(
        local, mesh=mesh, in_specs=placed, out_specs=P("row", "col"), check_vma=False
    )
```

profile of v0, /device:TPU:1, one launch (start us, length us, event | category | flops | bytes accessed | tf_op | source)
XLA Modules:
  0.0 570.3 jit_solution(9918086712655896282)
XLA Ops:
  6.5 0.0 all-reduce.3.cloned.1.call-start
  6.5 2.8 fusion.31
  9.3 2.9 fusion.32
  12.3 0.0 all-reduce.3.cloned.1.call-update
  12.3 0.0 all-gather.11.cloned.1.call-start
  12.3 0.7 all-gather.11.cloned.1.call-update
  13.0 0.0 all-gather.9.cloned.1.call-start
  13.1 0.7 all-gather.9.cloned.1.call-update
  13.8 0.0 all-gather.7.cloned.1.call-start
  13.8 0.5 all-gather.7.cloned.1.call-update
  14.4 0.0 all-gather.5.cloned.1.call-start
  14.4 0.0 copy-done.4
  14.4 285.5 %all-reduce.3.cloned.1.call-done = (f32[512,512]{0,1:T(8,128)}, f32[512,512]{1,0:T(8,128)}) async-done(((f32[512,512]{0,1:T(8,128)}, f32[512,512]{1,0:T(8,128)}), (f32[512,512]{0,1:T(8,128)}, f32[512,512]{1,0:T(8,128)})) %all-reduce.3.cloned.1.call-update) | async-done | bytes 2097168 | tf_op jit(solution)/shard_map/psum | solution.py:36
  300.0 1.6 copy.7
  301.6 0.0 copy-start.1
  301.6 0.0 copy-start.2
  301.6 0.0 copy-start.3
  301.6 0.0 copy-start.5
  301.7 0.0 copy-done
  301.7 1.3 copy.9
  303.0 0.0 copy-done.1
  303.0 0.0 copy-done.2
  303.0 0.0 copy-done.3
  303.0 0.0 copy-done.5
  303.0 3.1 fusion.2
  306.1 0.0 all-gather.5.cloned.1.call-update
  306.1 59.1 %all-gather.11.cloned.1.call-done = f32[512,512]{1,0:T(8,128)} async-done(((f32[16,512]{1,0:T(8,128)}), f32[512,512]{1,0:T(8,128)}) %all-gather.11.cloned.1.call-update) | async-done | bytes 1048592 | tf_op jit(solution)/shard_map/all_gather | solution.py:43
  365.2 60.7 %all-gather.9.cloned.1.call-done = f32[768,512]{1,0:T(8,128)} async-done(((f32[48,512]{1,0:T(8,128)}), f32[768,512]{1,0:T(8,128)}) %all-gather.9.cloned.1.call-update) | async-done | bytes 1572880 | tf_op jit(solution)/shard_map/all_gather | solution.py:27
  425.9 4.4 fusion
  430.3 58.0 %all-gather.7.cloned.1.call-done = f32[768,512]{1,0:T(8,128)} async-done(((f32[48,512]{1,0:T(8,128)}), f32[768,512]{1,0:T(8,128)}) %all-gather.7.cloned.1.call-update) | async-done | bytes 1572880 | tf_op jit(solution)/shard_map/all_gather | solution.py:26
  488.3 69.9 %all-gather.5.cloned.1.call-done = f32[512,512]{1,0:T(8,128)} async-done(((f32[16,512]{1,0:T(8,128)}), f32[512,512]{1,0:T(8,128)}) %all-gather.5.cloned.1.call-update) | async-done | bytes 1048592 | tf_op jit(solution)/shard_map/all_gather | solution.py:43
  558.2 5.6 bitcast_add_fusion
  (3 shorter events, 0.0 us)
Async XLA Ops:
  6.5 293.4 %all-reduce.3.cloned.1.call-start = ((), (), s32[]{:S(2)}) async-start(), calls=%async_computation.4 | async-start | bytes 4194304 | tf_op jit(solution)/shard_map/psum | solution.py:36
  9.3 5.1 copy-start.4
  12.3 352.9 %all-gather.11.cloned.1.call-start = ((), (), s32[]{:S(2)}) async-start(), calls=%async_computation.3 | async-start | bytes 1081344 | tf_op jit(solution)/shard_map/all_gather | solution.py:43
  13.0 412.8 %all-gather.9.cloned.1.call-start = ((), (), s32[]{:S(2)}) async-start(), calls=%async_computation.2 | async-start | bytes 1671168 | tf_op jit(solution)/shard_map/all_gather | solution.py:27
  13.8 474.5 %all-gather.7.cloned.1.call-start = ((), (), s32[]{:S(2)}) async-start(), calls=%async_computation.1 | async-start | bytes 1671168 | tf_op jit(solution)/shard_map/all_gather | solution.py:26
  14.4 543.9 %all-gather.5.cloned.1.call-start = ((), (), s32[]{:S(2)}) async-start(), calls=%async_computation | async-start | bytes 1081344 | tf_op jit(solution)/shard_map/all_gather | solution.py:43
  300.0 1.7 copy-start
  301.6 1.4 copy-start.1
  301.6 1.4 copy-start.2
  301.6 1.3 copy-start.3
  301.6 1.3 copy-start.5
Sparse Core Ops, SparseCore 0:
  12.4 287.5 all-reduce.2
  302.1 63.0 all-gather.10
  368.3 57.5 all-gather.8
  428.8 59.4 all-gather.6
  490.3 67.9 all-gather.4
where the time goes:
time: 571 us; the launch traced here: 570 us
  waiting for transfers between devices  535 us (94%)
  matrix products  18.8 us (3%)
  between operations  13.2 us (2%)
    psum x1, waiting for transfers between devices, local(): gram_left, gram_right = lax.psum((local_left, local_right), ('row', 'col'))  286 us
    all_gather x2, waiting for transfers between devices, local(): pieces = lax.all_gather((panel, left_factor), 'col', axis=0, tiled=True)  129 us
    all_gather x1, waiting for transfers between devices, local(): lax.all_gather(right_cotangent, 'row', axis=0, tiled=True)  60.7 us
    all_gather x1, waiting for transfers between devices, local(): lax.all_gather(right_factor, 'row', axis=0, tiled=True)  58 us
  transfers between devices with their start and end apart: 5, of which 5 were waited for; matrix products, arithmetic and copies ran while one was open for 2% of the time, Pallas kernels for 0%

commit v1 on v0

v1 whole, which is shorter than its diff:
```python
import jax
import jax.numpy as jnp
from jax import lax
from jax.sharding import Mesh
from jax.sharding import PartitionSpec as P

ROW = ("x", "yh")
COL = ("z", "yl", "core")
ALL = ROW + COL
SIZES = (4, 4, 8, 2, 2)
HIGHEST = lax.Precision.HIGHEST


def dot(a, b, contract):
    return lax.dot_general(
        a, b, (contract, ((), ())), precision=HIGHEST, preferred_element_type=jnp.float32
    )


def gather(block, axis, size):
    copies = jnp.broadcast_to(block[None], (size,) + block.shape)
    return lax.all_to_all(copies, axis, 0, 0)


def partial_core(left, left_cot, right, right_cot, singular):
    squares = singular * singular
    spread = squares[None, :] - squares[:, None]
    size_k = singular.shape[0]
    diagonal = jnp.eye(size_k, dtype=jnp.bool_)
    divided = jnp.where(
        diagonal, jnp.float32(0.0), 1.0 / jnp.where(diagonal, jnp.float32(1.0), spread)
    )
    inverse = 1.0 / singular
    rows = ((0,), (0,))
    gram_left = dot(left, left_cot, rows)
    gram_left_t = dot(left_cot, left, rows)
    gram_right = dot(right, right_cot, rows)
    gram_right_t = dot(right_cot, right, rows)
    core = divided * (gram_left - gram_left_t) * singular[None, :]
    core = core + singular[:, None] * (divided * (gram_right - gram_right_t))
    return core - gram_left * inverse[None, :] - inverse[:, None] * gram_right_t


def local(left, left_cot, right, right_cot, singular, singular_cot):
    size_k = singular.shape[0]
    inverse = 1.0 / singular
    n_all = 512
    mine = partial_core(left, left_cot, right, right_cot, singular)
    spread_out = lax.all_to_all(mine.reshape(n_all, 4, 128), ALL, 0, 0)

    left_pair = jnp.concatenate([left, left_cot * inverse[None, :]], axis=1)
    right_pair = jnp.concatenate([right_cot * inverse[None, :], right], axis=1)
    lefts = lax.all_gather(left_pair, COL, axis=0, tiled=True)
    rights = lax.all_gather(right_pair, ROW, axis=0, tiled=True)

    row = jnp.sum(spread_out, axis=0)
    core = gather(row, ALL, n_all).reshape(size_k, size_k) + jnp.diag(singular_cot)

    last = ((1,), (1,))
    flat = dot(lefts, rights, last)
    panel = dot(lefts[:, :size_k], core, ((1,), (0,)))
    return flat + dot(panel, rights[:, size_k:], last)


def solution(mesh):
    fine = Mesh(mesh.devices.reshape(SIZES), ALL)
    placed = (
        P(ROW + COL, None),
        P(ROW + COL, None),
        P(COL + ROW, None),
        P(COL + ROW, None),
        P(),
        P(),
    )
    return jax.shard_map(
        local, mesh=fine, in_specs=placed, out_specs=P(ROW, COL), check_vma=False
    )
```

time: 571 us -> 214 us (0.37)
  waiting for transfers between devices: 535 us -> 74.4 us
  blocking collectives: 0 us -> 97.8 us
  other arithmetic: 0.01 us -> 6.06 us
    psum x1 -> x0, waiting for transfers between devices: 286 us -> none  [local(): gram_left, gram_right = lax.psum((local_left, local_right), ('row', 'col'))]
    all_gather x4 -> x2, waiting for transfers between devices: 248 us -> 74.4 us  [the longest x1 74.3 us: local(): rights = lax.all_gather(right_pair, ROW, axis=0, tiled=True)]
    all_to_all x0 -> x2, blocking collectives: none -> 97.8 us  [the longest x1 55 us: local(): spread_out = lax.all_to_all(mine.reshape(n_all, 4, 128), ALL, 0, 0)]
    dot_general x5 -> x7, matrix products: 18.8 us -> 20.7 us  [dot(): lax.dot_general(a, b, (contract, ((), ())), precision=HIGHEST, preferred_...]
  transfers between devices with their start and end apart: 5 -> 2, of which waited for: 5 -> 1; matrix products, arithmetic and copies ran while one was open for 2% -> 6% of each run, Pallas kernels for 0% -> 0%
where the time goes in v1:
time: 214 us; the launch traced here: 213 us
  blocking collectives  97.8 us (46%)
  waiting for transfers between devices  74.4 us (35%)
  matrix products  20.7 us (10%)
  between operations  13.6 us (6%)
  other arithmetic  6.06 us (3%)
    all_gather x1, waiting for transfers between devices, local(): rights = lax.all_gather(right_pair, ROW, axis=0, tiled=True)  74.3 us
    all_to_all x1, blocking collectives, local(): spread_out = lax.all_to_all(mine.reshape(n_all, 4, 128), ALL, 0, 0)  55 us
    all_to_all x1, blocking collectives, gather(): return lax.all_to_all(copies, axis, 0, 0)  42.8 us
    dot_general x7, matrix products, dot(): lax.dot_general(a, b, (contract, ((), ())), precision=HIGHEST, preferred_...  20.7 us
  transfers between devices with their start and end apart: 2, of which 1 were waited for; matrix products, arithmetic and copies ran while one was open for 6% of the time, Pallas kernels for 0%

profile of v1, /device:TPU:1, one launch (start us, length us, event | category | flops | bytes accessed | tf_op | source)
XLA Modules:
  0.0 213.5 jit_solution(7543045240568604852)
XLA Ops:
  6.5 0.0 all-gather.3.cloned.1.call-start
  6.5 0.7 broadcast_divide_fusion
  7.3 0.8 broadcast_multiply_fusion.1
  8.1 1.4 pad_maximum_fusion.1
  9.5 0.0 all-gather.3.cloned.1.call-update
  9.5 0.0 all-gather.5.cloned.1.call-start
  9.5 0.9 broadcast_multiply_fusion
  10.4 1.6 pad_maximum_fusion
  12.0 0.0 all-gather.5.cloned.1.call-update
  12.1 1.8 fusion.11
  13.9 0.0 copy-done.2
  13.9 0.0 copy-done.3
  13.9 1.0 fusion.12
  14.9 0.0 copy-done.7
  14.9 0.0 copy-start.4
  14.9 0.0 copy-start.5
  14.9 1.1 fusion.8
  16.1 0.0 copy-done.4
  16.1 1.4 fusion.6
  17.5 0.4 copy.7
  17.9 55.0 %all_to_all.10 = f32[512,4,128]{2,1,0:T(4,128)S(1)} all-to-all(f32[512,4,128]{2,1,0:T(4,128)S(1)} %copy.7), channel_id=1, replica_groups=mesh['x'=4,'yh'=4,'z'=8,'yl'=2,'core'=2] {'x','yh','z','yl','core'}, dimensions={0} | all-to-all | bytes 2097152 | tf_op jit(solution)/shard_map/all_to_all | solution.py:49
  72.9 0.5 reduce_sum.9
  73.5 0.1 broadcast_in_dim.36
  73.6 0.0 copy-start.6
  73.6 42.8 %all_to_all.11 = f32[512,4,128]{2,1,0:T(4,128)S(1)} all-to-all(f32[512,4,128]{2,1,0:T(4,128)S(1)} %broadcast_in_dim.36), channel_id=1, replica_groups=mesh['x'=4,'yh'=4,'z'=8,'yl'=2,'core'=2] {'x','yh','z','yl','core'}, dimensions={0} | all-to-all | bytes 2097152 | tf_op jit(solution)/shard_map/all_to_all | solution.py:22
  116.4 0.4 copy.8
  116.8 0.1 bitcast_add_fusion
  116.9 0.0 all-gather.3.cloned.1.call-done
  116.9 4.2 %fusion.9 = f32[512,512]{1,0:T(8,128)} fusion(f32[512,512]{0,1:T(8,128)S(1)} %bitcast_add_fusion, f32[512,1024]{1,0:T(8,128)} %all-gather.3.cloned.1.call-done), kind=kOutput, calls=%fused_computation.12 | convolution fusion | flops 1610612736 | bytes 3145728 | tf_op jit(solution)/shard_map/dot_general | solution.py:15
  121.1 74.3 %all-gather.5.cloned.1.call-done = f32[768,1024]{1,0:T(8,128)} async-done(((f32[48,1024]{1,0:T(8,128)}), f32[768,1024]{1,0:T(8,128)}) %all-gather.5.cloned.1.call-update) | async-done | bytes 3145744 | tf_op jit(solution)/shard_map/all_gather | solution.py:54
  195.4 4.6 %fusion = f32[512,768]{1,0:T(8,128)S(1)} fusion(f32[512,512]{1,0:T(8,128)} %fusion.9, f32[768,1024]{1,0:T(8,128)} %all-gather.5.cloned.1.call-done), kind=kOutput, calls=%fused_computation | convolution fusion | flops 2415919104 | bytes 4194304 | tf_op jit(solution)/shard_map/dot_general | solution.py:15
  200.1 6.5 %convolution_add_fusion = f32[512,768]{1,0:T(8,128)} fusion(f32[512,768]{1,0:T(8,128)S(1)} %fusion, f32[512,1024]{1,0:T(8,128)S(1)} %copy-done.1, f32[768,1024]{1,0:T(8,128)S(1)} %copy-done), kind=kOutput, calls=%fused_computation.2 | convolution fusion | flops 4832231424 | bytes 8388608 | tf_op jit(solution)/shard_map/dot_general | solution.py:15
  (9 shorter events, 0.0 us)
Async XLA Ops:
  6.5 8.4 %copy-start.7 = (f32[512]{0:T(512)S(1)}, f32[512]{0:T(512)}, u32[]{:S(2)}) copy-start(f32[512]{0:T(512)} %param.10) | copy-start | bytes 6148
  6.5 7.3 %copy-start.2 = (f32[48,512]{1,0:T(8,128)S(1)}, f32[48,512]{1,0:T(8,128)}, u32[]{:S(2)}) copy-start(f32[48,512]{1,0:T(8,128)} %param.9) | copy-start | bytes 294916
  6.5 7.3 %copy-start.3 = (f32[48,512]{1,0:T(8,128)S(1)}, f32[48,512]{1,0:T(8,128)}, u32[]{:S(2)}) copy-start(f32[48,512]{1,0:T(8,128)} %param.8) | copy-start | bytes 294916
  6.5 110.3 %all-gather.3.cloned.1.call-start = ((), (), s32[]{:S(2)}) async-start(), calls=%async_computation.2 | async-start | bytes 2162688 | tf_op jit(solution)/shard_map/all_gather | solution.py:53
  9.5 186.0 %all-gather.5.cloned.1.call-start = ((), (), s32[]{:S(2)}) async-start(), calls=%async_computation.3 | async-start | bytes 3342336 | tf_op jit(solution)/shard_map/all_gather | solution.py:54
  14.9 1.2 copy-start.4
  14.9 1.2 copy-start.5
  73.6 43.2 %copy-start.6 = (f32[512]{0:T(512)S(1)}, f32[512]{0:T(512)}, u32[]{:S(2)}) copy-start(f32[512]{0:T(512)} %param.11) | copy-start | bytes 6148
  116.9 83.2 %copy-start.1 = (f32[512,1024]{1,0:T(8,128)S(1)}, f32[512,1024]{1,0:T(8,128)}, u32[]{:S(2)}) copy-start(f32[512,1024]{1,0:T(8,128)} %all-gather.3.cloned.1.call-done) | copy-start | bytes 6291460
  195.4 4.6 %copy-start = (f32[768,1024]{1,0:T(8,128)S(1)}, f32[768,1024]{1,0:T(8,128)}, u32[]{:S(2)}) copy-start(f32[768,1024]{1,0:T(8,128)} %all-gather.5.cloned.1.call-done) | copy-start | bytes 9437188
Sparse Core Ops, SparseCore 0:
  9.6 101.7 all-gather.2
  114.4 80.9 all-gather.4

commit v2 on v1

v2 whole, which is shorter than its diff:
```python
import jax
import jax.numpy as jnp
from jax import lax
from jax.sharding import Mesh
from jax.sharding import PartitionSpec as P

ROW = ("x", "yh")
COL = ("z", "yl", "core")
ALL = ROW + COL
CHIPS = ("x", "yh", "z", "yl")
SIZES = (4, 4, 8, 2, 2)
HIGHEST = lax.Precision.HIGHEST
HIGH = lax.Precision.HIGH
SWAP = [(0, 1), (1, 0)]


def dot(a, b, contract, precision):
    return lax.dot_general(
        a, b, (contract, ((), ())), precision=precision, preferred_element_type=jnp.float32
    )


def gather(block, axis, size):
    copies = jnp.broadcast_to(block[None], (size,) + block.shape)
    return lax.all_to_all(copies, axis, 0, 0)


def swap(block):
    return lax.ppermute(block, "core", SWAP)


def half_core(left, left_cot, right, right_cot, singular, core_index):
    size_k = singular.shape[0]
    half = size_k // 2
    start = core_index * half
    part = lambda a, axis: lax.dynamic_slice_in_dim(a, start, half, axis)
    mine = part(singular, 0)
    spread = (singular * singular)[None, :] - (mine * mine)[:, None]
    diagonal = (start + lax.broadcasted_iota(jnp.int32, (half, size_k), 0)) == (
        lax.broadcasted_iota(jnp.int32, (half, size_k), 1)
    )
    divided = jnp.where(
        diagonal, jnp.float32(0.0), 1.0 / jnp.where(diagonal, jnp.float32(1.0), spread)
    )
    rows = ((0,), (0,))
    gram_left = dot(part(left, 1), left_cot, rows, HIGHEST)
    gram_left_t = dot(part(left_cot, 1), left, rows, HIGHEST)
    gram_right = dot(part(right, 1), right_cot, rows, HIGHEST)
    gram_right_t = dot(part(right_cot, 1), right, rows, HIGHEST)
    across, down = singular[None, :], mine[:, None]
    core = divided * (gram_left * across - gram_left_t * down) * across
    core = core + down * (divided * (gram_right * across - gram_right_t * down))
    return core - gram_left - gram_right_t


def local(left, left_cot, right, right_cot, singular, singular_cot):
    size_k = singular.shape[0]
    n_chips = 256
    half = size_k // 2
    inverse = 1.0 / singular
    core_index = lax.axis_index("core")

    right_pair = jnp.concatenate([right_cot, right], axis=1)
    rights = lax.all_gather(right_pair, ROW, axis=0, tiled=True)

    left_over = left_cot * inverse[None, :]
    left_pair = jnp.concatenate([left, left_over], axis=1)
    lefts = gather(left_pair, ("z", "yl"), 16)
    other_lefts = swap(lefts)

    right_over = right_cot * inverse[None, :]
    sent = jnp.concatenate([left_pair, jnp.concatenate([right, right_over], axis=1)], axis=0)
    got = swap(sent)
    chip_left = jnp.concatenate([sent[:16], got[:16]], axis=0)
    chip_right = jnp.concatenate([sent[16:], got[16:]], axis=0)
    mine = half_core(
        chip_left[:, :size_k],
        chip_left[:, size_k:],
        chip_right[:, :size_k],
        chip_right[:, size_k:],
        singular,
        core_index,
    )
    pieces = lax.all_to_all(mine.reshape(n_chips, 4, 128), CHIPS, 0, 0)
    row = jnp.sum(pieces, axis=0)
    own_half = gather(row, CHIPS, n_chips).reshape(half, size_k)
    other_half = swap(own_half)
    first = core_index == 0
    core = jnp.concatenate(
        [jnp.where(first, own_half, other_half), jnp.where(first, other_half, own_half)], axis=0
    ) + jnp.diag(singular_cot)

    lefts = jnp.stack(
        [jnp.where(first, lefts, other_lefts), jnp.where(first, other_lefts, lefts)], axis=1
    ).reshape(-1, 2 * size_k)
    factor = lefts[:, :size_k]
    last = ((1,), (1,))
    panel = dot(factor, core, ((1,), (0,)), HIGH) + lefts[:, size_k:]
    flat = dot(factor * inverse[None, :], rights[:, :size_k], last, HIGH)
    return flat + dot(panel, rights[:, size_k:], last, HIGH)


def solution(mesh):
    fine = Mesh(mesh.devices.reshape(SIZES), ALL)
    placed = (
        P(ROW + COL, None),
        P(ROW + COL, None),
        P(COL + ROW, None),
        P(COL + ROW, None),
        P(),
        P(),
    )
    return jax.shard_map(
        local, mesh=fine, in_specs=placed, out_specs=P(ROW, COL), check_vma=False
    )
```

time: 214 us -> 165 us (0.77)
  blocking collectives: 97.8 us -> 0 us
  starting transfers between devices: 0.04 us -> 54.5 us
  matrix products: 20.7 us -> 9.74 us
  local copies, waits for them, and re-layouts: 0.92 us -> 4.24 us
    all_to_all x2 -> x0, blocking collectives: 97.8 us -> none  [the longest x1 55 us: local(): spread_out = lax.all_to_all(mine.reshape(n_all, 4, 128), ALL, 0, 0)]
    all_gather x1, waiting for transfers between devices: 74.3 us -> 0.02 us  [local(): rights = lax.all_gather(right_pair, ROW, axis=0, tiled=True)]
    all_to_all x0 -> x3, waiting for transfers between devices: none -> 73.5 us  [the longest x2 51 us: gather(): return lax.all_to_all(copies, axis, 0, 0)]
    all_to_all x0 -> x3, starting transfers between devices: none -> 37.5 us  [the longest x2 20.5 us: gather(): return lax.all_to_all(copies, axis, 0, 0)]
    ppermute x0 -> x3, starting transfers between devices: none -> 17 us  [swap(): return lax.ppermute(block, 'core', SWAP)]
    dot_general x7, matrix products: 20.7 us -> 9.74 us  [dot(): lax.dot_general(a, b, (contract, ((), ())), precision=precision, preferre...]
  transfers between devices with their start and end apart: 2 -> 7, of which waited for: 1 -> 4; matrix products, arithmetic and copies ran while one was open for 6% -> 7% of each run, Pallas kernels for 0% -> 0%
where the time goes in v2:
time: 165 us
  waiting for transfers between devices  75.1 us (46%)
  starting transfers between devices  54.5 us (33%)
  between operations  13.6 us (8%)
  matrix products  9.74 us (6%)
  other arithmetic  7.47 us (5%)
  local copies, waits for them, and re-layouts  4.24 us (3%)
    all_to_all x2, waiting for transfers between devices, gather(): return lax.all_to_all(copies, axis, 0, 0)  51 us
    all_to_all x1, waiting for transfers between devices, local(): pieces = lax.all_to_all(mine.reshape(n_chips, 4, 128), CHIPS, 0, 0)  22.5 us
    all_to_all x2, starting transfers between devices, gather(): return lax.all_to_all(copies, axis, 0, 0)  20.5 us
    all_to_all x1, starting transfers between devices, local(): pieces = lax.all_to_all(mine.reshape(n_chips, 4, 128), CHIPS, 0, 0)  17 us
    ppermute x3, starting transfers between devices, swap(): return lax.ppermute(block, 'core', SWAP)  17 us
    dot_general x7, matrix products, dot(): lax.dot_general(a, b, (contract, ((), ())), precision=precision, preferre...  9.74 us
  transfers between devices with their start and end apart: 7, of which 4 were waited for; matrix products, arithmetic and copies ran while one was open for 7% of the time, Pallas kernels for 0%

profile of v2, /device:TPU:1, one launch (start us, length us, event | category | flops | bytes accessed | tf_op | source)
XLA Modules:
  0.0 164.7 jit_solution(16390082819124307951)
XLA Ops:
  6.5 0.7 broadcast_divide_fusion
  7.2 0.8 broadcast_multiply_fusion.1
  8.0 0.9 broadcast_multiply_fusion
  8.9 0.9 maximum_maximum_fusion
  9.8 8.7 %collective-permute-start.1 = (f32[64,1024]{1,0:T(8,128)S(1)}, f32[64,1024]{1,0:T(8,128)S(1)}, u32[]{:S(2)}, u32[]{:S(2)}) collective-permute-start(f32[64,1024]{1,0:T(8,128)S(1)} %maximum_maximum_fusion), channel_id=1, source_target_pairs={{0,1},{1,0},{2,3},{3,2},{4,5},{5,4},{6,7},{7,6},{8,9},{9,8},{10,11... | collective-permute-start | bytes 786440 | tf_op jit(solution)/shard_map/ppermute | solution.py:29
  18.6 1.6 pad_maximum_fusion.2
  20.2 0.8 fusion.41
  21.1 0.9 pad_maximum_fusion.1
  22.0 0.6 fusion.25
  22.7 0.6 fusion.29
  23.4 0.8 fusion.15
  24.1 0.9 fusion.12
  25.0 1.0 reshape.18
  26.0 17.0 %all-to-all-start.1 = ((f32[256,4,128]{2,1,0:T(4,128)}), f32[256,4,128]{2,1,0:T(4,128)S(1)}, u32[]{:S(2)}, u32[]{:S(2)}) async-start(f32[256,4,128]{2,1,0:T(4,128)} %reshape.18), calls=%async_computation.1 | async-start | bytes 1048576 | tf_op jit(solution)/shard_map/all_to_all | solution.py:84
  43.0 22.5 %all-to-all-done.1 = f32[256,4,128]{2,1,0:T(4,128)S(1)} async-done(((f32[256,4,128]{2,1,0:T(4,128)}), f32[256,4,128]{2,1,0:T(4,128)S(1)}, u32[]{:S(2)}, u32[]{:S(2)}) %all-to-all-start.1) | async-done | bytes 524320 | tf_op jit(solution)/shard_map/all_to_all | solution.py:84
  65.6 1.1 broadcast_in_dim.42
  66.6 4.4 %all-to-all-start = ((f32[16,16,1024]{2,1,0:T(8,128)}), f32[16,16,1024]{2,1,0:T(8,128)S(1)}, u32[]{:S(2)}, u32[]{:S(2)}) async-start(f32[16,16,1024]{2,1,0:T(8,128)} %broadcast_in_dim.42), calls=%async_computation | async-start | bytes 2097152 | tf_op jit(solution)/shard_map/all_to_all | solution.py:25
  71.1 0.3 reduce_sum.9
  71.4 35.0 %all-to-all-done = f32[16,16,1024]{2,1,0:T(8,128)S(1)} async-done(((f32[16,16,1024]{2,1,0:T(8,128)}), f32[16,16,1024]{2,1,0:T(8,128)S(1)}, u32[]{:S(2)}, u32[]{:S(2)}) %all-to-all-start) | async-done | bytes 1048608 | tf_op jit(solution)/shard_map/all_to_all | solution.py:25
  106.3 0.9 broadcast_in_dim.44
  107.2 16.0 %all-to-all-start.2 = ((f32[256,4,128]{2,1,0:T(4,128)}), f32[256,4,128]{2,1,0:T(4,128)S(1)}, u32[]{:S(2)}, u32[]{:S(2)}) async-start(f32[256,4,128]{2,1,0:T(4,128)} %broadcast_in_dim.44), calls=%async_computation.2 | async-start | bytes 1048576 | tf_op jit(solution)/shard_map/all_to_all | solution.py:25
  123.2 3.0 %collective-permute-start = (f32[16,16,1024]{2,1,0:T(8,128)S(1)}, f32[16,16,1024]{2,1,0:T(8,128)S(1)}, u32[]{:S(2)}, u32[]{:S(2)}) collective-permute-start(f32[16,16,1024]{2,1,0:T(8,128)S(1)} %all-to-all-done), channel_id=1, source_target_pairs={{0,1},{1,0},{2,3},{3,2},{4,5},{5,4},{6,7},{7,6},{8,9},{9,8},{10,11... | collective-permute-start | bytes 3145736 | tf_op jit(solution)/shard_map/ppermute | solution.py:29
  126.2 16.0 %all-to-all-done.2 = f32[256,4,128]{2,1,0:T(4,128)S(1)} async-done(((f32[256,4,128]{2,1,0:T(4,128)}), f32[256,4,128]{2,1,0:T(4,128)S(1)}, u32[]{:S(2)}, u32[]{:S(2)}) %all-to-all-start.2) | async-done | bytes 524320 | tf_op jit(solution)/shard_map/all_to_all | solution.py:25
  142.2 0.8 copy.14
  143.1 5.3 %collective-permute-start.2 = (f32[256,512]{1,0:T(8,128)}, f32[256,512]{1,0:T(8,128)S(1)}, u32[]{:S(2)}, u32[]{:S(2)}) collective-permute-start(f32[256,512]{1,0:T(8,128)} %bitcast.15), channel_id=1, source_target_pairs={{0,1},{1,0},{2,3},{3,2},{4,5},{5,4},{6,7},{7,6},{8,9},{9,8},{10,11... | collective-permute-start | bytes 1572872 | tf_op jit(solution)/shard_map/ppermute | solution.py:29
  148.3 1.5 collective-permute-done.2
  150.0 0.2 select_bitcast_fusion.1
  150.2 0.2 pad_maximum_fusion
  150.5 0.4 copy-done.3
  150.9 1.1 convolution_add_fusion
  152.1 3.0 %fusion = f32[512,768]{1,0:T(8,128)S(1)} fusion(f32[512,512]{1,0:T(8,128)S(1)} %convolution_add_fusion, f32[768,1024]{1,0:T(8,128)} %all-gather.2.cloned.1.call-done), kind=kOutput, calls=%fused_computation.1 | convolution fusion | flops 1207959552 | bytes 4194304 | tf_op jit(solution)/shard_map/dot_general | solution.py:18
  155.1 2.7 %fusion.4 = f32[512,768]{1,0:T(8,128)} fusion(f32[512,768]{1,0:T(8,128)S(1)} %fusion, f32[768,1024]{1,0:T(8,128)S(1)} %copy-done, f32[512,1024]{1,0:T(8,128)S(1)} %bitcast.19, f32[512]{0:T(512)S(1)} %get-tuple-element.15), kind=kOutput, calls=%fused_computation.5 | convolution fusion | flops 1208614912 | bytes 5769216 | tf_op jit(solution)/shard_map/dot_general | solution.py:18
  (20 shorter events, 0.2 us)
Async XLA Ops:
  6.5 145.5 %all-gather.2.cloned.1.call-start = ((), (), s32[]{:S(2)}) async-start(), calls=%async_computation.3 | async-start | bytes 3342336 | tf_op jit(solution)/shard_map/all_gather | solution.py:64
  8.0 14.7 %copy-start.1 = (f32[16,512]{1,0:T(8,128)S(1)}, f32[16,512]{1,0:T(8,128)}, u32[]{:S(2)}) copy-start(f32[16,512]{1,0:T(8,128)} %param.6) | copy-start | bytes 98308
  9.8 11.2 %collective-permute-start.1 = (f32[64,1024]{1,0:T(8,128)S(1)}, f32[64,1024]{1,0:T(8,128)S(1)}, u32[]{:S(2)}, u32[]{:S(2)}) collective-permute-start(f32[64,1024]{1,0:T(8,128)S(1)} %maximum_maximum_fusion), channel_id=1, source_target_pairs={{0,1},{1,0},{2,3},{3,2},{4,5},{5,4},{6,7},{7,6},{8,9},{9,8},{10,11... | collective-permute-start | bytes 786440 | tf_op jit(solution)/shard_map/ppermute | solution.py:29
  20.2 3.2 %copy-start.2 = (f32[512]{0:T(512)S(1)}, f32[512]{0:T(512)}, u32[]{:S(2)}) copy-start(f32[512]{0:T(512)} %param.10) | copy-start | bytes 6148
  26.0 39.6 %all-to-all-start.1 = ((f32[256,4,128]{2,1,0:T(4,128)}), f32[256,4,128]{2,1,0:T(4,128)S(1)}, u32[]{:S(2)}, u32[]{:S(2)}) async-start(f32[256,4,128]{2,1,0:T(4,128)} %reshape.18), calls=%async_computation.1 | async-start | bytes 1048576 | tf_op jit(solution)/shard_map/all_to_all | solution.py:84
  66.6 39.7 %all-to-all-start = ((f32[16,16,1024]{2,1,0:T(8,128)}), f32[16,16,1024]{2,1,0:T(8,128)S(1)}, u32[]{:S(2)}, u32[]{:S(2)}) async-start(f32[16,16,1024]{2,1,0:T(8,128)} %broadcast_in_dim.42), calls=%async_computation | async-start | bytes 2097152 | tf_op jit(solution)/shard_map/all_to_all | solution.py:25
  107.2 35.0 %all-to-all-start.2 = ((f32[256,4,128]{2,1,0:T(4,128)}), f32[256,4,128]{2,1,0:T(4,128)S(1)}, u32[]{:S(2)}, u32[]{:S(2)}) async-start(f32[256,4,128]{2,1,0:T(4,128)} %broadcast_in_dim.44), calls=%async_computation.2 | async-start | bytes 1048576 | tf_op jit(solution)/shard_map/all_to_all | solution.py:25
  123.2 26.8 %collective-permute-start = (f32[16,16,1024]{2,1,0:T(8,128)S(1)}, f32[16,16,1024]{2,1,0:T(8,128)S(1)}, u32[]{:S(2)}, u32[]{:S(2)}) collective-permute-start(f32[16,16,1024]{2,1,0:T(8,128)S(1)} %all-to-all-done), channel_id=1, source_target_pairs={{0,1},{1,0},{2,3},{3,2},{4,5},{5,4},{6,7},{7,6},{8,9},{9,8},{10,11... | collective-permute-start | bytes 3145736 | tf_op jit(solution)/shard_map/ppermute | solution.py:29
  143.1 6.8 %collective-permute-start.2 = (f32[256,512]{1,0:T(8,128)}, f32[256,512]{1,0:T(8,128)S(1)}, u32[]{:S(2)}, u32[]{:S(2)}) collective-permute-start(f32[256,512]{1,0:T(8,128)} %bitcast.15), channel_id=1, source_target_pairs={{0,1},{1,0},{2,3},{3,2},{4,5},{5,4},{6,7},{7,6},{8,9},{9,8},{10,11... | collective-permute-start | bytes 1572872 | tf_op jit(solution)/shard_map/ppermute | solution.py:29
  150.2 0.7 copy-start.3
  152.1 3.1 %copy-start = (f32[768,1024]{1,0:T(8,128)S(1)}, f32[768,1024]{1,0:T(8,128)}, u32[]{:S(2)}) copy-start(f32[768,1024]{1,0:T(8,128)} %all-gather.2.cloned.1.call-done) | copy-start | bytes 9437188
Sparse Core Ops, SparseCore 0:
  20.3 84.2 all-gather.1

commit v3 on v2

--- a/solution.py
+++ b/solution.py
@@ -7,7 +7,7 @@
 ROW = ("x", "yh")
 COL = ("z", "yl", "core")
 ALL = ROW + COL
-CHIPS = ("x", "yh", "z", "yl")
+PLANE = ("z", "yl")
 SIZES = (4, 4, 8, 2, 2)
 HIGHEST = lax.Precision.HIGHEST
 HIGH = lax.Precision.HIGH
@@ -53,22 +53,40 @@
     return core - gram_left - gram_right_t
 
 
+def shift(block, axis, size, by):
+    return lax.ppermute(block, axis, [(i, (i + by) % size) for i in range(size)])
+
+
+def near_left(pair):
+    at_low = lax.axis_index("yl") == 0
+    other = shift(pair, "yl", 2, 1)
+    own = jnp.stack([jnp.where(at_low, pair, other), jnp.where(at_low, other, pair)])
+    return shift(own, "z", 8, 1), own, shift(own, "z", 8, -1)
+
+
+def line_left(below, own, above):
+    far_below = shift(jnp.stack([below, own, above]), "z", 8, 3)
+    far_above = shift(jnp.stack([below, own]), "z", 8, -3)
+    ring = [own, above, far_above[0], far_above[1]]
+    ring = ring + [far_below[0], far_below[1], far_below[2], below]
+    ring = jnp.stack(ring + ring)
+    return lax.dynamic_slice_in_dim(ring, 8 - lax.axis_index("z"), 8, 0)
+
+
 def local(left, left_cot, right, right_cot, singular, singular_cot):
     size_k = singular.shape[0]
-    n_chips = 256
     half = size_k // 2
-    inverse = 1.0 / singular
     core_index = lax.axis_index("core")
+    first = core_index == 0
 
     right_pair = jnp.concatenate([right_cot, right], axis=1)
+    right_pair, left, left_cot = lax.optimization_barrier((right_pair, left, left_cot))
     rights = lax.all_gather(right_pair, ROW, axis=0, tiled=True)
 
+    inverse = 1.0 / singular
     left_over = left_cot * inverse[None, :]
+    right_over = right_cot * inverse[None, :]
     left_pair = jnp.concatenate([left, left_over], axis=1)
-    lefts = gather(left_pair, ("z", "yl"), 16)
-    other_lefts = swap(lefts)
-
-    right_over = right_cot * inverse[None, :]
     sent = jnp.concatenate([left_pair, jnp.concatenate([right, right_over], axis=1)], axis=0)
     got = swap(sent)
     chip_left = jnp.concatenate([sent[:16], got[:16]], axis=0)
@@ -81,17 +99,22 @@
         singular,
         core_index,
     )
-    pieces = lax.all_to_all(mine.reshape(n_chips, 4, 128), CHIPS, 0, 0)
-    row = jnp.sum(pieces, axis=0)
-    own_half = gather(row, CHIPS, n_chips).reshape(half, size_k)
+    pieces = lax.all_to_all(mine.reshape(16, 16, size_k), PLANE, 0, 0)
+    near = near_left(left_pair)
+    near, rows = lax.optimization_barrier((near, jnp.sum(pieces, axis=0)))
+    line = line_left(*near)
+    pieces = gather(rows, ROW, 16)
+    line, rows = lax.optimization_barrier((line, jnp.sum(pieces, axis=0)))
+    line = line.reshape(16, 16, 2 * size_k)
+    other_line = swap(line)
+    own_half = gather(rows, PLANE, 16).reshape(half, size_k)
     other_half = swap(own_half)
-    first = core_index == 0
     core = jnp.concatenate(
         [jnp.where(first, own_half, other_half), jnp.where(first, other_half, own_half)], axis=0
     ) + jnp.diag(singular_cot)
 
     lefts = jnp.stack(
-        [jnp.where(first, lefts, other_lefts), jnp.where(first, other_lefts, lefts)], axis=1
+        [jnp.where(first, line, other_line), jnp.where(first, other_line, line)], axis=1
     ).reshape(-1, 2 * size_k)
     factor = lefts[:, :size_k]
     last = ((1,), (1,))

time: 165 us -> 152 us (0.921)
  waiting for transfers between devices: 75.1 us -> 36.8 us
  blocking collectives: 0 us -> 21.7 us
  local copies, waits for them, and re-layouts: 4.24 us -> 9.76 us
  starting transfers between devices: 54.5 us -> 50.1 us
    all_to_all x2 -> x1, waiting for transfers between devices: 51 us -> 15.6 us  [gather(): return lax.all_to_all(copies, axis, 0, 0)]
    all_to_all x1, waiting for transfers between devices: 22.5 us -> 0.01 us  [local(): pieces = lax.all_to_all(mine.reshape(16, 16, size_k), PLANE, 0, 0)]
    all_to_all x0 -> x1, blocking collectives: none -> 21.7 us  [gather(): return lax.all_to_all(copies, axis, 0, 0)]
    ppermute x0 -> x5, waiting for transfers between devices: none -> 20.8 us  [shift(): lax.ppermute(block, axis, [(i, (i + by) % size) for i in range(size)])]
    ppermute x0 -> x5, starting transfers between devices: none -> 18.1 us  [shift(): lax.ppermute(block, axis, [(i, (i + by) % size) for i in range(size)])]
    all_to_all x1, starting transfers between devices: 17 us -> 5.81 us  [local(): pieces = lax.all_to_all(mine.reshape(16, 16, size_k), PLANE, 0, 0)]
    all_to_all x2 -> x1, starting transfers between devices: 20.5 us -> 10.3 us  [gather(): return lax.all_to_all(copies, axis, 0, 0)]
    unnamed x9 -> x17, local copies, waits for them, and re-layouts: 1.27 us -> 6.85 us
  transfers between devices with their start and end apart: 7 -> 11, of which waited for: 4 -> 6; matrix products, arithmetic and copies ran while one was open for 7% -> 12% of each run, Pallas kernels for 0% -> 0%
where the time goes in v3:
time: 152 us; the launch traced here: 151 us
  starting transfers between devices  50.1 us (33%)
  waiting for transfers between devices  36.8 us (24%)
  blocking collectives  21.7 us (14%)
  between operations  13.7 us (9%)
  matrix products  10.5 us (7%)
  local copies, waits for them, and re-layouts  9.76 us (6%)
  other arithmetic  8.6 us (6%)
    all_to_all x1, blocking collectives, gather(): return lax.all_to_all(copies, axis, 0, 0)  21.7 us
    ppermute x5, waiting for transfers between devices, shift(): lax.ppermute(block, axis, [(i, (i + by) % size) for i in range(size)])  20.8 us
    ppermute x5, starting transfers between devices, shift(): lax.ppermute(block, axis, [(i, (i + by) % size) for i in range(size)])  18.1 us
    ppermute x3, starting transfers between devices, swap(): return lax.ppermute(block, 'core', SWAP)  16 us
    all_to_all x1, waiting for transfers between devices, gather(): return lax.all_to_all(copies, axis, 0, 0)  15.6 us
    dot_general x7, matrix products, dot(): lax.dot_general(a, b, (contract, ((), ())), precision=precision, preferre...  10.5 us
    all_to_all x1, starting transfers between devices, gather(): return lax.all_to_all(copies, axis, 0, 0)  10.3 us
    unnamed x17, local copies, waits for them, and re-layouts  6.85 us
  transfers between devices with their start and end apart: 11, of which 6 were waited for; matrix products, arithmetic and copies ran while one was open for 12% of the time, Pallas kernels for 0%

profile of v3, /device:TPU:1, one launch (start us, length us, event | category | flops | bytes accessed | tf_op | source)
XLA Modules:
  0.0 151.2 jit_solution(17550158001539540336)
XLA Ops:
  7.2 1.6 %pad_maximum_fusion.4 = f32[48,1024]{1,0:T(8,128)} fusion(f32[48,512]{1,0:T(8,128)} %param.8, f32[48,512]{1,0:T(8,128)} %param.9), kind=kLoop, calls=%fused_computation.39 | loop fusion | flops 49152 | bytes 393216 | tf_op jit(solution)/shard_map/concatenate | solution.py:82
  8.9 0.9 broadcast_multiply_fusion
  9.8 0.8 broadcast_multiply_fusion.1
  10.5 0.9 maximum_maximum_fusion
  11.5 8.7 %collective-permute-start.3 = (f32[64,1024]{1,0:T(8,128)S(1)}, f32[64,1024]{1,0:T(8,128)S(1)}, u32[]{:S(2)}, u32[]{:S(2)}) collective-permute-start(f32[64,1024]{1,0:T(8,128)S(1)} %maximum_maximum_fusion), channel_id=1, source_target_pairs={{0,1},{1,0},{2,3},{3,2},{4,5},{5,4},{6,7},{7,6},{8,9},{9,8},{10,11... | collective-permute-start | bytes 786440 | tf_op jit(solution)/shard_map/ppermute | solution.py:29
  20.3 0.8 fusion.41
  21.4 0.9 pad_maximum_fusion.1
  23.7 0.8 fusion.15
  24.5 1.7 %fusion.12 = f32[256,512]{1,0:T(8,128)} fusion(f32[256,512]{1,0:T(8,128)S(1)} %fusion.25, f32[256,512]{1,0:T(8,128)S(1)} %fusion.29, f32[256,512]{1,0:T(8,128)S(1)} %fusion.15, f32[256]{0:T(256)S(1)} %get-tuple-element.24, f32[512]{0:T(512)S(1)} %copy-done.2, f32[256]{0:T(256)S(1)} %get-tuple-element.23, f32[512]{0:T(512)S(1)} %get-tuple-element.36, ...), kind=kOutput, calls=%fused_computation.14 | convolution fusion | flops 52035584 | bytes 2202628 | tf_op jit(solution)/shard_map/dot_general | solution.py:18
  26.1 5.8 %all-to-all-start = ((f32[16,16,512]{2,1,0:T(8,128)}), f32[16,16,512]{2,1,0:T(8,128)S(1)}, u32[]{:S(2)}, u32[]{:S(2)}) async-start(f32[16,16,512]{2,1,0:T(8,128)} %bitcast.2), calls=%async_computation | async-start | bytes 1048576 | tf_op jit(solution)/shard_map/all_to_all | solution.py:102
  32.0 3.3 %collective-permute-start = (f32[16,1024]{1,0:T(8,128)S(1)}, f32[16,1024]{1,0:T(8,128)S(1)}, u32[]{:S(2)}, u32[]{:S(2)}) collective-permute-start(f32[16,1024]{1,0:T(8,128)S(1)} %pad_maximum_fusion.7), channel_id=1, source_target_pairs={{0,2},{2,0},{1,3},{3,1},{4,6},{6,4},{5,7},{7,5},{8,10},{10,8},{9,1... | collective-permute-start | bytes 196616 | tf_op jit(solution)/shard_map/ppermute | solution.py:57
  35.3 8.8 %collective-permute-done = f32[16,1024]{1,0:T(8,128)S(1)} collective-permute-done((f32[16,1024]{1,0:T(8,128)S(1)}, f32[16,1024]{1,0:T(8,128)S(1)}, u32[]{:S(2)}, u32[]{:S(2)}) %collective-permute-start) | collective-permute-done | bytes 65568 | tf_op jit(solution)/shard_map/ppermute | solution.py:57
  44.1 3.1 %collective-permute-start.1 = (f32[2,16,1024]{2,1,0:T(8,128)S(1)}, f32[2,16,1024]{2,1,0:T(8,128)S(1)}, u32[]{:S(2)}, u32[]{:S(2)}) collective-permute-start(f32[2,16,1024]{2,1,0:T(8,128)S(1)} %pad_maximum_fusion.5), channel_id=1, source_target_pairs={{0,4},{4,8},{8,12},{12,16},{16,20},{20,24},{24,28},{28,0},{1,5},{5... | collective-permute-start | bytes 393224 | tf_op jit(solution)/shard_map/ppermute | solution.py:57
  47.3 3.3 %collective-permute-start.2 = (f32[2,16,1024]{2,1,0:T(8,128)S(1)}, f32[2,16,1024]{2,1,0:T(8,128)S(1)}, u32[]{:S(2)}, u32[]{:S(2)}) collective-permute-start(f32[2,16,1024]{2,1,0:T(8,128)S(1)} %pad_maximum_fusion.5), channel_id=1, source_target_pairs={{0,28},{4,0},{8,4},{12,8},{16,12},{20,16},{24,20},{28,24},{1,29},{... | collective-permute-start | bytes 393224 | tf_op jit(solution)/shard_map/ppermute | solution.py:57
  50.7 0.8 collective-permute-done.1
  51.4 1.8 %collective-permute-done.2 = f32[2,16,1024]{2,1,0:T(8,128)S(1)} collective-permute-done((f32[2,16,1024]{2,1,0:T(8,128)S(1)}, f32[2,16,1024]{2,1,0:T(8,128)S(1)}, u32[]{:S(2)}, u32[]{:S(2)}) %collective-permute-start.2) | collective-permute-done | bytes 131104 | tf_op jit(solution)/shard_map/ppermute | solution.py:57
  53.3 6.3 %collective-permute-start.5 = (f32[3,2,16,1024]{3,2,1,0:T(8,128)S(1)}, f32[3,2,16,1024]{3,2,1,0:T(8,128)S(1)}, u32[]{:S(2)}, u32[]{:S(2)}) collective-permute-start(f32[3,2,16,1024]{3,2,1,0:T(8,128)S(1)} %pad_maximum_fusion.2), channel_id=1, source_target_pairs={{0,12},{4,16},{8,20},{12,24},{16,28},{20,0},{24,4},{28,8},{1,13},{... | collective-permute-start | bytes 1179656 | tf_op jit(solution)/shard_map/ppermute | solution.py:57
  59.7 2.0 %collective-permute-start.4 = (f32[2,2,16,1024]{3,2,1,0:T(8,128)S(1)}, f32[2,2,16,1024]{3,2,1,0:T(8,128)S(1)}, u32[]{:S(2)}, u32[]{:S(2)}) collective-permute-start(f32[2,2,16,1024]{3,2,1,0:T(8,128)S(1)} %pad_maximum_fusion.3), channel_id=1, source_target_pairs={{0,20},{4,24},{8,28},{12,0},{16,4},{20,8},{24,12},{28,16},{1,21},{... | collective-permute-start | bytes 786440 | tf_op jit(solution)/shard_map/ppermute | solution.py:57
  62.3 0.9 broadcast_in_dim.43
  63.1 10.3 %all-to-all-start.1 = ((f32[16,16,512]{2,1,0:T(8,128)}), f32[16,16,512]{2,1,0:T(8,128)S(1)}, u32[]{:S(2)}, u32[]{:S(2)}) async-start(f32[16,16,512]{2,1,0:T(8,128)} %broadcast_in_dim.43), calls=%async_computation.1 | async-start | bytes 1048576 | tf_op jit(solution)/shard_map/all_to_all | solution.py:25
  74.8 9.4 %collective-permute-done.5 = f32[3,2,16,1024]{3,2,1,0:T(8,128)S(1)} collective-permute-done((f32[3,2,16,1024]{3,2,1,0:T(8,128)S(1)}, f32[3,2,16,1024]{3,2,1,0:T(8,128)S(1)}, u32[]{:S(2)}, u32[]{:S(2)}) %collective-permute-start.5) | collective-permute-done | bytes 393248 | tf_op jit(solution)/shard_map/ppermute | solution.py:57
  84.2 0.8 constant_dynamic-update-slice_fusion.6
  87.7 0.8 constant_dynamic-update-slice_fusion.1
  89.1 1.3 constant_dynamic-slice_fusion
  90.4 15.6 %all-to-all-done.1 = f32[16,16,512]{2,1,0:T(8,128)S(1)} async-done(((f32[16,16,512]{2,1,0:T(8,128)}), f32[16,16,512]{2,1,0:T(8,128)S(1)}, u32[]{:S(2)}, u32[]{:S(2)}) %all-to-all-start.1) | async-done | bytes 524320 | tf_op jit(solution)/shard_map/all_to_all | solution.py:25
  106.0 4.1 %collective-permute-start.6 = (f32[16,16,1024]{2,1,0:T(8,128)S(1)}, f32[16,16,1024]{2,1,0:T(8,128)}, u32[]{:S(2)}, u32[]{:S(2)}) collective-permute-start(f32[16,16,1024]{2,1,0:T(8,128)S(1)} %bitcast.30), channel_id=1, source_target_pairs={{0,1},{1,0},{2,3},{3,2},{4,5},{5,4},{6,7},{7,6},{8,9},{9,8},{10,11... | collective-permute-start | bytes 3145736 | tf_op jit(solution)/shard_map/ppermute | solution.py:29
  110.2 21.7 %all_to_all.15 = f32[16,16,512]{2,1,0:T(8,128)S(1)} all-to-all(f32[16,16,512]{2,1,0:T(8,128)S(1)} %broadcast_in_dim.44), channel_id=1, replica_groups=mesh['x'=4,'yh'=4,'z'=8,'yl'=2,'core'=2] {'z','yl'}, dimensions={0} | all-to-all | bytes 1048576 | tf_op jit(solution)/shard_map/all_to_all | solution.py:25
  131.9 3.1 %collective-permute-start.7 = (f32[256,512]{1,0:T(8,128)S(1)}, f32[256,512]{1,0:T(8,128)S(1)}, u32[]{:S(2)}, u32[]{:S(2)}) collective-permute-start(f32[256,512]{1,0:T(8,128)S(1)} %bitcast.33), channel_id=1, source_target_pairs={{0,1},{1,0},{2,3},{3,2},{4,5},{5,4},{6,7},{7,6},{8,9},{9,8},{10,11... | collective-permute-start | bytes 1572872 | tf_op jit(solution)/shard_map/ppermute | solution.py:29
  135.1 1.5 select_bitcast_fusion.1
  137.5 1.1 convolution_add_fusion
  138.7 3.0 %fusion = f32[512,768]{1,0:T(8,128)S(1)} fusion(f32[512,512]{1,0:T(8,128)S(1)} %convolution_add_fusion, f32[768,1024]{1,0:T(8,128)} %all-gather.2.cloned.1.call-done), kind=kOutput, calls=%fused_computation.1 | convolution fusion | flops 1207959552 | bytes 4194304 | tf_op jit(solution)/shard_map/dot_general | solution.py:18
  141.7 2.7 %fusion.4 = f32[512,768]{1,0:T(8,128)} fusion(f32[512,768]{1,0:T(8,128)S(1)} %fusion, f32[768,1024]{1,0:T(8,128)S(1)} %copy-done, f32[512,1024]{1,0:T(8,128)S(1)} %bitcast.29, f32[512]{0:T(512)S(1)} %get-tuple-element.35), kind=kOutput, calls=%fused_computation.5 | convolution fusion | flops 1208614912 | bytes 5769216 | tf_op jit(solution)/shard_map/dot_general | solution.py:18
  (43 shorter events, 8.9 us)
Async XLA Ops:
  6.5 132.1 %all-gather.2.cloned.1.call-start = ((), (), s32[]{:S(2)}) async-start(), calls=%async_computation.3 | async-start | bytes 3342336 | tf_op jit(solution)/shard_map/all_gather | solution.py:84
  7.2 15.8 %copy-start.1 = (f32[16,512]{1,0:T(8,128)S(1)}, f32[16,512]{1,0:T(8,128)}, u32[]{:S(2)}) copy-start(f32[16,512]{1,0:T(8,128)} %param.6) | copy-start | bytes 98308
  11.5 12.2 %copy-start.2 = (f32[512]{0:T(512)S(1)}, f32[512]{0:T(512)}, u32[]{:S(2)}) copy-start(f32[512]{0:T(512)} %param.10) | copy-start | bytes 6148
  11.5 9.9 %collective-permute-start.3 = (f32[64,1024]{1,0:T(8,128)S(1)}, f32[64,1024]{1,0:T(8,128)S(1)}, u32[]{:S(2)}, u32[]{:S(2)}) collective-permute-start(f32[64,1024]{1,0:T(8,128)S(1)} %maximum_maximum_fusion), channel_id=1, source_target_pairs={{0,1},{1,0},{2,3},{3,2},{4,5},{5,4},{6,7},{7,6},{8,9},{9,8},{10,11... | collective-permute-start | bytes 786440 | tf_op jit(solution)/shard_map/ppermute | solution.py:29
  26.1 24.5 %all-to-all-start = ((f32[16,16,512]{2,1,0:T(8,128)}), f32[16,16,512]{2,1,0:T(8,128)S(1)}, u32[]{:S(2)}, u32[]{:S(2)}) async-start(f32[16,16,512]{2,1,0:T(8,128)} %bitcast.2), calls=%async_computation | async-start | bytes 1048576 | tf_op jit(solution)/shard_map/all_to_all | solution.py:102
  32.0 12.1 %collective-permute-start = (f32[16,1024]{1,0:T(8,128)S(1)}, f32[16,1024]{1,0:T(8,128)S(1)}, u32[]{:S(2)}, u32[]{:S(2)}) collective-permute-start(f32[16,1024]{1,0:T(8,128)S(1)} %pad_maximum_fusion.7), channel_id=1, source_target_pairs={{0,2},{2,0},{1,3},{3,1},{4,6},{6,4},{5,7},{7,5},{8,10},{10,8},{9,1... | collective-permute-start | bytes 196616 | tf_op jit(solution)/shard_map/ppermute | solution.py:57
  44.1 7.3 %collective-permute-start.1 = (f32[2,16,1024]{2,1,0:T(8,128)S(1)}, f32[2,16,1024]{2,1,0:T(8,128)S(1)}, u32[]{:S(2)}, u32[]{:S(2)}) collective-permute-start(f32[2,16,1024]{2,1,0:T(8,128)S(1)} %pad_maximum_fusion.5), channel_id=1, source_target_pairs={{0,4},{4,8},{8,12},{12,16},{16,20},{20,24},{24,28},{28,0},{1,5},{5... | collective-permute-start | bytes 393224 | tf_op jit(solution)/shard_map/ppermute | solution.py:57
  47.3 6.0 %collective-permute-start.2 = (f32[2,16,1024]{2,1,0:T(8,128)S(1)}, f32[2,16,1024]{2,1,0:T(8,128)S(1)}, u32[]{:S(2)}, u32[]{:S(2)}) collective-permute-start(f32[2,16,1024]{2,1,0:T(8,128)S(1)} %pad_maximum_fusion.5), channel_id=1, source_target_pairs={{0,28},{4,0},{8,4},{12,8},{16,12},{20,16},{24,20},{28,24},{1,29},{... | collective-permute-start | bytes 393224 | tf_op jit(solution)/shard_map/ppermute | solution.py:57
  53.3 30.9 %collective-permute-start.5 = (f32[3,2,16,1024]{3,2,1,0:T(8,128)S(1)}, f32[3,2,16,1024]{3,2,1,0:T(8,128)S(1)}, u32[]{:S(2)}, u32[]{:S(2)}) collective-permute-start(f32[3,2,16,1024]{3,2,1,0:T(8,128)S(1)} %pad_maximum_fusion.2), channel_id=1, source_target_pairs={{0,12},{4,16},{8,20},{12,24},{16,28},{20,0},{24,4},{28,8},{1,13},{... | collective-permute-start | bytes 1179656 | tf_op jit(solution)/shard_map/ppermute | solution.py:57
  59.7 14.4 %collective-permute-start.4 = (f32[2,2,16,1024]{3,2,1,0:T(8,128)S(1)}, f32[2,2,16,1024]{3,2,1,0:T(8,128)S(1)}, u32[]{:S(2)}, u32[]{:S(2)}) collective-permute-start(f32[2,2,16,1024]{3,2,1,0:T(8,128)S(1)} %pad_maximum_fusion.3), channel_id=1, source_target_pairs={{0,20},{4,24},{8,28},{12,0},{16,4},{20,8},{24,12},{28,16},{1,21},{... | collective-permute-start | bytes 786440 | tf_op jit(solution)/shard_map/ppermute | solution.py:57
  63.1 42.9 %all-to-all-start.1 = ((f32[16,16,512]{2,1,0:T(8,128)}), f32[16,16,512]{2,1,0:T(8,128)S(1)}, u32[]{:S(2)}, u32[]{:S(2)}) async-start(f32[16,16,512]{2,1,0:T(8,128)} %broadcast_in_dim.43), calls=%async_computation.1 | async-start | bytes 1048576 | tf_op jit(solution)/shard_map/all_to_all | solution.py:25
  106.0 29.0 %collective-permute-start.6 = (f32[16,16,1024]{2,1,0:T(8,128)S(1)}, f32[16,16,1024]{2,1,0:T(8,128)}, u32[]{:S(2)}, u32[]{:S(2)}) collective-permute-start(f32[16,16,1024]{2,1,0:T(8,128)S(1)} %bitcast.30), channel_id=1, source_target_pairs={{0,1},{1,0},{2,3},{3,2},{4,5},{5,4},{6,7},{7,6},{8,9},{9,8},{10,11... | collective-permute-start | bytes 3145736 | tf_op jit(solution)/shard_map/ppermute | solution.py:29
  131.9 4.9 %collective-permute-start.7 = (f32[256,512]{1,0:T(8,128)S(1)}, f32[256,512]{1,0:T(8,128)S(1)}, u32[]{:S(2)}, u32[]{:S(2)}) collective-permute-start(f32[256,512]{1,0:T(8,128)S(1)} %bitcast.33), channel_id=1, source_target_pairs={{0,1},{1,0},{2,3},{3,2},{4,5},{5,4},{6,7},{7,6},{8,9},{9,8},{10,11... | collective-permute-start | bytes 1572872 | tf_op jit(solution)/shard_map/ppermute | solution.py:29
  136.8 0.7 copy-start.3
  138.6 3.1 %copy-start = (f32[768,1024]{1,0:T(8,128)S(1)}, f32[768,1024]{1,0:T(8,128)}, u32[]{:S(2)}) copy-start(f32[768,1024]{1,0:T(8,128)} %all-gather.2.cloned.1.call-done) | copy-start | bytes 9437188
Sparse Core Ops, SparseCore 0:
  20.4 82.7 all-gather.1

commit v4 on v1

v4 whole, which is shorter than its diff:
```python
import jax
import jax.numpy as jnp
from jax import lax
from jax.experimental import pallas as pl
from jax.experimental.pallas import tpu as pltpu
from jax.sharding import Mesh
from jax.sharding import PartitionSpec as P

ROW = ("x", "yh")
COL = ("z", "yl", "core")
ALL = ROW + COL
OUTER = ("x", "z")
INNER = ("yh", "yl")
SIZES = (4, 4, 8, 2, 2)
SIZE_K = 512
HALF = 256
HIGHEST = lax.Precision.HIGHEST
HIGH = lax.Precision.HIGH
SWAP = [(0, 1), (1, 0)]


def dot(a, b, contract, precision):
    return lax.dot_general(
        a, b, (contract, ((), ())), precision=precision, preferred_element_type=jnp.float32
    )


def gather(block, axis, size):
    copies = jnp.broadcast_to(block[None], (size,) + block.shape)
    return lax.all_to_all(copies, axis, 0, 0)


def shift(block, axis, size, by):
    return lax.ppermute(block, axis, [(i, (i + by) % size) for i in range(size)])


def swap(block):
    return lax.ppermute(block, "core", SWAP)


def pack_kernel(left, left_cot, right, right_cot, right_pair, left_pair, stacked):
    right_pair[:, :SIZE_K] = right_cot[...]
    right_pair[:, SIZE_K:] = right[...]
    left_pair[:, :SIZE_K] = left[...]
    left_pair[:, SIZE_K:] = left_cot[...]
    stacked[:48, :SIZE_K] = right_cot[...]
    stacked[:48, SIZE_K:] = right[...]
    stacked[48:, :SIZE_K] = left[...]
    stacked[48:, SIZE_K:] = left_cot[...]


def pack(left, left_cot, right, right_cot):
    shapes = ((48, 1024), (16, 1024), (64, 1024))
    return pl.pallas_call(
        pack_kernel,
        out_shape=[jax.ShapeDtypeStruct(s, jnp.float32) for s in shapes],
        cost_estimate=pl.CostEstimate(flops=0, bytes_accessed=1 << 20, transcendentals=0),
        name="pack",
    )(left, left_cot, right, right_cot)


def half_core_kernel(core_index, own, got, s_row, out, lhs, rhs, lhs2, rhs2):
    begin = pl.multiple_of(core_index[0] * HALF, HALF)
    half = pl.ds(begin, HALF)
    cot_half = pl.ds(pl.multiple_of(begin + SIZE_K, HALF), HALF)
    s_all = s_row[...]
    s_half = s_row[:, half]
    inv_all = 1.0 / s_all
    inv_half = 1.0 / s_half
    for i, block in enumerate((own, got)):
        left = pl.ds(16 * i, 16)
        lhs[left, :] = block[48:, half]
        rhs[left, :] = block[48:, SIZE_K:] * s_all
        lhs2[left, :] = block[48:, half]
        rhs2[left, :] = block[48:, SIZE_K:] * inv_all
        left = pl.ds(32 + 16 * i, 16)
        lhs[left, :] = -block[48:, cot_half]
        rhs[left, :] = block[48:, :SIZE_K] * s_all
        right = pl.ds(64 + 48 * i, 48)
        lhs[right, :] = block[:48, cot_half] * s_half
        rhs[right, :] = block[:48, :SIZE_K]
        right = pl.ds(160 + 48 * i, 48)
        lhs[right, :] = -block[:48, half] * s_half
        rhs[right, :] = block[:48, SIZE_K:]
        right = pl.ds(32 + 48 * i, 48)
        lhs2[right, :] = block[:48, half] * inv_half
        rhs2[right, :] = block[:48, SIZE_K:]
    rows = ((0,), (0,))
    eye = lax.broadcasted_iota(jnp.int32, (HALF, HALF), 0) == (
        lax.broadcasted_iota(jnp.int32, (HALF, HALF), 1)
    )
    s_down = jnp.sum(jnp.where(eye, s_half, 0.0), axis=1, keepdims=True)
    spread = s_all * s_all - s_down * s_down
    diagonal = (lax.broadcasted_iota(jnp.int32, (HALF, SIZE_K), 0) + begin) == (
        lax.broadcasted_iota(jnp.int32, (HALF, SIZE_K), 1)
    )
    divided = jnp.where(diagonal, 0.0, 1.0 / jnp.where(diagonal, 1.0, spread))
    main = dot(lhs[...], rhs[...], rows, HIGHEST)
    out[...] = divided * main - dot(lhs2[...], rhs2[...], rows, HIGHEST)


def half_core(core_index, own, got, singular):
    vmem = pl.BlockSpec(memory_space=pltpu.VMEM)
    return pl.pallas_call(
        half_core_kernel,
        out_shape=jax.ShapeDtypeStruct((HALF, SIZE_K), jnp.float32),
        in_specs=[pl.BlockSpec(memory_space=pltpu.SMEM)] + [vmem] * 3,
        out_specs=vmem,
        scratch_shapes=[
            pltpu.VMEM((256, HALF), jnp.float32),
            pltpu.VMEM((256, SIZE_K), jnp.float32),
            pltpu.VMEM((128, HALF), jnp.float32),
            pltpu.VMEM((128, SIZE_K), jnp.float32),
        ],
        cost_estimate=pl.CostEstimate(
            flops=2 * 6 * 384 * HALF * SIZE_K, bytes_accessed=1 << 20, transcendentals=0
        ),
        name="half_core",
    )(core_index.reshape(1), own, got, singular.reshape(1, -1))


def local(left, left_cot, right, right_cot, singular, singular_cot):
    core_index = lax.axis_index("core")
    first = core_index == 0
    at_low = lax.axis_index("yl") == 0

    right_pair, left_pair, stacked = pack(left, left_cot, right, right_cot)
    rights = lax.all_gather(right_pair, ROW, axis=0, tiled=True)
    other = shift(left_pair, "yl", 2, 1)
    got = swap(stacked)
    mine = half_core(core_index, stacked, got, singular)
    pieces = lax.all_to_all(mine.reshape(32, 8, SIZE_K), OUTER, 0, 0)

    own = jnp.stack([jnp.where(at_low, left_pair, other), jnp.where(at_low, other, left_pair)])
    below, above = shift(own, "z", 8, 1), shift(own, "z", 8, -1)

    below, above, rows = lax.optimization_barrier((below, above, jnp.sum(pieces, axis=0)))
    pieces = gather(rows, INNER, 8)
    far_below = shift(jnp.stack([below, own, above]), "z", 8, 3)
    far_above = shift(jnp.stack([below, own]), "z", 8, -3)
    ring = [own[None], above[None], far_above, far_below, below[None]]
    line = jnp.concatenate(ring + ring, axis=0)
    line = lax.dynamic_slice_in_dim(line, 8 - lax.axis_index("z"), 8, 0).reshape(16, 16, 1024)

    line, rows = lax.optimization_barrier((line, jnp.sum(pieces, axis=0)))
    own_half = gather(rows, OUTER, 32).reshape(HALF, SIZE_K)
    other_line = swap(line)
    lefts = jnp.stack(
        [jnp.where(first, line, other_line), jnp.where(first, other_line, line)], axis=1
    ).reshape(-1, 1024)
    other_half = swap(own_half)
    core = jnp.concatenate(
        [jnp.where(first, own_half, other_half), jnp.where(first, other_half, own_half)], axis=0
    ) + jnp.diag(singular_cot)

    inverse = (1.0 / singular)[None, :]
    factor = lefts[:, :SIZE_K]
    last = ((1,), (1,))
    panel = dot(factor, core, ((1,), (0,)), HIGH) + lefts[:, SIZE_K:] * inverse
    flat = dot(factor * inverse, rights[:, :SIZE_K], last, HIGH)
    return flat + dot(panel, rights[:, SIZE_K:], last, HIGH)


def solution(mesh):
    fine = Mesh(mesh.devices.reshape(SIZES), ALL)
    placed = (
        P(ROW + COL, None),
        P(ROW + COL, None),
        P(COL + ROW, None),
        P(COL + ROW, None),
        P(),
        P(),
    )
    return jax.shard_map(local, mesh=fine, in_specs=placed, out_specs=P(ROW, COL), check_vma=False)
```

time: 214 us -> 125 us (0.58)
  the two profiles are of different devices: /device:TPU:1 before, /device:TPU:121 now
where the time goes in v4:
time: 125 us; the launch traced here: 124 us
  starting transfers between devices  52.7 us (42%)
  waiting for transfers between devices  42.6 us (34%)
  between operations  13.7 us (11%)
  matrix products  6.84 us (5%)
  Pallas kernels  4.74 us (4%)
  local copies, waits for them, and re-layouts  2.46 us (2%)
  other arithmetic  1.47 us (1%)
    all_to_all x2, waiting for transfers between devices, gather(): return lax.all_to_all(copies, axis, 0, 0)  21.4 us
    ppermute x5, starting transfers between devices, shift(): lax.ppermute(block, axis, [(i, (i + by) % size) for i in range(size)])  16.5 us
    ppermute x5, waiting for transfers between devices, shift(): lax.ppermute(block, axis, [(i, (i + by) % size) for i in range(size)])  15.2 us
    all_to_all x2, starting transfers between devices, gather(): return lax.all_to_all(copies, axis, 0, 0)  14 us
    all_to_all x1, starting transfers between devices, local(): pieces = lax.all_to_all(mine.reshape(32, 8, SIZE_K), OUTER, 0, 0)  12 us
    ppermute x3, starting transfers between devices, swap(): return lax.ppermute(block, 'core', SWAP)  10.2 us
    dot_general x3, matrix products, dot(): lax.dot_general(a, b, (contract, ((), ())), precision=precision, preferre...  6.84 us
    all_to_all x1, waiting for transfers between devices, local(): pieces = lax.all_to_all(mine.reshape(32, 8, SIZE_K), OUTER, 0, 0)  3.63 us
  transfers between devices with their start and end apart: 12, of which 9 were waited for; matrix products, arithmetic and copies ran while one was open for 3% of the time, Pallas kernels for 2%

profile of v4, /device:TPU:121, one launch (start us, length us, event | category | flops | bytes accessed | tf_op | source)
XLA Modules:
  0.0 124.5 jit_solution(7142225743777904392)
XLA Ops:
  6.5 1.8 %pack.1 = (f32[48,1024]{1,0:T(8,128)}, f32[16,1024]{1,0:T(8,128)}, f32[64,1024]{1,0:T(8,128)}) custom-call(f32[16,512]{1,0:T(8,128)} %left.1, f32[16,512]{1,0:T(8,128)} %left_cot.1, f32[48,512]{1,0:T(8,128)} %right.1, f32[48,512]{1,0:T(8,128)} %right_cot.1), custom_call_target="tpu_custom_call" | custom-call | bytes 1048576 | tf_op jit(solution)/shard_map/pack/pallas_call | solution.py:54
  8.4 2.6 %collective-permute-start.3 = (f32[64,1024]{1,0:T(8,128)}, f32[64,1024]{1,0:T(8,128)S(1)}, u32[]{:S(2)}, u32[]{:S(2)}) collective-permute-start(f32[64,1024]{1,0:T(8,128)} %get-tuple-element.14.own), channel_id=1, source_target_pairs={{0,1},{1,0},{2,3},{3,2},{4,5},{5,4},{6,7},{7,6},{8,9},{9,8},{10,11... | collective-permute-start | bytes 786440 | tf_op jit(solution)/shard_map/ppermute | solution.py:38
  11.0 1.3 %collective-permute-done.3.got = f32[64,1024]{1,0:T(8,128)S(1)} collective-permute-done((f32[64,1024]{1,0:T(8,128)}, f32[64,1024]{1,0:T(8,128)S(1)}, u32[]{:S(2)}, u32[]{:S(2)}) %collective-permute-start.3) | collective-permute-done | bytes 262176 | tf_op jit(solution)/shard_map/ppermute | solution.py:38
  12.3 0.7 copy-done.3
  13.0 2.9 %half_core.1 = f32[256,512]{1,0:T(8,128)} custom-call(s32[1]{0:T(128)} %bitcast.3.core_index, f32[64,1024]{1,0:T(8,128)} %get-tuple-element.14.own, f32[64,1024]{1,0:T(8,128)} %copy-done.3, f32[1,512]{1,0:T(1,128)} %bitcast.38), custom_call_target="tpu_custom_call" | custom-call | flops 603979776 | bytes 1048576 | tf_op jit(solution)/shard_map/half_core/pallas_call | solution.py:104
  15.9 12.0 %all-to-all-start = ((f32[32,8,512]{2,1,0:T(8,128)}), f32[32,8,512]{2,1,0:T(8,128)S(1)}, u32[]{:S(2)}, u32[]{:S(2)}) async-start(f32[32,8,512]{2,1,0:T(8,128)} %bitcast.37), calls=%async_computation | async-start | bytes 1048576 | tf_op jit(solution)/shard_map/all_to_all | solution.py:132
  28.0 3.0 %collective-permute-start = (f32[16,1024]{1,0:T(8,128)S(1)}, f32[16,1024]{1,0:T(8,128)S(1)}, u32[]{:S(2)}, u32[]{:S(2)}) collective-permute-start(f32[16,1024]{1,0:T(8,128)S(1)} %copy-done.1), channel_id=1, source_target_pairs={{0,2},{2,0},{1,3},{3,1},{4,6},{6,4},{5,7},{7,5},{8,10},{10,8},{9,1... | collective-permute-start | bytes 196616 | tf_op jit(solution)/shard_map/ppermute | solution.py:34
  31.0 4.3 %collective-permute-done = f32[16,1024]{1,0:T(8,128)S(1)} collective-permute-done((f32[16,1024]{1,0:T(8,128)S(1)}, f32[16,1024]{1,0:T(8,128)S(1)}, u32[]{:S(2)}, u32[]{:S(2)}) %collective-permute-start) | collective-permute-done | bytes 65568 | tf_op jit(solution)/shard_map/ppermute | solution.py:34
  35.3 3.3 %collective-permute-start.1 = (f32[2,16,1024]{2,1,0:T(8,128)S(1)}, f32[2,16,1024]{2,1,0:T(8,128)S(1)}, u32[]{:S(2)}, u32[]{:S(2)}) collective-permute-start(f32[2,16,1024]{2,1,0:T(8,128)S(1)} %get-tuple-element.26), channel_id=1, source_target_pairs={{0,4},{4,8},{8,12},{12,16},{16,20},{20,24},{24,28},{28,0},{1,5},{5... | collective-permute-start | bytes 393224 | tf_op jit(solution)/shard_map/ppermute | solution.py:34
  38.6 2.0 %collective-permute-start.2 = (f32[2,16,1024]{2,1,0:T(8,128)S(1)}, f32[2,16,1024]{2,1,0:T(8,128)S(1)}, u32[]{:S(2)}, u32[]{:S(2)}) collective-permute-start(f32[2,16,1024]{2,1,0:T(8,128)S(1)} %get-tuple-element.26), channel_id=1, source_target_pairs={{0,28},{4,0},{8,4},{12,8},{16,12},{20,16},{24,20},{28,24},{1,29},{... | collective-permute-start | bytes 393224 | tf_op jit(solution)/shard_map/ppermute | solution.py:34
  40.6 3.6 %all-to-all-done = f32[32,8,512]{2,1,0:T(8,128)S(1)} async-done(((f32[32,8,512]{2,1,0:T(8,128)}), f32[32,8,512]{2,1,0:T(8,128)S(1)}, u32[]{:S(2)}, u32[]{:S(2)}) %all-to-all-start) | async-done | bytes 524320 | tf_op jit(solution)/shard_map/all_to_all | solution.py:132
  44.3 1.0 collective-permute-done.2
  45.3 0.8 pad_maximum_fusion.1
  46.1 5.0 %collective-permute-start.5 = (f32[3,2,16,1024]{3,2,1,0:T(8,128)}, f32[3,2,16,1024]{3,2,1,0:T(8,128)S(1)}, u32[]{:S(2)}, u32[]{:S(2)}) collective-permute-start(f32[3,2,16,1024]{3,2,1,0:T(8,128)} %pad_maximum_fusion.1), channel_id=1, source_target_pairs={{0,12},{4,16},{8,20},{12,24},{16,28},{20,0},{24,4},{28,8},{1,13},{... | collective-permute-start | bytes 1179656 | tf_op jit(solution)/shard_map/ppermute | solution.py:34
  51.1 3.3 %collective-permute-start.4 = (f32[2,2,16,1024]{3,2,1,0:T(8,128)S(1)}, f32[2,2,16,1024]{3,2,1,0:T(8,128)S(1)}, u32[]{:S(2)}, u32[]{:S(2)}) collective-permute-start(f32[2,2,16,1024]{3,2,1,0:T(8,128)S(1)} %pad_maximum_fusion.2), channel_id=1, source_target_pairs={{0,20},{4,24},{8,28},{12,0},{16,4},{20,8},{24,12},{28,16},{1,21},{... | collective-permute-start | bytes 786440 | tf_op jit(solution)/shard_map/ppermute | solution.py:34
  54.4 0.6 broadcast_in_dim.40
  55.1 6.1 %all-to-all-start.1 = ((f32[8,8,512]{2,1,0:T(8,128)}), f32[8,8,512]{2,1,0:T(8,128)S(1)}, u32[]{:S(2)}, u32[]{:S(2)}) async-start(f32[8,8,512]{2,1,0:T(8,128)} %broadcast_in_dim.40), calls=%async_computation.1 | async-start | bytes 262144 | tf_op jit(solution)/shard_map/all_to_all | solution.py:30
  61.2 8.2 %all-to-all-done.1 = f32[8,8,512]{2,1,0:T(8,128)S(1)} async-done(((f32[8,8,512]{2,1,0:T(8,128)}), f32[8,8,512]{2,1,0:T(8,128)S(1)}, u32[]{:S(2)}, u32[]{:S(2)}) %all-to-all-start.1) | async-done | bytes 131104 | tf_op jit(solution)/shard_map/all_to_all | solution.py:30
  69.4 3.1 %collective-permute-done.4 = f32[2,2,16,1024]{3,2,1,0:T(8,128)S(1)} collective-permute-done((f32[2,2,16,1024]{3,2,1,0:T(8,128)S(1)}, f32[2,2,16,1024]{3,2,1,0:T(8,128)S(1)}, u32[]{:S(2)}, u32[]{:S(2)}) %collective-permute-start.4) | collective-permute-done | bytes 262176 | tf_op jit(solution)/shard_map/ppermute | solution.py:34
  72.5 6.7 %collective-permute-done.5 = f32[3,2,16,1024]{3,2,1,0:T(8,128)S(1)} collective-permute-done((f32[3,2,16,1024]{3,2,1,0:T(8,128)}, f32[3,2,16,1024]{3,2,1,0:T(8,128)S(1)}, u32[]{:S(2)}, u32[]{:S(2)}) %collective-permute-start.5) | collective-permute-done | bytes 393248 | tf_op jit(solution)/shard_map/ppermute | solution.py:34
  79.5 0.1 constant_dynamic-slice_fusion
  79.6 0.9 broadcast_in_dim.41
  80.5 7.9 %all-to-all-start.2 = ((f32[32,8,512]{2,1,0:T(8,128)}), f32[32,8,512]{2,1,0:T(8,128)S(1)}, u32[]{:S(2)}, u32[]{:S(2)}) async-start(f32[32,8,512]{2,1,0:T(8,128)} %broadcast_in_dim.41), calls=%async_computation.2 | async-start | bytes 1048576 | tf_op jit(solution)/shard_map/all_to_all | solution.py:30
  88.3 3.0 %collective-permute-start.6 = (f32[16,16,1024]{2,1,0:T(8,128)S(1)}, f32[16,16,1024]{2,1,0:T(8,128)S(1)}, u32[]{:S(2)}, u32[]{:S(2)}) collective-permute-start(f32[16,16,1024]{2,1,0:T(8,128)S(1)} %bitcast.31), channel_id=1, source_target_pairs={{0,1},{1,0},{2,3},{3,2},{4,5},{5,4},{6,7},{7,6},{8,9},{9,8},{10,11... | collective-permute-start | bytes 3145736 | tf_op jit(solution)/shard_map/ppermute | solution.py:38
  91.3 13.2 %all-to-all-done.2 = f32[32,8,512]{2,1,0:T(8,128)S(1)} async-done(((f32[32,8,512]{2,1,0:T(8,128)}), f32[32,8,512]{2,1,0:T(8,128)S(1)}, u32[]{:S(2)}, u32[]{:S(2)}) %all-to-all-start.2) | async-done | bytes 524320 | tf_op jit(solution)/shard_map/all_to_all | solution.py:30
  104.5 4.6 %collective-permute-start.7 = (f32[256,512]{1,0:T(8,128)S(1)}, f32[256,512]{1,0:T(8,128)S(1)}, u32[]{:S(2)}, u32[]{:S(2)}) collective-permute-start(f32[256,512]{1,0:T(8,128)S(1)} %bitcast.33), channel_id=1, source_target_pairs={{0,1},{1,0},{2,3},{3,2},{4,5},{5,4},{6,7},{7,6},{8,9},{9,8},{10,11... | collective-permute-start | bytes 1572872 | tf_op jit(solution)/shard_map/ppermute | solution.py:38
  109.1 0.2 select_bitcast_fusion.1
  109.4 0.2 pad_maximum_fusion
  109.6 1.0 collective-permute-done.7
  110.7 1.1 convolution_add_fusion
  111.9 3.0 %fusion = f32[512,768]{1,0:T(8,128)S(1)} fusion(f32[512,512]{1,0:T(8,128)S(1)} %convolution_add_fusion, f32[768,1024]{1,0:T(8,128)} %all-gather.2.cloned.1.call-done), kind=kOutput, calls=%fused_computation.1 | convolution fusion | flops 1207959552 | bytes 4194304 | tf_op jit(solution)/shard_map/dot_general | solution.py:23
  114.9 2.7 %fusion.4 = f32[512,768]{1,0:T(8,128)} fusion(f32[512,768]{1,0:T(8,128)S(1)} %fusion, f32[768,1024]{1,0:T(8,128)S(1)} %copy-done, f32[512,1024]{1,0:T(8,128)S(1)} %bitcast.30, f32[512]{0:T(512)S(1)} %broadcast_divide_fusion), kind=kOutput, calls=%fused_computation.5 | convolution fusion | flops 1208614912 | bytes 5769216 | tf_op jit(solution)/shard_map/dot_general | solution.py:23
  (31 shorter events, 0.4 us)
Async XLA Ops:
  6.5 105.3 %all-gather.2.cloned.1.call-start = ((), (), s32[]{:S(2)}) async-start(), calls=%async_computation.3 | async-start | bytes 3342336 | tf_op jit(solution)/shard_map/all_gather | solution.py:128
  8.3 19.6 %copy-start.1 = (f32[16,1024]{1,0:T(8,128)S(1)}, f32[16,1024]{1,0:T(8,128)}, u32[]{:S(2)}) copy-start(f32[16,1024]{1,0:T(8,128)} %get-tuple-element.13) | copy-start | bytes 196612
  8.4 3.9 %collective-permute-start.3 = (f32[64,1024]{1,0:T(8,128)}, f32[64,1024]{1,0:T(8,128)S(1)}, u32[]{:S(2)}, u32[]{:S(2)}) collective-permute-start(f32[64,1024]{1,0:T(8,128)} %get-tuple-element.14.own), channel_id=1, source_target_pairs={{0,1},{1,0},{2,3},{3,2},{4,5},{5,4},{6,7},{7,6},{8,9},{9,8},{10,11... | collective-permute-start | bytes 786440 | tf_op jit(solution)/shard_map/ppermute | solution.py:38
  12.3 0.7 copy-start.3
  15.9 28.3 %all-to-all-start = ((f32[32,8,512]{2,1,0:T(8,128)}), f32[32,8,512]{2,1,0:T(8,128)S(1)}, u32[]{:S(2)}, u32[]{:S(2)}) async-start(f32[32,8,512]{2,1,0:T(8,128)} %bitcast.37), calls=%async_computation | async-start | bytes 1048576 | tf_op jit(solution)/shard_map/all_to_all | solution.py:132
  28.0 7.3 %collective-permute-start = (f32[16,1024]{1,0:T(8,128)S(1)}, f32[16,1024]{1,0:T(8,128)S(1)}, u32[]{:S(2)}, u32[]{:S(2)}) collective-permute-start(f32[16,1024]{1,0:T(8,128)S(1)} %copy-done.1), channel_id=1, source_target_pairs={{0,2},{2,0},{1,3},{3,1},{4,6},{6,4},{5,7},{7,5},{8,10},{10,8},{9,1... | collective-permute-start | bytes 196616 | tf_op jit(solution)/shard_map/ppermute | solution.py:34
  35.3 9.0 %collective-permute-start.1 = (f32[2,16,1024]{2,1,0:T(8,128)S(1)}, f32[2,16,1024]{2,1,0:T(8,128)S(1)}, u32[]{:S(2)}, u32[]{:S(2)}) collective-permute-start(f32[2,16,1024]{2,1,0:T(8,128)S(1)} %get-tuple-element.26), channel_id=1, source_target_pairs={{0,4},{4,8},{8,12},{12,16},{16,20},{20,24},{24,28},{28,0},{1,5},{5... | collective-permute-start | bytes 393224 | tf_op jit(solution)/shard_map/ppermute | solution.py:34
  38.6 6.8 %collective-permute-start.2 = (f32[2,16,1024]{2,1,0:T(8,128)S(1)}, f32[2,16,1024]{2,1,0:T(8,128)S(1)}, u32[]{:S(2)}, u32[]{:S(2)}) collective-permute-start(f32[2,16,1024]{2,1,0:T(8,128)S(1)} %get-tuple-element.26), channel_id=1, source_target_pairs={{0,28},{4,0},{8,4},{12,8},{16,12},{20,16},{24,20},{28,24},{1,29},{... | collective-permute-start | bytes 393224 | tf_op jit(solution)/shard_map/ppermute | solution.py:34
  46.1 33.2 %collective-permute-start.5 = (f32[3,2,16,1024]{3,2,1,0:T(8,128)}, f32[3,2,16,1024]{3,2,1,0:T(8,128)S(1)}, u32[]{:S(2)}, u32[]{:S(2)}) collective-permute-start(f32[3,2,16,1024]{3,2,1,0:T(8,128)} %pad_maximum_fusion.1), channel_id=1, source_target_pairs={{0,12},{4,16},{8,20},{12,24},{16,28},{20,0},{24,4},{28,8},{1,13},{... | collective-permute-start | bytes 1179656 | tf_op jit(solution)/shard_map/ppermute | solution.py:34
  51.1 21.4 %collective-permute-start.4 = (f32[2,2,16,1024]{3,2,1,0:T(8,128)S(1)}, f32[2,2,16,1024]{3,2,1,0:T(8,128)S(1)}, u32[]{:S(2)}, u32[]{:S(2)}) collective-permute-start(f32[2,2,16,1024]{3,2,1,0:T(8,128)S(1)} %pad_maximum_fusion.2), channel_id=1, source_target_pairs={{0,20},{4,24},{8,28},{12,0},{16,4},{20,8},{24,12},{28,16},{1,21},{... | collective-permute-start | bytes 786440 | tf_op jit(solution)/shard_map/ppermute | solution.py:34
  55.1 14.3 %all-to-all-start.1 = ((f32[8,8,512]{2,1,0:T(8,128)}), f32[8,8,512]{2,1,0:T(8,128)S(1)}, u32[]{:S(2)}, u32[]{:S(2)}) async-start(f32[8,8,512]{2,1,0:T(8,128)} %broadcast_in_dim.40), calls=%async_computation.1 | async-start | bytes 262144 | tf_op jit(solution)/shard_map/all_to_all | solution.py:30
  79.4 29.7 %copy-start.2 = (f32[512]{0:T(512)S(1)}, f32[512]{0:T(512)}, u32[]{:S(2)}) copy-start(f32[512]{0:T(512)} %param.10) | copy-start | bytes 6148
  80.5 24.0 %all-to-all-start.2 = ((f32[32,8,512]{2,1,0:T(8,128)}), f32[32,8,512]{2,1,0:T(8,128)S(1)}, u32[]{:S(2)}, u32[]{:S(2)}) async-start(f32[32,8,512]{2,1,0:T(8,128)} %broadcast_in_dim.41), calls=%async_computation.2 | async-start | bytes 1048576 | tf_op jit(solution)/shard_map/all_to_all | solution.py:30
  88.3 20.8 %collective-permute-start.6 = (f32[16,16,1024]{2,1,0:T(8,128)S(1)}, f32[16,16,1024]{2,1,0:T(8,128)S(1)}, u32[]{:S(2)}, u32[]{:S(2)}) collective-permute-start(f32[16,16,1024]{2,1,0:T(8,128)S(1)} %bitcast.31), channel_id=1, source_target_pairs={{0,1},{1,0},{2,3},{3,2},{4,5},{5,4},{6,7},{7,6},{8,9},{9,8},{10,11... | collective-permute-start | bytes 3145736 | tf_op jit(solution)/shard_map/ppermute | solution.py:38
  104.5 6.1 %collective-permute-start.7 = (f32[256,512]{1,0:T(8,128)S(1)}, f32[256,512]{1,0:T(8,128)S(1)}, u32[]{:S(2)}, u32[]{:S(2)}) collective-permute-start(f32[256,512]{1,0:T(8,128)S(1)} %bitcast.33), channel_id=1, source_target_pairs={{0,1},{1,0},{2,3},{3,2},{4,5},{5,4},{6,7},{7,6},{8,9},{9,8},{10,11... | collective-permute-start | bytes 1572872 | tf_op jit(solution)/shard_map/ppermute | solution.py:38
  109.6 1.1 copy-start.4
  111.9 3.1 %copy-start = (f32[768,1024]{1,0:T(8,128)S(1)}, f32[768,1024]{1,0:T(8,128)}, u32[]{:S(2)}) copy-start(f32[768,1024]{1,0:T(8,128)} %all-gather.2.cloned.1.call-done) | copy-start | bytes 9437188
Sparse Core Ops, SparseCore 0:
  10.4 77.2 all-gather.1

commit v5 on v4

--- a/solution.py
+++ b/solution.py
@@ -136,13 +136,14 @@
 
     below, above, rows = lax.optimization_barrier((below, above, jnp.sum(pieces, axis=0)))
     pieces = gather(rows, INNER, 8)
-    far_below = shift(jnp.stack([below, own, above]), "z", 8, 3)
-    far_above = shift(jnp.stack([below, own]), "z", 8, -3)
-    ring = [own[None], above[None], far_above, far_below, below[None]]
+    mid_below = shift(jnp.stack([below, own]), "z", 8, 2)
+    mid_above = shift(jnp.stack([own, above]), "z", 8, -2)
+    last_above = shift(mid_above[1], "z", 8, -1)
+    ring = [own[None], above[None], mid_above, last_above[None], mid_below, below[None]]
     line = jnp.concatenate(ring + ring, axis=0)
-    line = lax.dynamic_slice_in_dim(line, 8 - lax.axis_index("z"), 8, 0).reshape(16, 16, 1024)
-
-    line, rows = lax.optimization_barrier((line, jnp.sum(pieces, axis=0)))
+    line = lax.dynamic_slice_in_dim(line, 8 - lax.axis_index("z"), 8, 0)
+    line = line.reshape(16, 16, 1024)
+    rows = jnp.sum(pieces, axis=0)
     own_half = gather(rows, OUTER, 32).reshape(HALF, SIZE_K)
     other_line = swap(line)
     lefts = jnp.stack(
@@ -158,6 +159,7 @@
     last = ((1,), (1,))
     panel = dot(factor, core, ((1,), (0,)), HIGH) + lefts[:, SIZE_K:] * inverse
     flat = dot(factor * inverse, rights[:, :SIZE_K], last, HIGH)
+    flat = lax.optimization_barrier(flat)
     return flat + dot(panel, rights[:, SIZE_K:], last, HIGH)
 
 

time: 125 us -> 119 us (0.952)
  the two profiles are of different devices: /device:TPU:121 before, /device:TPU:25 now
where the time goes in v5:
time: 119 us; the launch traced here: 118 us
  starting transfers between devices  60.6 us (51%)
  waiting for transfers between devices  19.9 us (17%)
  between operations  13.7 us (12%)
  local copies, waits for them, and re-layouts  10.4 us (9%)
  matrix products  6.82 us (6%)
  Pallas kernels  4.73 us (4%)
  other arithmetic  2.01 us (2%)
    ppermute x6, starting transfers between devices, shift(): lax.ppermute(block, axis, [(i, (i + by) % size) for i in range(size)])  24.2 us
    all_to_all x2, starting transfers between devices, gather(): return lax.all_to_all(copies, axis, 0, 0)  16 us
    all_to_all x1, starting transfers between devices, local(): pieces = lax.all_to_all(mine.reshape(32, 8, SIZE_K), OUTER, 0, 0)  12.9 us
    ppermute x6, waiting for transfers between devices, shift(): lax.ppermute(block, axis, [(i, (i + by) % size) for i in range(size)])  10.9 us
    ppermute x3, starting transfers between devices, swap(): return lax.ppermute(block, 'core', SWAP)  7.6 us
    unnamed x19, local copies, waits for them, and re-layouts  6.88 us
    dot_general x3, matrix products, dot(): lax.dot_general(a, b, (contract, ((), ())), precision=precision, preferre...  6.82 us
    all_to_all x2, waiting for transfers between devices, gather(): return lax.all_to_all(copies, axis, 0, 0)  6.64 us
  transfers between devices with their start and end apart: 13, of which 6 were waited for; matrix products, arithmetic and copies ran while one was open for 11% of the time, Pallas kernels for 2%

profile of v5, /device:TPU:25, one launch (start us, length us, event | category | flops | bytes accessed | tf_op | source)
XLA Modules:
  0.0 118.1 jit_solution(15661575898570025814)
XLA Ops:
  6.5 1.8 %pack.1 = (f32[48,1024]{1,0:T(8,128)}, f32[16,1024]{1,0:T(8,128)}, f32[64,1024]{1,0:T(8,128)}) custom-call(f32[16,512]{1,0:T(8,128)} %left.1, f32[16,512]{1,0:T(8,128)} %left_cot.1, f32[48,512]{1,0:T(8,128)} %right.1, f32[48,512]{1,0:T(8,128)} %right_cot.1), custom_call_target="tpu_custom_call" | custom-call | bytes 1048576 | tf_op jit(solution)/shard_map/pack/pallas_call | solution.py:54
  8.3 2.7 %collective-permute-start.3 = (f32[64,1024]{1,0:T(8,128)}, f32[64,1024]{1,0:T(8,128)S(1)}, u32[]{:S(2)}, u32[]{:S(2)}) collective-permute-start(f32[64,1024]{1,0:T(8,128)} %get-tuple-element.12.own), channel_id=1, source_target_pairs={{0,1},{1,0},{2,3},{3,2},{4,5},{5,4},{6,7},{7,6},{8,9},{9,8},{10,11... | collective-permute-start | bytes 786440 | tf_op jit(solution)/shard_map/ppermute | solution.py:38
  11.1 1.3 %collective-permute-done.3.got = f32[64,1024]{1,0:T(8,128)S(1)} collective-permute-done((f32[64,1024]{1,0:T(8,128)}, f32[64,1024]{1,0:T(8,128)S(1)}, u32[]{:S(2)}, u32[]{:S(2)}) %collective-permute-start.3) | collective-permute-done | bytes 262176 | tf_op jit(solution)/shard_map/ppermute | solution.py:38
  12.4 0.7 copy-done.3
  13.1 2.9 %half_core.1 = f32[256,512]{1,0:T(8,128)} custom-call(s32[1]{0:T(128)} %bitcast.3.core_index, f32[64,1024]{1,0:T(8,128)} %get-tuple-element.12.own, f32[64,1024]{1,0:T(8,128)} %copy-done.3, f32[1,512]{1,0:T(1,128)} %bitcast.43), custom_call_target="tpu_custom_call" | custom-call | flops 603979776 | bytes 1048576 | tf_op jit(solution)/shard_map/half_core/pallas_call | solution.py:104
  16.0 12.9 %all-to-all-start = ((f32[32,8,512]{2,1,0:T(8,128)}), f32[32,8,512]{2,1,0:T(8,128)S(1)}, u32[]{:S(2)}, u32[]{:S(2)}) async-start(f32[32,8,512]{2,1,0:T(8,128)} %bitcast.42), calls=%async_computation | async-start | bytes 1048576 | tf_op jit(solution)/shard_map/all_to_all | solution.py:132
  28.9 2.1 %collective-permute-start = (f32[16,1024]{1,0:T(8,128)S(1)}, f32[16,1024]{1,0:T(8,128)S(1)}, u32[]{:S(2)}, u32[]{:S(2)}) collective-permute-start(f32[16,1024]{1,0:T(8,128)S(1)} %copy-done.1), channel_id=1, source_target_pairs={{0,2},{2,0},{1,3},{3,1},{4,6},{6,4},{5,7},{7,5},{8,10},{10,8},{9,1... | collective-permute-start | bytes 196616 | tf_op jit(solution)/shard_map/ppermute | solution.py:34
  31.0 4.7 %collective-permute-done = f32[16,1024]{1,0:T(8,128)S(1)} collective-permute-done((f32[16,1024]{1,0:T(8,128)S(1)}, f32[16,1024]{1,0:T(8,128)S(1)}, u32[]{:S(2)}, u32[]{:S(2)}) %collective-permute-start) | collective-permute-done | bytes 65568 | tf_op jit(solution)/shard_map/ppermute | solution.py:34
  35.8 3.3 %collective-permute-start.1 = (f32[2,16,1024]{2,1,0:T(8,128)S(1)}, f32[2,16,1024]{2,1,0:T(8,128)S(1)}, u32[]{:S(2)}, u32[]{:S(2)}) collective-permute-start(f32[2,16,1024]{2,1,0:T(8,128)S(1)} %get-tuple-element.24), channel_id=1, source_target_pairs={{0,4},{4,8},{8,12},{12,16},{16,20},{20,24},{24,28},{28,0},{1,5},{5... | collective-permute-start | bytes 393224 | tf_op jit(solution)/shard_map/ppermute | solution.py:34
  39.1 4.0 %collective-permute-start.2 = (f32[2,16,1024]{2,1,0:T(8,128)S(1)}, f32[2,16,1024]{2,1,0:T(8,128)S(1)}, u32[]{:S(2)}, u32[]{:S(2)}) collective-permute-start(f32[2,16,1024]{2,1,0:T(8,128)S(1)} %get-tuple-element.24), channel_id=1, source_target_pairs={{0,28},{4,0},{8,4},{12,8},{16,12},{20,16},{24,20},{28,24},{1,29},{... | collective-permute-start | bytes 393224 | tf_op jit(solution)/shard_map/ppermute | solution.py:34
  43.2 3.4 %collective-permute-done.1 = f32[2,16,1024]{2,1,0:T(8,128)S(1)} collective-permute-done((f32[2,16,1024]{2,1,0:T(8,128)S(1)}, f32[2,16,1024]{2,1,0:T(8,128)S(1)}, u32[]{:S(2)}, u32[]{:S(2)}) %collective-permute-start.1) | collective-permute-done | bytes 131104 | tf_op jit(solution)/shard_map/ppermute | solution.py:34
  46.7 3.9 %collective-permute-start.4 = (f32[2,2,16,1024]{3,2,1,0:T(8,128)S(1)}, f32[2,2,16,1024]{3,2,1,0:T(8,128)S(1)}, u32[]{:S(2)}, u32[]{:S(2)}) collective-permute-start(f32[2,2,16,1024]{3,2,1,0:T(8,128)S(1)} %get-tuple-element.22), channel_id=1, source_target_pairs={{0,24},{4,28},{8,0},{12,4},{16,8},{20,12},{24,16},{28,20},{1,25},{... | collective-permute-start | bytes 786440 | tf_op jit(solution)/shard_map/ppermute | solution.py:34
  51.9 7.0 %all-to-all-start.1 = ((f32[8,8,512]{2,1,0:T(8,128)}), f32[8,8,512]{2,1,0:T(8,128)S(1)}, u32[]{:S(2)}, u32[]{:S(2)}) async-start(f32[8,8,512]{2,1,0:T(8,128)} %broadcast_in_dim.44), calls=%async_computation.1 | async-start | bytes 262144 | tf_op jit(solution)/shard_map/all_to_all | solution.py:30
  58.9 8.3 %collective-permute-start.5 = (f32[2,16,1024]{2,1,0:T(8,128)S(1)}, f32[2,16,1024]{2,1,0:T(8,128)S(1)}, u32[]{:S(2)}, u32[]{:S(2)}) collective-permute-start(f32[2,16,1024]{2,1,0:T(8,128)S(1)} %slice_bitcast_fusion), channel_id=1, source_target_pairs={{0,28},{4,0},{8,4},{12,8},{16,12},{20,16},{24,20},{28,24},{1,29},{... | collective-permute-start | bytes 393224 | tf_op jit(solution)/shard_map/ppermute | solution.py:34
  67.9 2.5 %collective-permute-start.6 = (f32[2,2,16,1024]{3,2,1,0:T(8,128)S(1)}, f32[2,2,16,1024]{3,2,1,0:T(8,128)S(1)}, u32[]{:S(2)}, u32[]{:S(2)}) collective-permute-start(f32[2,2,16,1024]{3,2,1,0:T(8,128)S(1)} %get-tuple-element.21), channel_id=1, source_target_pairs={{0,8},{4,12},{8,16},{12,20},{16,24},{20,28},{24,0},{28,4},{1,9},{5... | collective-permute-start | bytes 786440 | tf_op jit(solution)/shard_map/ppermute | solution.py:34
  70.5 0.9 broadcast_in_dim.45
  71.3 8.9 %all-to-all-start.2 = ((f32[32,8,512]{2,1,0:T(8,128)}), f32[32,8,512]{2,1,0:T(8,128)S(1)}, u32[]{:S(2)}, u32[]{:S(2)}) async-start(f32[32,8,512]{2,1,0:T(8,128)} %broadcast_in_dim.45), calls=%async_computation.2 | async-start | bytes 1048576 | tf_op jit(solution)/shard_map/all_to_all | solution.py:30
  80.3 0.7 constant_dynamic-update-slice_fusion.7
  81.0 0.7 bitcast_dynamic-update-slice_fusion
  81.7 2.7 %collective-permute-done.6 = f32[2,2,16,1024]{3,2,1,0:T(8,128)S(1)} collective-permute-done((f32[2,2,16,1024]{3,2,1,0:T(8,128)S(1)}, f32[2,2,16,1024]{3,2,1,0:T(8,128)S(1)}, u32[]{:S(2)}, u32[]{:S(2)}) %collective-permute-start.6) | collective-permute-done | bytes 262176 | tf_op jit(solution)/shard_map/ppermute | solution.py:34
  84.4 0.7 constant_dynamic-update-slice_fusion.6
  87.1 0.7 constant_dynamic-update-slice_fusion.2
  88.5 0.7 constant_dynamic-update-slice_fusion.1
  89.2 0.7 constant_dynamic-update-slice_fusion
  89.9 1.3 %constant_dynamic-slice_fusion = f32[8,2,16,1024]{3,2,1,0:T(8,128)S(1)} fusion(f32[16,2,16,1024]{3,2,1,0:T(8,128)} %constant_dynamic-update-slice_fusion, s32[]{:T(128)S(6)} %select_n.48), kind=kLoop, calls=%fused_computation.42 | loop fusion | bytes 2097156 | tf_op jit(solution)/shard_map/dynamic_slice | solution.py:144
  91.2 2.3 %collective-permute-start.7 = (f32[16,16,1024]{2,1,0:T(8,128)S(1)}, f32[16,16,1024]{2,1,0:T(8,128)S(1)}, u32[]{:S(2)}, u32[]{:S(2)}) collective-permute-start(f32[16,16,1024]{2,1,0:T(8,128)S(1)} %bitcast.38), channel_id=1, source_target_pairs={{0,1},{1,0},{2,3},{3,2},{4,5},{5,4},{6,7},{7,6},{8,9},{9,8},{10,11... | collective-permute-start | bytes 3145736 | tf_op jit(solution)/shard_map/ppermute | solution.py:38
  93.5 6.6 %all-to-all-done.2 = f32[32,8,512]{2,1,0:T(8,128)S(1)} async-done(((f32[32,8,512]{2,1,0:T(8,128)}), f32[32,8,512]{2,1,0:T(8,128)S(1)}, u32[]{:S(2)}, u32[]{:S(2)}) %all-to-all-start.2) | async-done | bytes 524320 | tf_op jit(solution)/shard_map/all_to_all | solution.py:30
  100.1 2.6 %collective-permute-start.8 = (f32[256,512]{1,0:T(8,128)S(1)}, f32[256,512]{1,0:T(8,128)S(1)}, u32[]{:S(2)}, u32[]{:S(2)}) collective-permute-start(f32[256,512]{1,0:T(8,128)S(1)} %bitcast.39), channel_id=1, source_target_pairs={{0,1},{1,0},{2,3},{3,2},{4,5},{5,4},{6,7},{7,6},{8,9},{9,8},{10,11... | collective-permute-start | bytes 1572872 | tf_op jit(solution)/shard_map/ppermute | solution.py:38
  103.2 1.0 collective-permute-done.8
  104.3 1.1 convolution_add_fusion
  105.5 3.0 %fusion.2 = f32[512,768]{1,0:T(8,128)S(1)} fusion(f32[768,1024]{1,0:T(8,128)} %all-gather.2.cloned.1.call-done, f32[512,1024]{1,0:T(8,128)S(1)} %bitcast.37, f32[512]{0:T(512)S(1)} %broadcast_divide_fusion), kind=kOutput, calls=%fused_computation.3 | convolution fusion | flops 1208221696 | bytes 4196352 | tf_op jit(solution)/shard_map/dot_general | solution.py:23
  108.5 2.7 %fusion.4 = f32[512,768]{1,0:T(8,128)} fusion(f32[512,768]{1,0:T(8,128)S(1)} %fusion.2, f32[512,512]{1,0:T(8,128)S(1)} %convolution_add_fusion, f32[768,1024]{1,0:T(8,128)S(1)} %copy-done), kind=kOutput, calls=%fused_computation.5 | convolution fusion | flops 1208352768 | bytes 5767168 | tf_op jit(solution)/shard_map/dot_general | solution.py:23
  (35 shorter events, 5.4 us)
Async XLA Ops:
  6.5 98.9 %all-gather.2.cloned.1.call-start = ((), (), s32[]{:S(2)}) async-start(), calls=%async_computation.3 | async-start | bytes 3342336 | tf_op jit(solution)/shard_map/all_gather | solution.py:128
  8.3 20.6 %copy-start.1 = (f32[16,1024]{1,0:T(8,128)S(1)}, f32[16,1024]{1,0:T(8,128)}, u32[]{:S(2)}) copy-start(f32[16,1024]{1,0:T(8,128)} %get-tuple-element.11) | copy-start | bytes 196612
  8.3 4.1 %collective-permute-start.3 = (f32[64,1024]{1,0:T(8,128)}, f32[64,1024]{1,0:T(8,128)S(1)}, u32[]{:S(2)}, u32[]{:S(2)}) collective-permute-start(f32[64,1024]{1,0:T(8,128)} %get-tuple-element.12.own), channel_id=1, source_target_pairs={{0,1},{1,0},{2,3},{3,2},{4,5},{5,4},{6,7},{7,6},{8,9},{9,8},{10,11... | collective-permute-start | bytes 786440 | tf_op jit(solution)/shard_map/ppermute | solution.py:38
  12.4 0.7 copy-start.3
  16.0 27.1 %all-to-all-start = ((f32[32,8,512]{2,1,0:T(8,128)}), f32[32,8,512]{2,1,0:T(8,128)S(1)}, u32[]{:S(2)}, u32[]{:S(2)}) async-start(f32[32,8,512]{2,1,0:T(8,128)} %bitcast.42), calls=%async_computation | async-start | bytes 1048576 | tf_op jit(solution)/shard_map/all_to_all | solution.py:132
  28.9 6.8 %collective-permute-start = (f32[16,1024]{1,0:T(8,128)S(1)}, f32[16,1024]{1,0:T(8,128)S(1)}, u32[]{:S(2)}, u32[]{:S(2)}) collective-permute-start(f32[16,1024]{1,0:T(8,128)S(1)} %copy-done.1), channel_id=1, source_target_pairs={{0,2},{2,0},{1,3},{3,1},{4,6},{6,4},{5,7},{7,5},{8,10},{10,8},{9,1... | collective-permute-start | bytes 196616 | tf_op jit(solution)/shard_map/ppermute | solution.py:34
  35.8 10.8 %collective-permute-start.1 = (f32[2,16,1024]{2,1,0:T(8,128)S(1)}, f32[2,16,1024]{2,1,0:T(8,128)S(1)}, u32[]{:S(2)}, u32[]{:S(2)}) collective-permute-start(f32[2,16,1024]{2,1,0:T(8,128)S(1)} %get-tuple-element.24), channel_id=1, source_target_pairs={{0,4},{4,8},{8,12},{12,16},{16,20},{20,24},{24,28},{28,0},{1,5},{5... | collective-permute-start | bytes 393224 | tf_op jit(solution)/shard_map/ppermute | solution.py:34
  39.1 7.5 %collective-permute-start.2 = (f32[2,16,1024]{2,1,0:T(8,128)S(1)}, f32[2,16,1024]{2,1,0:T(8,128)S(1)}, u32[]{:S(2)}, u32[]{:S(2)}) collective-permute-start(f32[2,16,1024]{2,1,0:T(8,128)S(1)} %get-tuple-element.24), channel_id=1, source_target_pairs={{0,28},{4,0},{8,4},{12,8},{16,12},{20,16},{24,20},{28,24},{1,29},{... | collective-permute-start | bytes 393224 | tf_op jit(solution)/shard_map/ppermute | solution.py:34
  46.7 12.3 %collective-permute-start.4 = (f32[2,2,16,1024]{3,2,1,0:T(8,128)S(1)}, f32[2,2,16,1024]{3,2,1,0:T(8,128)S(1)}, u32[]{:S(2)}, u32[]{:S(2)}) collective-permute-start(f32[2,2,16,1024]{3,2,1,0:T(8,128)S(1)} %get-tuple-element.22), channel_id=1, source_target_pairs={{0,24},{4,28},{8,0},{12,4},{16,8},{20,12},{24,16},{28,20},{1,25},{... | collective-permute-start | bytes 786440 | tf_op jit(solution)/shard_map/ppermute | solution.py:34
  51.9 18.6 %all-to-all-start.1 = ((f32[8,8,512]{2,1,0:T(8,128)}), f32[8,8,512]{2,1,0:T(8,128)S(1)}, u32[]{:S(2)}, u32[]{:S(2)}) async-start(f32[8,8,512]{2,1,0:T(8,128)} %broadcast_in_dim.44), calls=%async_computation.1 | async-start | bytes 262144 | tf_op jit(solution)/shard_map/all_to_all | solution.py:30
  58.9 22.0 %collective-permute-start.5 = (f32[2,16,1024]{2,1,0:T(8,128)S(1)}, f32[2,16,1024]{2,1,0:T(8,128)S(1)}, u32[]{:S(2)}, u32[]{:S(2)}) collective-permute-start(f32[2,16,1024]{2,1,0:T(8,128)S(1)} %slice_bitcast_fusion), channel_id=1, source_target_pairs={{0,28},{4,0},{8,4},{12,8},{16,12},{20,16},{24,20},{28,24},{1,29},{... | collective-permute-start | bytes 393224 | tf_op jit(solution)/shard_map/ppermute | solution.py:34
  67.9 16.5 %collective-permute-start.6 = (f32[2,2,16,1024]{3,2,1,0:T(8,128)S(1)}, f32[2,2,16,1024]{3,2,1,0:T(8,128)S(1)}, u32[]{:S(2)}, u32[]{:S(2)}) collective-permute-start(f32[2,2,16,1024]{3,2,1,0:T(8,128)S(1)} %get-tuple-element.21), channel_id=1, source_target_pairs={{0,8},{4,12},{8,16},{12,20},{16,24},{20,28},{24,0},{28,4},{1,9},{5... | collective-permute-start | bytes 786440 | tf_op jit(solution)/shard_map/ppermute | solution.py:34
  71.3 28.8 %all-to-all-start.2 = ((f32[32,8,512]{2,1,0:T(8,128)}), f32[32,8,512]{2,1,0:T(8,128)S(1)}, u32[]{:S(2)}, u32[]{:S(2)}) async-start(f32[32,8,512]{2,1,0:T(8,128)} %broadcast_in_dim.45), calls=%async_computation.2 | async-start | bytes 1048576 | tf_op jit(solution)/shard_map/all_to_all | solution.py:30
  85.7 17.0 %copy-start.2 = (f32[512]{0:T(512)S(1)}, f32[512]{0:T(512)}, u32[]{:S(2)}) copy-start(f32[512]{0:T(512)} %param.10) | copy-start | bytes 6148
  91.2 11.6 %collective-permute-start.7 = (f32[16,16,1024]{2,1,0:T(8,128)S(1)}, f32[16,16,1024]{2,1,0:T(8,128)S(1)}, u32[]{:S(2)}, u32[]{:S(2)}) collective-permute-start(f32[16,16,1024]{2,1,0:T(8,128)S(1)} %bitcast.38), channel_id=1, source_target_pairs={{0,1},{1,0},{2,3},{3,2},{4,5},{5,4},{6,7},{7,6},{8,9},{9,8},{10,11... | collective-permute-start | bytes 3145736 | tf_op jit(solution)/shard_map/ppermute | solution.py:38
  100.1 4.1 %collective-permute-start.8 = (f32[256,512]{1,0:T(8,128)S(1)}, f32[256,512]{1,0:T(8,128)S(1)}, u32[]{:S(2)}, u32[]{:S(2)}) collective-permute-start(f32[256,512]{1,0:T(8,128)S(1)} %bitcast.39), channel_id=1, source_target_pairs={{0,1},{1,0},{2,3},{3,2},{4,5},{5,4},{6,7},{7,6},{8,9},{9,8},{10,11... | collective-permute-start | bytes 1572872 | tf_op jit(solution)/shard_map/ppermute | solution.py:38
  103.2 1.1 copy-start.4
  105.5 3.1 %copy-start = (f32[768,1024]{1,0:T(8,128)S(1)}, f32[768,1024]{1,0:T(8,128)}, u32[]{:S(2)}) copy-start(f32[768,1024]{1,0:T(8,128)} %all-gather.2.cloned.1.call-done) | copy-start | bytes 9437188
Sparse Core Ops, SparseCore 0:
  11.2 78.4 all-gather.1

commit v6 on v5

--- a/solution.py
+++ b/solution.py
@@ -38,22 +38,44 @@
     return lax.ppermute(block, "core", SWAP)
 
 
-def pack_kernel(left, left_cot, right, right_cot, right_pair, left_pair, stacked):
-    right_pair[:, :SIZE_K] = right_cot[...]
-    right_pair[:, SIZE_K:] = right[...]
-    left_pair[:, :SIZE_K] = left[...]
-    left_pair[:, SIZE_K:] = left_cot[...]
-    stacked[:48, :SIZE_K] = right_cot[...]
-    stacked[:48, SIZE_K:] = right[...]
-    stacked[48:, :SIZE_K] = left[...]
-    stacked[48:, SIZE_K:] = left_cot[...]
+def pack_kernel(left, left_cot, right, right_cot, right_pair, left_pair, stacked, held, sems):
+    low, high = pl.ds(0, SIZE_K), pl.ds(SIZE_K, SIZE_K)
+    top, bottom = pl.ds(0, 48), pl.ds(48, 16)
+
+    def start(i, source, target):
+        copy = pltpu.make_async_copy(source, target, sems.at[i])
+        copy.start()
+        return copy
+
+    reads = [
+        start(0, right_cot, held.at[top, low]),
+        start(1, right, held.at[top, high]),
+        start(2, left, held.at[bottom, low]),
+        start(3, left_cot, held.at[bottom, high]),
+    ]
+    for copy in reads:
+        copy.wait()
+    writes = [
+        start(4, held, stacked),
+        start(5, held.at[top, :], right_pair),
+        start(6, held.at[bottom, :], left_pair),
+    ]
+    for copy in writes:
+        copy.wait()
 
 
 def pack(left, left_cot, right, right_cot):
     shapes = ((48, 1024), (16, 1024), (64, 1024))
+    hbm = pl.BlockSpec(memory_space=pl.ANY)
     return pl.pallas_call(
         pack_kernel,
         out_shape=[jax.ShapeDtypeStruct(s, jnp.float32) for s in shapes],
+        in_specs=[hbm] * 4,
+        out_specs=[hbm] * 3,
+        scratch_shapes=[
+            pltpu.VMEM((64, 1024), jnp.float32),
+            pltpu.SemaphoreType.DMA((7,)),
+        ],
         cost_estimate=pl.CostEstimate(flops=0, bytes_accessed=1 << 20, transcendentals=0),
         name="pack",
     )(left, left_cot, right, right_cot)
@@ -115,8 +137,29 @@
         cost_estimate=pl.CostEstimate(
             flops=2 * 6 * 384 * HALF * SIZE_K, bytes_accessed=1 << 20, transcendentals=0
         ),
+        compiler_params=pltpu.CompilerParams(vmem_limit_bytes=12 << 20),
         name="half_core",
     )(core_index.reshape(1), own, got, singular.reshape(1, -1))
+
+
+def place_kernel(z, below, own, above, mid_below, mid_above, last_above, out):
+    blocks = [own[...], above[...], mid_above[0], mid_above[1], last_above[...]]
+    blocks = blocks + [mid_below[0], mid_below[1], below[...]]
+    for i, block in enumerate(blocks):
+        out[lax.rem(z[0] + i, 8)] = block
+
+
+def place(z, *blocks):
+    vmem = pl.BlockSpec(memory_space=pltpu.VMEM)
+    return pl.pallas_call(
+        place_kernel,
+        out_shape=jax.ShapeDtypeStruct((8,) + blocks[1].shape, jnp.float32),
+        in_specs=[pl.BlockSpec(memory_space=pltpu.SMEM)] + [vmem] * 6,
+        out_specs=vmem,
+        cost_estimate=pl.CostEstimate(flops=0, bytes_accessed=2 << 20, transcendentals=0),
+        compiler_params=pltpu.CompilerParams(vmem_limit_bytes=8 << 20),
+        name="place",
+    )(z.reshape(1), *blocks)
 
 
 def local(left, left_cot, right, right_cot, singular, singular_cot):
@@ -134,14 +177,11 @@
     own = jnp.stack([jnp.where(at_low, left_pair, other), jnp.where(at_low, other, left_pair)])
     below, above = shift(own, "z", 8, 1), shift(own, "z", 8, -1)
 
-    below, above, rows = lax.optimization_barrier((below, above, jnp.sum(pieces, axis=0)))
-    pieces = gather(rows, INNER, 8)
     mid_below = shift(jnp.stack([below, own]), "z", 8, 2)
     mid_above = shift(jnp.stack([own, above]), "z", 8, -2)
+    pieces = gather(jnp.sum(pieces, axis=0), INNER, 8)
     last_above = shift(mid_above[1], "z", 8, -1)
-    ring = [own[None], above[None], mid_above, last_above[None], mid_below, below[None]]
-    line = jnp.concatenate(ring + ring, axis=0)
-    line = lax.dynamic_slice_in_dim(line, 8 - lax.axis_index("z"), 8, 0)
+    line = place(lax.axis_index("z"), below, own, above, mid_below, mid_above, last_above)
     line = line.reshape(16, 16, 1024)
     rows = jnp.sum(pieces, axis=0)
     own_half = gather(rows, OUTER, 32).reshape(HALF, SIZE_K)

time: 119 us -> 115 us (0.966)
  the two profiles are of different devices: /device:TPU:25 before, /device:TPU:1 now
where the time goes in v6:
time: 115 us; the launch traced here: 114 us
  starting transfers between devices  61.1 us (53%)
  waiting for transfers between devices  23.1 us (20%)
  between operations  13.7 us (12%)
  matrix products  6.82 us (6%)
  Pallas kernels  3.78 us (3%)
  local copies, waits for them, and re-layouts  3.74 us (3%)
  other arithmetic  1.95 us (2%)
    ppermute x3, starting transfers between devices, swap(): return lax.ppermute(block, 'core', SWAP)  19.9 us
    ppermute x6, starting transfers between devices, shift(): lax.ppermute(block, axis, [(i, (i + by) % size) for i in range(size)])  19.8 us
    all_to_all x2, starting transfers between devices, gather(): return lax.all_to_all(copies, axis, 0, 0)  13.9 us
    ppermute x6, waiting for transfers between devices, shift(): lax.ppermute(block, axis, [(i, (i + by) % size) for i in range(size)])  13.3 us
    all_to_all x2, waiting for transfers between devices, gather(): return lax.all_to_all(copies, axis, 0, 0)  8.2 us
    all_to_all x1, starting transfers between devices, local(): pieces = lax.all_to_all(mine.reshape(32, 8, SIZE_K), OUTER, 0, 0)  7.54 us
    dot_general x3, matrix products, dot(): lax.dot_general(a, b, (contract, ((), ())), precision=precision, preferre...  6.82 us
  transfers between devices with their start and end apart: 13, of which 6 were waited for; matrix products, arithmetic and copies ran while one was open for 4% of the time, Pallas kernels for 2%

profile of v6, /device:TPU:1, one launch (start us, length us, event | category | flops | bytes accessed | tf_op | source)
XLA Modules:
  0.0 114.2 jit_solution(15321219476919560237)
XLA Ops:
  6.5 1.8 %pack.1 = (f32[48,1024]{1,0:T(8,128)}, f32[16,1024]{1,0:T(8,128)}, f32[64,1024]{1,0:T(8,128)}) custom-call(f32[16,512]{1,0:T(8,128)} %left.1, f32[16,512]{1,0:T(8,128)} %left_cot.1, f32[48,512]{1,0:T(8,128)} %right.1, f32[48,512]{1,0:T(8,128)} %right_cot.1), custom_call_target="tpu_custom_call" | custom-call | bytes 1048576 | tf_op jit(solution)/shard_map/pack/pallas_call | solution.py:70
  8.4 8.7 %collective-permute-start.7 = (f32[64,1024]{1,0:T(8,128)}, f32[64,1024]{1,0:T(8,128)S(1)}, u32[]{:S(2)}, u32[]{:S(2)}) collective-permute-start(f32[64,1024]{1,0:T(8,128)} %get-tuple-element.10.own), channel_id=1, source_target_pairs={{0,1},{1,0},{2,3},{3,2},{4,5},{5,4},{6,7},{7,6},{8,9},{9,8},{10,11... | collective-permute-start | bytes 786440 | tf_op jit(solution)/shard_map/ppermute | solution.py:38
  17.1 1.3 %collective-permute-done.7.got = f32[64,1024]{1,0:T(8,128)S(1)} collective-permute-done((f32[64,1024]{1,0:T(8,128)}, f32[64,1024]{1,0:T(8,128)S(1)}, u32[]{:S(2)}, u32[]{:S(2)}) %collective-permute-start.7) | collective-permute-done | bytes 262176 | tf_op jit(solution)/shard_map/ppermute | solution.py:38
  18.5 0.7 copy-done
  19.2 0.9 copy-done.2
  20.1 1.9 %half_core.1 = f32[256,512]{1,0:T(8,128)} custom-call(s32[1]{0:T(128)} %bitcast.12.core_index, f32[64,1024]{1,0:T(8,128)S(1)} %copy-done.2, f32[64,1024]{1,0:T(8,128)S(1)} %collective-permute-done.7.got, f32[1,512]{1,0:T(1,128)S(1)} %bitcast.31), custom_call_target="tpu_custom_call" | custom-call | flops 603979776 | bytes 1048576 | tf_op jit(solution)/shard_map/half_core/pallas_call | solution.py:126
  22.0 7.5 %all-to-all-start = ((f32[32,8,512]{2,1,0:T(8,128)}), f32[32,8,512]{2,1,0:T(8,128)S(1)}, u32[]{:S(2)}, u32[]{:S(2)}) async-start(f32[32,8,512]{2,1,0:T(8,128)} %bitcast.14), calls=%async_computation | async-start | bytes 1048576 | tf_op jit(solution)/shard_map/all_to_all | solution.py:175
  29.6 3.2 %collective-permute-start = (f32[16,1024]{1,0:T(8,128)S(1)}, f32[16,1024]{1,0:T(8,128)S(1)}, u32[]{:S(2)}, u32[]{:S(2)}) collective-permute-start(f32[16,1024]{1,0:T(8,128)S(1)} %copy-done.4), channel_id=1, source_target_pairs={{0,2},{2,0},{1,3},{3,1},{4,6},{6,4},{5,7},{7,5},{8,10},{10,8},{9,1... | collective-permute-start | bytes 196616 | tf_op jit(solution)/shard_map/ppermute | solution.py:34
  32.8 4.6 %collective-permute-done = f32[16,1024]{1,0:T(8,128)S(1)} collective-permute-done((f32[16,1024]{1,0:T(8,128)S(1)}, f32[16,1024]{1,0:T(8,128)S(1)}, u32[]{:S(2)}, u32[]{:S(2)}) %collective-permute-start) | collective-permute-done | bytes 65568 | tf_op jit(solution)/shard_map/ppermute | solution.py:34
  37.4 2.8 %collective-permute-start.1 = (f32[2,16,1024]{2,1,0:T(8,128)S(1)}, f32[2,16,1024]{2,1,0:T(8,128)S(1)}, u32[]{:S(2)}, u32[]{:S(2)}) collective-permute-start(f32[2,16,1024]{2,1,0:T(8,128)S(1)} %get-tuple-element.18.own), channel_id=1, source_target_pairs={{0,4},{4,8},{8,12},{12,16},{16,20},{20,24},{24,28},{28,0},{1,5},{5... | collective-permute-start | bytes 393224 | tf_op jit(solution)/shard_map/ppermute | solution.py:34
  40.3 3.7 %collective-permute-start.2 = (f32[2,16,1024]{2,1,0:T(8,128)S(1)}, f32[2,16,1024]{2,1,0:T(8,128)S(1)}, u32[]{:S(2)}, u32[]{:S(2)}) collective-permute-start(f32[2,16,1024]{2,1,0:T(8,128)S(1)} %get-tuple-element.18.own), channel_id=1, source_target_pairs={{0,28},{4,0},{8,4},{12,8},{16,12},{20,16},{24,20},{28,24},{1,29},{... | collective-permute-start | bytes 393224 | tf_op jit(solution)/shard_map/ppermute | solution.py:34
  43.9 3.1 %collective-permute-done.1.below = f32[2,16,1024]{2,1,0:T(8,128)S(1)} collective-permute-done((f32[2,16,1024]{2,1,0:T(8,128)S(1)}, f32[2,16,1024]{2,1,0:T(8,128)S(1)}, u32[]{:S(2)}, u32[]{:S(2)}) %collective-permute-start.1) | collective-permute-done | bytes 131104 | tf_op jit(solution)/shard_map/ppermute | solution.py:34
  47.1 3.6 %collective-permute-start.4 = (f32[2,2,16,1024]{3,2,1,0:T(8,128)S(1)}, f32[2,2,16,1024]{3,2,1,0:T(8,128)S(1)}, u32[]{:S(2)}, u32[]{:S(2)}) collective-permute-start(f32[2,2,16,1024]{3,2,1,0:T(8,128)S(1)} %get-tuple-element.15), channel_id=1, source_target_pairs={{0,24},{4,28},{8,0},{12,4},{16,8},{20,12},{24,16},{28,20},{1,25},{... | collective-permute-start | bytes 786440 | tf_op jit(solution)/shard_map/ppermute | solution.py:34
  50.7 0.7 broadcast_in_dim.31
  51.4 7.6 %all-to-all-start.1 = ((f32[8,8,512]{2,1,0:T(8,128)}), f32[8,8,512]{2,1,0:T(8,128)S(1)}, u32[]{:S(2)}, u32[]{:S(2)}) async-start(f32[8,8,512]{2,1,0:T(8,128)} %broadcast_in_dim.31), calls=%async_computation.1 | async-start | bytes 262144 | tf_op jit(solution)/shard_map/all_to_all | solution.py:30
  59.1 2.2 %collective-permute-start.3 = (f32[2,2,16,1024]{3,2,1,0:T(8,128)S(1)}, f32[2,2,16,1024]{3,2,1,0:T(8,128)S(1)}, u32[]{:S(2)}, u32[]{:S(2)}) collective-permute-start(f32[2,2,16,1024]{3,2,1,0:T(8,128)S(1)} %get-tuple-element.16), channel_id=1, source_target_pairs={{0,8},{4,12},{8,16},{12,20},{16,24},{20,28},{24,0},{28,4},{1,9},{5... | collective-permute-start | bytes 786440 | tf_op jit(solution)/shard_map/ppermute | solution.py:34
  61.3 8.2 %all-to-all-done.1 = f32[8,8,512]{2,1,0:T(8,128)S(1)} async-done(((f32[8,8,512]{2,1,0:T(8,128)}), f32[8,8,512]{2,1,0:T(8,128)S(1)}, u32[]{:S(2)}, u32[]{:S(2)}) %all-to-all-start.1) | async-done | bytes 131104 | tf_op jit(solution)/shard_map/all_to_all | solution.py:30
  69.5 0.9 broadcast_in_dim.32
  70.3 6.2 %all-to-all-start.2 = ((f32[32,8,512]{2,1,0:T(8,128)}), f32[32,8,512]{2,1,0:T(8,128)S(1)}, u32[]{:S(2)}, u32[]{:S(2)}) async-start(f32[32,8,512]{2,1,0:T(8,128)} %broadcast_in_dim.32), calls=%async_computation.2 | async-start | bytes 1048576 | tf_op jit(solution)/shard_map/all_to_all | solution.py:30
  76.6 4.4 %collective-permute-start.5 = (f32[2,16,1024]{2,1,0:T(8,128)S(1)}, f32[2,16,1024]{2,1,0:T(8,128)S(1)}, u32[]{:S(2)}, u32[]{:S(2)}) collective-permute-start(f32[2,16,1024]{2,1,0:T(8,128)S(1)} %slice_bitcast_fusion), channel_id=1, source_target_pairs={{0,28},{4,0},{8,4},{12,8},{16,12},{20,16},{24,20},{28,24},{1,29},{... | collective-permute-start | bytes 393224 | tf_op jit(solution)/shard_map/ppermute | solution.py:34
  81.0 5.6 %collective-permute-done.5.last_above = f32[2,16,1024]{2,1,0:T(8,128)S(1)} collective-permute-done((f32[2,16,1024]{2,1,0:T(8,128)S(1)}, f32[2,16,1024]{2,1,0:T(8,128)S(1)}, u32[]{:S(2)}, u32[]{:S(2)}) %collective-permute-start.5) | collective-permute-done | bytes 131104 | tf_op jit(solution)/shard_map/ppermute | solution.py:34
  86.5 0.1 place.1
  86.6 9.0 %collective-permute-start.6 = (f32[16,16,1024]{2,1,0:T(8,128)S(1)}, f32[16,16,1024]{2,1,0:T(8,128)}, u32[]{:S(2)}, u32[]{:S(2)}) collective-permute-start(f32[16,16,1024]{2,1,0:T(8,128)S(1)} %bitcast.28), channel_id=1, source_target_pairs={{0,1},{1,0},{2,3},{3,2},{4,5},{5,4},{6,7},{7,6},{8,9},{9,8},{10,11... | collective-permute-start | bytes 3145736 | tf_op jit(solution)/shard_map/ppermute | solution.py:38
  95.6 2.1 %collective-permute-start.8 = (f32[256,512]{1,0:T(8,128)S(1)}, f32[256,512]{1,0:T(8,128)S(1)}, u32[]{:S(2)}, u32[]{:S(2)}) collective-permute-start(f32[256,512]{1,0:T(8,128)S(1)} %bitcast.34), channel_id=1, source_target_pairs={{0,1},{1,0},{2,3},{3,2},{4,5},{5,4},{6,7},{7,6},{8,9},{9,8},{10,11... | collective-permute-start | bytes 1572872 | tf_op jit(solution)/shard_map/ppermute | solution.py:38
  97.8 0.2 collective-permute-done.6
  98.0 1.5 %select_bitcast_fusion.1 = (f32[16,1,16,1024]{3,2,1,0:T(8,128)S(1)}, f32[16,1,16,1024]{3,2,1,0:T(8,128)S(1)}) fusion(f32[16,16,1024]{2,1,0:T(8,128)} %collective-permute-done.6, pred[]{:T(512)S(6)} %eq.10, f32[8,2,16,1024]{3,2,1,0:T(8,128)S(1)} %place.1), kind=kLoop, calls=%fused_computation.15 | loop fusion | flops 524288 | bytes 4194305 | tf_op jit(solution)/shard_map/stack | solution.py:189
  99.5 0.2 pad_maximum_fusion
  99.8 0.1 broadcast_select_fusion.1
  99.9 0.6 copy-done.5
  100.5 1.1 convolution_add_fusion
  101.6 3.0 %fusion.2 = f32[512,768]{1,0:T(8,128)S(1)} fusion(f32[768,1024]{1,0:T(8,128)} %all-gather.2.cloned.1.call-done, f32[512,1024]{1,0:T(8,128)S(1)} %bitcast.33, f32[512]{0:T(512)S(1)} %broadcast_divide_fusion), kind=kOutput, calls=%fused_computation.3 | convolution fusion | flops 1208221696 | bytes 4196352 | tf_op jit(solution)/shard_map/dot_general | solution.py:23
  104.7 2.7 %fusion.4 = f32[512,768]{1,0:T(8,128)} fusion(f32[512,768]{1,0:T(8,128)S(1)} %fusion.2, f32[512,512]{1,0:T(8,128)S(1)} %convolution_add_fusion, f32[768,1024]{1,0:T(8,128)S(1)} %copy-done.3), kind=kOutput, calls=%fused_computation.5 | convolution fusion | flops 1208352768 | bytes 5767168 | tf_op jit(solution)/shard_map/dot_general | solution.py:23
  (25 shorter events, 0.2 us)
Async XLA Ops:
  6.5 95.1 %all-gather.2.cloned.1.call-start = ((), (), s32[]{:S(2)}) async-start(), calls=%async_computation.3 | async-start | bytes 3342336 | tf_op jit(solution)/shard_map/all_gather | solution.py:171
  8.3 21.2 %copy-start.4 = (f32[16,1024]{1,0:T(8,128)S(1)}, f32[16,1024]{1,0:T(8,128)}, u32[]{:S(2)}) copy-start(f32[16,1024]{1,0:T(8,128)} %get-tuple-element.8) | copy-start | bytes 196612
  8.4 10.1 %collective-permute-start.7 = (f32[64,1024]{1,0:T(8,128)}, f32[64,1024]{1,0:T(8,128)S(1)}, u32[]{:S(2)}, u32[]{:S(2)}) collective-permute-start(f32[64,1024]{1,0:T(8,128)} %get-tuple-element.10.own), channel_id=1, source_target_pairs={{0,1},{1,0},{2,3},{3,2},{4,5},{5,4},{6,7},{7,6},{8,9},{9,8},{10,11... | collective-permute-start | bytes 786440 | tf_op jit(solution)/shard_map/ppermute | solution.py:38
  18.5 0.7 copy-start
  19.2 0.9 copy-start.2
  22.0 28.7 %all-to-all-start = ((f32[32,8,512]{2,1,0:T(8,128)}), f32[32,8,512]{2,1,0:T(8,128)S(1)}, u32[]{:S(2)}, u32[]{:S(2)}) async-start(f32[32,8,512]{2,1,0:T(8,128)} %bitcast.14), calls=%async_computation | async-start | bytes 1048576 | tf_op jit(solution)/shard_map/all_to_all | solution.py:175
  29.6 7.8 %collective-permute-start = (f32[16,1024]{1,0:T(8,128)S(1)}, f32[16,1024]{1,0:T(8,128)S(1)}, u32[]{:S(2)}, u32[]{:S(2)}) collective-permute-start(f32[16,1024]{1,0:T(8,128)S(1)} %copy-done.4), channel_id=1, source_target_pairs={{0,2},{2,0},{1,3},{3,1},{4,6},{6,4},{5,7},{7,5},{8,10},{10,8},{9,1... | collective-permute-start | bytes 196616 | tf_op jit(solution)/shard_map/ppermute | solution.py:34
  37.4 9.6 %collective-permute-start.1 = (f32[2,16,1024]{2,1,0:T(8,128)S(1)}, f32[2,16,1024]{2,1,0:T(8,128)S(1)}, u32[]{:S(2)}, u32[]{:S(2)}) collective-permute-start(f32[2,16,1024]{2,1,0:T(8,128)S(1)} %get-tuple-element.18.own), channel_id=1, source_target_pairs={{0,4},{4,8},{8,12},{12,16},{16,20},{20,24},{24,28},{28,0},{1,5},{5... | collective-permute-start | bytes 393224 | tf_op jit(solution)/shard_map/ppermute | solution.py:34
  40.3 6.8 %collective-permute-start.2 = (f32[2,16,1024]{2,1,0:T(8,128)S(1)}, f32[2,16,1024]{2,1,0:T(8,128)S(1)}, u32[]{:S(2)}, u32[]{:S(2)}) collective-permute-start(f32[2,16,1024]{2,1,0:T(8,128)S(1)} %get-tuple-element.18.own), channel_id=1, source_target_pairs={{0,28},{4,0},{8,4},{12,8},{16,12},{20,16},{24,20},{28,24},{1,29},{... | collective-permute-start | bytes 393224 | tf_op jit(solution)/shard_map/ppermute | solution.py:34
  47.1 29.5 %collective-permute-start.4 = (f32[2,2,16,1024]{3,2,1,0:T(8,128)S(1)}, f32[2,2,16,1024]{3,2,1,0:T(8,128)S(1)}, u32[]{:S(2)}, u32[]{:S(2)}) collective-permute-start(f32[2,2,16,1024]{3,2,1,0:T(8,128)S(1)} %get-tuple-element.15), channel_id=1, source_target_pairs={{0,24},{4,28},{8,0},{12,4},{16,8},{20,12},{24,16},{28,20},{1,25},{... | collective-permute-start | bytes 786440 | tf_op jit(solution)/shard_map/ppermute | solution.py:34
  51.4 18.1 %all-to-all-start.1 = ((f32[8,8,512]{2,1,0:T(8,128)}), f32[8,8,512]{2,1,0:T(8,128)S(1)}, u32[]{:S(2)}, u32[]{:S(2)}) async-start(f32[8,8,512]{2,1,0:T(8,128)} %broadcast_in_dim.31), calls=%async_computation.1 | async-start | bytes 262144 | tf_op jit(solution)/shard_map/all_to_all | solution.py:30
  59.0 38.7 %copy-start.1 = (f32[512]{0:T(512)S(1)}, f32[512]{0:T(512)}, u32[]{:S(2)}) copy-start(f32[512]{0:T(512)} %param.10) | copy-start | bytes 6148
  59.1 21.9 %collective-permute-start.3 = (f32[2,2,16,1024]{3,2,1,0:T(8,128)S(1)}, f32[2,2,16,1024]{3,2,1,0:T(8,128)S(1)}, u32[]{:S(2)}, u32[]{:S(2)}) collective-permute-start(f32[2,2,16,1024]{3,2,1,0:T(8,128)S(1)} %get-tuple-element.16), channel_id=1, source_target_pairs={{0,8},{4,12},{8,16},{12,20},{16,24},{20,28},{24,0},{28,4},{1,9},{5... | collective-permute-start | bytes 786440 | tf_op jit(solution)/shard_map/ppermute | solution.py:34
  70.3 25.3 %all-to-all-start.2 = ((f32[32,8,512]{2,1,0:T(8,128)}), f32[32,8,512]{2,1,0:T(8,128)S(1)}, u32[]{:S(2)}, u32[]{:S(2)}) async-start(f32[32,8,512]{2,1,0:T(8,128)} %broadcast_in_dim.32), calls=%async_computation.2 | async-start | bytes 1048576 | tf_op jit(solution)/shard_map/all_to_all | solution.py:30
  76.6 9.9 %collective-permute-start.5 = (f32[2,16,1024]{2,1,0:T(8,128)S(1)}, f32[2,16,1024]{2,1,0:T(8,128)S(1)}, u32[]{:S(2)}, u32[]{:S(2)}) collective-permute-start(f32[2,16,1024]{2,1,0:T(8,128)S(1)} %slice_bitcast_fusion), channel_id=1, source_target_pairs={{0,28},{4,0},{8,4},{12,8},{16,12},{20,16},{24,20},{28,24},{1,29},{... | collective-permute-start | bytes 393224 | tf_op jit(solution)/shard_map/ppermute | solution.py:34
  86.6 11.4 %collective-permute-start.6 = (f32[16,16,1024]{2,1,0:T(8,128)S(1)}, f32[16,16,1024]{2,1,0:T(8,128)}, u32[]{:S(2)}, u32[]{:S(2)}) collective-permute-start(f32[16,16,1024]{2,1,0:T(8,128)S(1)} %bitcast.28), channel_id=1, source_target_pairs={{0,1},{1,0},{2,3},{3,2},{4,5},{5,4},{6,7},{7,6},{8,9},{9,8},{10,11... | collective-permute-start | bytes 3145736 | tf_op jit(solution)/shard_map/ppermute | solution.py:38
  95.6 4.1 %collective-permute-start.8 = (f32[256,512]{1,0:T(8,128)S(1)}, f32[256,512]{1,0:T(8,128)S(1)}, u32[]{:S(2)}, u32[]{:S(2)}) collective-permute-start(f32[256,512]{1,0:T(8,128)S(1)} %bitcast.34), channel_id=1, source_target_pairs={{0,1},{1,0},{2,3},{3,2},{4,5},{5,4},{6,7},{7,6},{8,9},{9,8},{10,11... | collective-permute-start | bytes 1572872 | tf_op jit(solution)/shard_map/ppermute | solution.py:38
  99.8 0.7 copy-start.5
  101.6 3.1 %copy-start.3 = (f32[768,1024]{1,0:T(8,128)S(1)}, f32[768,1024]{1,0:T(8,128)}, u32[]{:S(2)}) copy-start(f32[768,1024]{1,0:T(8,128)} %all-gather.2.cloned.1.call-done) | copy-start | bytes 9437188
Sparse Core Ops, SparseCore 0:
  10.4 80.3 all-gather.1

commit v7 on v6

--- a/solution.py
+++ b/solution.py
@@ -149,45 +149,49 @@
         out[lax.rem(z[0] + i, 8)] = block
 
 
-def place(z, *blocks):
+def merge_kernel(index, mine, theirs, out):
+    out[:, index[0]] = mine[...]
+    out[:, 1 - index[0]] = theirs[...]
+
+
+def assemble(kernel, shape, index, *blocks):
     vmem = pl.BlockSpec(memory_space=pltpu.VMEM)
     return pl.pallas_call(
-        place_kernel,
-        out_shape=jax.ShapeDtypeStruct((8,) + blocks[1].shape, jnp.float32),
-        in_specs=[pl.BlockSpec(memory_space=pltpu.SMEM)] + [vmem] * 6,
+        kernel,
+        out_shape=jax.ShapeDtypeStruct(shape, jnp.float32),
+        in_specs=[pl.BlockSpec(memory_space=pltpu.SMEM)] + [vmem] * len(blocks),
         out_specs=vmem,
         cost_estimate=pl.CostEstimate(flops=0, bytes_accessed=2 << 20, transcendentals=0),
-        compiler_params=pltpu.CompilerParams(vmem_limit_bytes=8 << 20),
-        name="place",
-    )(z.reshape(1), *blocks)
+        compiler_params=pltpu.CompilerParams(vmem_limit_bytes=10 << 20),
+    )(index.reshape(1), *blocks)
 
 
 def local(left, left_cot, right, right_cot, singular, singular_cot):
     core_index = lax.axis_index("core")
     first = core_index == 0
-    at_low = lax.axis_index("yl") == 0
 
     right_pair, left_pair, stacked = pack(left, left_cot, right, right_cot)
     rights = lax.all_gather(right_pair, ROW, axis=0, tiled=True)
-    other = shift(left_pair, "yl", 2, 1)
     got = swap(stacked)
     mine = half_core(core_index, stacked, got, singular)
     pieces = lax.all_to_all(mine.reshape(32, 8, SIZE_K), OUTER, 0, 0)
 
-    own = jnp.stack([jnp.where(at_low, left_pair, other), jnp.where(at_low, other, left_pair)])
+    own = left_pair
     below, above = shift(own, "z", 8, 1), shift(own, "z", 8, -1)
-
     mid_below = shift(jnp.stack([below, own]), "z", 8, 2)
     mid_above = shift(jnp.stack([own, above]), "z", 8, -2)
     pieces = gather(jnp.sum(pieces, axis=0), INNER, 8)
     last_above = shift(mid_above[1], "z", 8, -1)
-    line = place(lax.axis_index("z"), below, own, above, mid_below, mid_above, last_above)
-    line = line.reshape(16, 16, 1024)
+    blocks = (below, own, above, mid_below, mid_above, last_above)
+    line = assemble(place_kernel, (8, 16, 1024), lax.axis_index("z"), *blocks)
+    other_line = shift(line, "yl", 2, 1)
+    plane = assemble(merge_kernel, (8, 2, 16, 1024), lax.axis_index("yl"), line, other_line)
+    plane = plane.reshape(16, 16, 1024)
     rows = jnp.sum(pieces, axis=0)
     own_half = gather(rows, OUTER, 32).reshape(HALF, SIZE_K)
-    other_line = swap(line)
-    lefts = jnp.stack(
-        [jnp.where(first, line, other_line), jnp.where(first, other_line, line)], axis=1
+    other_plane = swap(plane)
+    lefts = assemble(
+        merge_kernel, (16, 2, 16, 1024), core_index, plane, other_plane
     ).reshape(-1, 1024)
     other_half = swap(own_half)
     core = jnp.concatenate(

time: 115 us -> 123 us (1.070)
  waiting for transfers between devices: 23.1 us -> 32.2 us
  starting transfers between devices: 61.1 us -> 59 us
  local copies, waits for them, and re-layouts: 3.74 us -> 5.37 us
    ppermute x6, waiting for transfers between devices: 13.3 us -> 30.5 us  [shift(): lax.ppermute(block, axis, [(i, (i + by) % size) for i in range(size)])]
    all_to_all x2, waiting for transfers between devices: 8.2 us -> 0.01 us  [gather(): return lax.all_to_all(copies, axis, 0, 0)]
    ppermute x3, starting transfers between devices: 19.9 us -> 13.5 us  [swap(): return lax.ppermute(block, 'core', SWAP)]
    all_to_all x2, starting transfers between devices: 13.9 us -> 17.4 us  [gather(): return lax.all_to_all(copies, axis, 0, 0)]
    another operation x4 -> x0, other arithmetic: 1.76 us -> none  [the longest x2 1.73 us: local(): jnp.stack([jnp.where(first, line, other_line), jnp.where(first, other_lin...]
    unnamed x12 -> x16, local copies, waits for them, and re-layouts: 2.21 us -> 3.84 us
  transfers between devices with their start and end apart: 13 -> 13, of which waited for: 6 -> 5; matrix products, arithmetic and copies ran while one was open for 4% -> 3% of each run, Pallas kernels for 2% -> 2%
where the time goes in v7:
time: 123 us; the launch traced here: 122 us
  starting transfers between devices  59 us (48%)
  waiting for transfers between devices  32.2 us (26%)
  between operations  13.7 us (11%)
  matrix products  6.81 us (6%)
  local copies, waits for them, and re-layouts  5.37 us (4%)
  Pallas kernels  3.95 us (3%)
  other arithmetic  1.38 us (1%)
    ppermute x6, waiting for transfers between devices, shift(): lax.ppermute(block, axis, [(i, (i + by) % size) for i in range(size)])  30.5 us
    ppermute x6, starting transfers between devices, shift(): lax.ppermute(block, axis, [(i, (i + by) % size) for i in range(size)])  20.6 us
    all_to_all x2, starting transfers between devices, gather(): return lax.all_to_all(copies, axis, 0, 0)  17.4 us
    ppermute x3, starting transfers between devices, swap(): return lax.ppermute(block, 'core', SWAP)  13.5 us
    all_to_all x1, starting transfers between devices, local(): pieces = lax.all_to_all(mine.reshape(32, 8, SIZE_K), OUTER, 0, 0)  7.54 us
    dot_general x3, matrix products, dot(): lax.dot_general(a, b, (contract, ((), ())), precision=precision, preferre...  6.81 us
    unnamed x16, local copies, waits for them, and re-layouts  3.84 us
  transfers between devices with their start and end apart: 13, of which 5 were waited for; matrix products, arithmetic and copies ran while one was open for 3% of the time, Pallas kernels for 2%

profile of v7, /device:TPU:1, one launch (start us, length us, event | category | flops | bytes accessed | tf_op | source)
XLA Modules:
  0.0 122.5 jit_solution(10246825606706739990)
XLA Ops:
  6.5 1.8 %pack.1 = (f32[48,1024]{1,0:T(8,128)}, f32[16,1024]{1,0:T(8,128)}, f32[64,1024]{1,0:T(8,128)}) custom-call(f32[16,512]{1,0:T(8,128)} %left.1, f32[16,512]{1,0:T(8,128)} %left_cot.1, f32[48,512]{1,0:T(8,128)} %right.1, f32[48,512]{1,0:T(8,128)} %right_cot.1), custom_call_target="tpu_custom_call" | custom-call | bytes 1048576 | tf_op jit(solution)/shard_map/pack/pallas_call | solution.py:70
  8.4 8.7 %collective-permute-start.7 = (f32[64,1024]{1,0:T(8,128)}, f32[64,1024]{1,0:T(8,128)S(1)}, u32[]{:S(2)}, u32[]{:S(2)}) collective-permute-start(f32[64,1024]{1,0:T(8,128)} %get-tuple-element.10.own), channel_id=1, source_target_pairs={{0,1},{1,0},{2,3},{3,2},{4,5},{5,4},{6,7},{7,6},{8,9},{9,8},{10,11... | collective-permute-start | bytes 786440 | tf_op jit(solution)/shard_map/ppermute | solution.py:38
  17.1 1.3 %collective-permute-done.7.got = f32[64,1024]{1,0:T(8,128)S(1)} collective-permute-done((f32[64,1024]{1,0:T(8,128)}, f32[64,1024]{1,0:T(8,128)S(1)}, u32[]{:S(2)}, u32[]{:S(2)}) %collective-permute-start.7) | collective-permute-done | bytes 262176 | tf_op jit(solution)/shard_map/ppermute | solution.py:38
  18.5 0.7 copy-done.3
  19.1 0.9 copy-done.5
  20.1 1.9 %half_core.1 = f32[256,512]{1,0:T(8,128)} custom-call(s32[1]{0:T(128)} %bitcast.index.core_index, f32[64,1024]{1,0:T(8,128)S(1)} %copy-done.5, f32[64,1024]{1,0:T(8,128)S(1)} %collective-permute-done.7.got, f32[1,512]{1,0:T(1,128)S(1)} %bitcast.23), custom_call_target="tpu_custom_call" | custom-call | flops 603979776 | bytes 1048576 | tf_op jit(solution)/shard_map/half_core/pallas_call | solution.py:126
  22.0 7.5 %all-to-all-start = ((f32[32,8,512]{2,1,0:T(8,128)}), f32[32,8,512]{2,1,0:T(8,128)S(1)}, u32[]{:S(2)}, u32[]{:S(2)}) async-start(f32[32,8,512]{2,1,0:T(8,128)} %bitcast.10), calls=%async_computation | async-start | bytes 1048576 | tf_op jit(solution)/shard_map/all_to_all | solution.py:177
  29.6 3.1 %collective-permute-start = (f32[16,1024]{1,0:T(8,128)S(1)}, f32[16,1024]{1,0:T(8,128)S(1)}, u32[]{:S(2)}, u32[]{:S(2)}) collective-permute-start(f32[16,1024]{1,0:T(8,128)S(1)} %copy-done.2), channel_id=1, source_target_pairs={{0,4},{4,8},{8,12},{12,16},{16,20},{20,24},{24,28},{28,0},{1,5},{5... | collective-permute-start | bytes 196616 | tf_op jit(solution)/shard_map/ppermute | solution.py:34
  32.7 3.4 %collective-permute-start.1 = (f32[16,1024]{1,0:T(8,128)S(1)}, f32[16,1024]{1,0:T(8,128)S(1)}, u32[]{:S(2)}, u32[]{:S(2)}) collective-permute-start(f32[16,1024]{1,0:T(8,128)S(1)} %copy-done.2), channel_id=1, source_target_pairs={{0,28},{4,0},{8,4},{12,8},{16,12},{20,16},{24,20},{28,24},{1,29},{... | collective-permute-start | bytes 196616 | tf_op jit(solution)/shard_map/ppermute | solution.py:34
  36.1 7.8 %collective-permute-done.below = f32[16,1024]{1,0:T(8,128)S(1)} collective-permute-done((f32[16,1024]{1,0:T(8,128)S(1)}, f32[16,1024]{1,0:T(8,128)S(1)}, u32[]{:S(2)}, u32[]{:S(2)}) %collective-permute-start) | collective-permute-done | bytes 65568 | tf_op jit(solution)/shard_map/ppermute | solution.py:34
  43.9 4.8 %collective-permute-start.3 = (f32[2,16,1024]{2,1,0:T(8,128)S(1)}, f32[2,16,1024]{2,1,0:T(8,128)S(1)}, u32[]{:S(2)}, u32[]{:S(2)}) collective-permute-start(f32[2,16,1024]{2,1,0:T(8,128)S(1)} %get-tuple-element.13), channel_id=1, source_target_pairs={{0,24},{4,28},{8,0},{12,4},{16,8},{20,12},{24,16},{28,20},{1,25},{... | collective-permute-start | bytes 393224 | tf_op jit(solution)/shard_map/ppermute | solution.py:34
  48.7 1.9 %collective-permute-start.2 = (f32[2,16,1024]{2,1,0:T(8,128)S(1)}, f32[2,16,1024]{2,1,0:T(8,128)S(1)}, u32[]{:S(2)}, u32[]{:S(2)}) collective-permute-start(f32[2,16,1024]{2,1,0:T(8,128)S(1)} %get-tuple-element.14), channel_id=1, source_target_pairs={{0,8},{4,12},{8,16},{12,20},{16,24},{20,28},{24,0},{28,4},{1,9},{5... | collective-permute-start | bytes 393224 | tf_op jit(solution)/shard_map/ppermute | solution.py:34
  50.7 0.7 broadcast_in_dim.31
  51.4 6.8 %all-to-all-start.1 = ((f32[8,8,512]{2,1,0:T(8,128)}), f32[8,8,512]{2,1,0:T(8,128)S(1)}, u32[]{:S(2)}, u32[]{:S(2)}) async-start(f32[8,8,512]{2,1,0:T(8,128)} %broadcast_in_dim.31), calls=%async_computation.1 | async-start | bytes 262144 | tf_op jit(solution)/shard_map/all_to_all | solution.py:30
  58.2 4.0 %collective-permute-start.4 = (f32[16,1024]{1,0:T(8,128)S(1)}, f32[16,1024]{1,0:T(8,128)S(1)}, u32[]{:S(2)}, u32[]{:S(2)}) collective-permute-start(f32[16,1024]{1,0:T(8,128)S(1)} %slice_bitcast_fusion), channel_id=1, source_target_pairs={{0,28},{4,0},{8,4},{12,8},{16,12},{20,16},{24,20},{28,24},{1,29},{... | collective-permute-start | bytes 196616 | tf_op jit(solution)/shard_map/ppermute | solution.py:34
  62.2 1.7 %collective-permute-done.4.last_above = f32[16,1024]{1,0:T(8,128)S(1)} collective-permute-done((f32[16,1024]{1,0:T(8,128)S(1)}, f32[16,1024]{1,0:T(8,128)S(1)}, u32[]{:S(2)}, u32[]{:S(2)}) %collective-permute-start.4) | collective-permute-done | bytes 65568 | tf_op jit(solution)/shard_map/ppermute | solution.py:34
  64.1 3.4 %collective-permute-start.5 = (f32[8,16,1024]{2,1,0:T(8,128)S(1)}, f32[8,16,1024]{2,1,0:T(8,128)S(1)}, u32[]{:S(2)}, u32[]{:S(2)}) collective-permute-start(f32[8,16,1024]{2,1,0:T(8,128)S(1)} %shard_map.64.mine), channel_id=1, source_target_pairs={{0,2},{2,0},{1,3},{3,1},{4,6},{6,4},{5,7},{7,5},{8,10},{10,8},{9,1... | collective-permute-start | bytes 1572872 | tf_op jit(solution)/shard_map/ppermute | solution.py:34
  67.5 0.9 broadcast_in_dim.32
  68.3 10.6 %all-to-all-start.2 = ((f32[32,8,512]{2,1,0:T(8,128)}), f32[32,8,512]{2,1,0:T(8,128)}, u32[]{:S(2)}, u32[]{:S(2)}) async-start(f32[32,8,512]{2,1,0:T(8,128)} %broadcast_in_dim.32), calls=%async_computation.2 | async-start | bytes 1048576 | tf_op jit(solution)/shard_map/all_to_all | solution.py:30
  78.9 21.0 %collective-permute-done.5.theirs = f32[8,16,1024]{2,1,0:T(8,128)S(1)} collective-permute-done((f32[8,16,1024]{2,1,0:T(8,128)S(1)}, f32[8,16,1024]{2,1,0:T(8,128)S(1)}, u32[]{:S(2)}, u32[]{:S(2)}) %collective-permute-start.5) | collective-permute-done | bytes 524320 | tf_op jit(solution)/shard_map/ppermute | solution.py:34
  99.9 0.1 shard_map.65
  100.0 2.8 %collective-permute-start.6 = (f32[16,16,1024]{2,1,0:T(8,128)S(1)}, f32[16,16,1024]{2,1,0:T(8,128)S(1)}, u32[]{:S(2)}, u32[]{:S(2)}) collective-permute-start(f32[16,16,1024]{2,1,0:T(8,128)S(1)} %bitcast.18), channel_id=1, source_target_pairs={{0,1},{1,0},{2,3},{3,2},{4,5},{5,4},{6,7},{7,6},{8,9},{9,8},{10,11... | collective-permute-start | bytes 3145736 | tf_op jit(solution)/shard_map/ppermute | solution.py:38
  102.8 1.9 %collective-permute-start.8 = (f32[256,512]{1,0:T(8,128)}, f32[256,512]{1,0:T(8,128)}, u32[]{:S(2)}, u32[]{:S(2)}) collective-permute-start(f32[256,512]{1,0:T(8,128)} %bitcast.11), channel_id=1, source_target_pairs={{0,1},{1,0},{2,3},{3,2},{4,5},{5,4},{6,7},{7,6},{8,9},{9,8},{10,11... | collective-permute-start | bytes 1572872 | tf_op jit(solution)/shard_map/ppermute | solution.py:38
  104.8 0.3 collective-permute-done.6.theirs
  105.1 1.0 copy-done
  106.0 1.2 copy-done.1
  107.3 0.1 shard_map.66
  107.4 1.3 %broadcast_select_fusion.1 = (f32[256,512]{1,0:T(8,128)S(1)}, f32[256,512]{1,0:T(8,128)S(1)}) fusion(f32[256,512]{1,0:T(8,128)} %collective-permute-done.8, pred[]{:T(512)S(6)} %eq.7, f32[32,8,512]{2,1,0:T(8,128)} %all-to-all-done.2), kind=kLoop, calls=%fused_computation.19 | loop fusion | flops 262144 | bytes 2097153 | tf_op jit(solution)/shard_map/jit(_where)/select_n | solution.py:198
  108.7 1.1 convolution_add_fusion
  109.8 0.0 all-gather.2.cloned.1.call-done
  109.9 3.0 %fusion.2 = f32[512,768]{1,0:T(8,128)S(1)} fusion(f32[768,1024]{1,0:T(8,128)} %all-gather.2.cloned.1.call-done, f32[512,1024]{1,0:T(8,128)S(1)} %bitcast.17, f32[512]{0:T(512)S(1)} %broadcast_divide_fusion), kind=kOutput, calls=%fused_computation.2 | convolution fusion | flops 1208221696 | bytes 4196352 | tf_op jit(solution)/shard_map/dot_general | solution.py:23
  112.9 2.7 %fusion.4 = f32[512,768]{1,0:T(8,128)} fusion(f32[512,768]{1,0:T(8,128)S(1)} %fusion.2, f32[512,512]{1,0:T(8,128)S(1)} %convolution_add_fusion, f32[768,1024]{1,0:T(8,128)S(1)} %copy-done.6), kind=kOutput, calls=%fused_computation.4 | convolution fusion | flops 1208352768 | bytes 5767168 | tf_op jit(solution)/shard_map/dot_general | solution.py:23
  (27 shorter events, 0.2 us)
Async XLA Ops:
  6.5 103.3 %all-gather.2.cloned.1.call-start = ((), (), s32[]{:S(2)}) async-start(), calls=%async_computation.3 | async-start | bytes 3342336 | tf_op jit(solution)/shard_map/all_gather | solution.py:174
  8.3 21.2 %copy-start.2 = (f32[16,1024]{1,0:T(8,128)S(1)}, f32[16,1024]{1,0:T(8,128)}, u32[]{:S(2)}) copy-start(f32[16,1024]{1,0:T(8,128)} %get-tuple-element.8.own) | copy-start | bytes 196612
  8.4 10.1 %collective-permute-start.7 = (f32[64,1024]{1,0:T(8,128)}, f32[64,1024]{1,0:T(8,128)S(1)}, u32[]{:S(2)}, u32[]{:S(2)}) collective-permute-start(f32[64,1024]{1,0:T(8,128)} %get-tuple-element.10.own), channel_id=1, source_target_pairs={{0,1},{1,0},{2,3},{3,2},{4,5},{5,4},{6,7},{7,6},{8,9},{9,8},{10,11... | collective-permute-start | bytes 786440 | tf_op jit(solution)/shard_map/ppermute | solution.py:38
  18.5 0.7 copy-start.3
  19.1 0.9 copy-start.5
  22.0 28.6 %all-to-all-start = ((f32[32,8,512]{2,1,0:T(8,128)}), f32[32,8,512]{2,1,0:T(8,128)S(1)}, u32[]{:S(2)}, u32[]{:S(2)}) async-start(f32[32,8,512]{2,1,0:T(8,128)} %bitcast.10), calls=%async_computation | async-start | bytes 1048576 | tf_op jit(solution)/shard_map/all_to_all | solution.py:177
  29.6 14.3 %collective-permute-start = (f32[16,1024]{1,0:T(8,128)S(1)}, f32[16,1024]{1,0:T(8,128)S(1)}, u32[]{:S(2)}, u32[]{:S(2)}) collective-permute-start(f32[16,1024]{1,0:T(8,128)S(1)} %copy-done.2), channel_id=1, source_target_pairs={{0,4},{4,8},{8,12},{12,16},{16,20},{20,24},{24,28},{28,0},{1,5},{5... | collective-permute-start | bytes 196616 | tf_op jit(solution)/shard_map/ppermute | solution.py:34
  32.7 11.1 %collective-permute-start.1 = (f32[16,1024]{1,0:T(8,128)S(1)}, f32[16,1024]{1,0:T(8,128)S(1)}, u32[]{:S(2)}, u32[]{:S(2)}) collective-permute-start(f32[16,1024]{1,0:T(8,128)S(1)} %copy-done.2), channel_id=1, source_target_pairs={{0,28},{4,0},{8,4},{12,8},{16,12},{20,16},{24,20},{28,24},{1,29},{... | collective-permute-start | bytes 196616 | tf_op jit(solution)/shard_map/ppermute | solution.py:34
  43.9 14.3 %collective-permute-start.3 = (f32[2,16,1024]{2,1,0:T(8,128)S(1)}, f32[2,16,1024]{2,1,0:T(8,128)S(1)}, u32[]{:S(2)}, u32[]{:S(2)}) collective-permute-start(f32[2,16,1024]{2,1,0:T(8,128)S(1)} %get-tuple-element.13), channel_id=1, source_target_pairs={{0,24},{4,28},{8,0},{12,4},{16,8},{20,12},{24,16},{28,20},{1,25},{... | collective-permute-start | bytes 393224 | tf_op jit(solution)/shard_map/ppermute | solution.py:34
  48.7 13.5 %collective-permute-start.2 = (f32[2,16,1024]{2,1,0:T(8,128)S(1)}, f32[2,16,1024]{2,1,0:T(8,128)S(1)}, u32[]{:S(2)}, u32[]{:S(2)}) collective-permute-start(f32[2,16,1024]{2,1,0:T(8,128)S(1)} %get-tuple-element.14), channel_id=1, source_target_pairs={{0,8},{4,12},{8,16},{12,20},{16,24},{20,28},{24,0},{28,4},{1,9},{5... | collective-permute-start | bytes 393224 | tf_op jit(solution)/shard_map/ppermute | solution.py:34
  51.4 16.1 %all-to-all-start.1 = ((f32[8,8,512]{2,1,0:T(8,128)}), f32[8,8,512]{2,1,0:T(8,128)S(1)}, u32[]{:S(2)}, u32[]{:S(2)}) async-start(f32[8,8,512]{2,1,0:T(8,128)} %broadcast_in_dim.31), calls=%async_computation.1 | async-start | bytes 262144 | tf_op jit(solution)/shard_map/all_to_all | solution.py:30
  58.2 5.8 %collective-permute-start.4 = (f32[16,1024]{1,0:T(8,128)S(1)}, f32[16,1024]{1,0:T(8,128)S(1)}, u32[]{:S(2)}, u32[]{:S(2)}) collective-permute-start(f32[16,1024]{1,0:T(8,128)S(1)} %slice_bitcast_fusion), channel_id=1, source_target_pairs={{0,28},{4,0},{8,4},{12,8},{16,12},{20,16},{24,20},{28,24},{1,29},{... | collective-permute-start | bytes 196616 | tf_op jit(solution)/shard_map/ppermute | solution.py:34
  64.0 40.7 %copy-start.4 = (f32[512]{0:T(512)S(1)}, f32[512]{0:T(512)}, u32[]{:S(2)}) copy-start(f32[512]{0:T(512)} %param.10) | copy-start | bytes 6148
  64.1 35.9 %collective-permute-start.5 = (f32[8,16,1024]{2,1,0:T(8,128)S(1)}, f32[8,16,1024]{2,1,0:T(8,128)S(1)}, u32[]{:S(2)}, u32[]{:S(2)}) collective-permute-start(f32[8,16,1024]{2,1,0:T(8,128)S(1)} %shard_map.64.mine), channel_id=1, source_target_pairs={{0,2},{2,0},{1,3},{3,1},{4,6},{6,4},{5,7},{7,5},{8,10},{10,8},{9,1... | collective-permute-start | bytes 1572872 | tf_op jit(solution)/shard_map/ppermute | solution.py:34
  68.3 34.5 %all-to-all-start.2 = ((f32[32,8,512]{2,1,0:T(8,128)}), f32[32,8,512]{2,1,0:T(8,128)}, u32[]{:S(2)}, u32[]{:S(2)}) async-start(f32[32,8,512]{2,1,0:T(8,128)} %broadcast_in_dim.32), calls=%async_computation.2 | async-start | bytes 1048576 | tf_op jit(solution)/shard_map/all_to_all | solution.py:30
  100.0 5.1 %collective-permute-start.6 = (f32[16,16,1024]{2,1,0:T(8,128)S(1)}, f32[16,16,1024]{2,1,0:T(8,128)S(1)}, u32[]{:S(2)}, u32[]{:S(2)}) collective-permute-start(f32[16,16,1024]{2,1,0:T(8,128)S(1)} %bitcast.18), channel_id=1, source_target_pairs={{0,1},{1,0},{2,3},{3,2},{4,5},{5,4},{6,7},{7,6},{8,9},{9,8},{10,11... | collective-permute-start | bytes 3145736 | tf_op jit(solution)/shard_map/ppermute | solution.py:38
  102.8 4.6 %collective-permute-start.8 = (f32[256,512]{1,0:T(8,128)}, f32[256,512]{1,0:T(8,128)}, u32[]{:S(2)}, u32[]{:S(2)}) collective-permute-start(f32[256,512]{1,0:T(8,128)} %bitcast.11), channel_id=1, source_target_pairs={{0,1},{1,0},{2,3},{3,2},{4,5},{5,4},{6,7},{7,6},{8,9},{9,8},{10,11... | collective-permute-start | bytes 1572872 | tf_op jit(solution)/shard_map/ppermute | solution.py:38
  105.1 1.0 copy-start
  106.0 1.2 %copy-start.1 = (f32[16,16,1024]{2,1,0:T(8,128)S(1)}, f32[16,16,1024]{2,1,0:T(8,128)}, u32[]{:S(2)}) copy-start(f32[16,16,1024]{2,1,0:T(8,128)} %copy-done) | copy-start | bytes 3145732
  107.4 1.3 %copy-start.7 = (f32[512]{0:T(512)S(1)}, f32[512]{0:T(512)}, u32[]{:S(2)}) copy-start(f32[512]{0:T(512)} %param.11) | copy-start | bytes 6148
  109.9 3.0 %copy-start.6 = (f32[768,1024]{1,0:T(8,128)S(1)}, f32[768,1024]{1,0:T(8,128)}, u32[]{:S(2)}) copy-start(f32[768,1024]{1,0:T(8,128)} %all-gather.2.cloned.1.call-done) | copy-start | bytes 9437188
Sparse Core Ops, SparseCore 0:
  10.4 89.4 all-gather.1

commit v8 on v7

--- a/solution.py
+++ b/solution.py
@@ -7,11 +7,12 @@
 from jax.sharding import PartitionSpec as P
 
 ROW = ("x", "yh")
-COL = ("z", "yl", "core")
+COL = ("zh", "zl", "yl", "core")
 ALL = ROW + COL
-OUTER = ("x", "z")
-INNER = ("yh", "yl")
-SIZES = (4, 4, 8, 2, 2)
+Z = ("zh", "zl")
+OUTER = ("x", "zl", "yl")
+INNER = ("yh", "zh")
+SIZES = (4, 4, 4, 2, 2, 2)
 SIZE_K = 512
 HALF = 256
 HIGHEST = lax.Precision.HIGHEST
@@ -169,29 +170,30 @@
 def local(left, left_cot, right, right_cot, singular, singular_cot):
     core_index = lax.axis_index("core")
     first = core_index == 0
+    at_low = lax.axis_index("yl") == 0
 
     right_pair, left_pair, stacked = pack(left, left_cot, right, right_cot)
     rights = lax.all_gather(right_pair, ROW, axis=0, tiled=True)
+    other = shift(left_pair, "yl", 2, 1)
     got = swap(stacked)
     mine = half_core(core_index, stacked, got, singular)
-    pieces = lax.all_to_all(mine.reshape(32, 8, SIZE_K), OUTER, 0, 0)
-
-    own = left_pair
-    below, above = shift(own, "z", 8, 1), shift(own, "z", 8, -1)
-    mid_below = shift(jnp.stack([below, own]), "z", 8, 2)
-    mid_above = shift(jnp.stack([own, above]), "z", 8, -2)
-    pieces = gather(jnp.sum(pieces, axis=0), INNER, 8)
-    last_above = shift(mid_above[1], "z", 8, -1)
+    pieces = lax.all_to_all(mine.reshape(16, 16, SIZE_K), OUTER, 0, 0)
+
+    own = jnp.stack([jnp.where(at_low, left_pair, other), jnp.where(at_low, other, left_pair)])
+    below, above = shift(own, Z, 8, 1), shift(own, Z, 8, -1)
+
+    mid_below = shift(jnp.stack([below, own]), Z, 8, 2)
+    mid_above = shift(jnp.stack([own, above]), Z, 8, -2)
+    pieces = gather(jnp.sum(pieces, axis=0), INNER, 16)
+    last_above = shift(mid_above[1], Z, 8, -1)
     blocks = (below, own, above, mid_below, mid_above, last_above)
-    line = assemble(place_kernel, (8, 16, 1024), lax.axis_index("z"), *blocks)
-    other_line = shift(line, "yl", 2, 1)
-    plane = assemble(merge_kernel, (8, 2, 16, 1024), lax.axis_index("yl"), line, other_line)
-    plane = plane.reshape(16, 16, 1024)
+    line = assemble(place_kernel, (8, 2, 16, 1024), lax.axis_index(Z), *blocks)
+    line = line.reshape(16, 16, 1024)
     rows = jnp.sum(pieces, axis=0)
-    own_half = gather(rows, OUTER, 32).reshape(HALF, SIZE_K)
-    other_plane = swap(plane)
+    own_half = gather(rows, OUTER, 16).reshape(HALF, SIZE_K)
+    other_line = swap(line)
     lefts = assemble(
-        merge_kernel, (16, 2, 16, 1024), core_index, plane, other_plane
+        merge_kernel, (16, 2, 16, 1024), core_index, line, other_line
     ).reshape(-1, 1024)
     other_half = swap(own_half)
     core = jnp.concatenate(
@@ -200,11 +202,9 @@
 
     inverse = (1.0 / singular)[None, :]
     factor = lefts[:, :SIZE_K]
-    last = ((1,), (1,))
     panel = dot(factor, core, ((1,), (0,)), HIGH) + lefts[:, SIZE_K:] * inverse
-    flat = dot(factor * inverse, rights[:, :SIZE_K], last, HIGH)
-    flat = lax.optimization_barrier(flat)
-    return flat + dot(panel, rights[:, SIZE_K:], last, HIGH)
+    both = jnp.concatenate([factor * inverse, panel], axis=1)
+    return dot(both, rights, ((1,), (1,)), HIGH)
 
 
 def solution(mesh):

time: 123 us -> 121 us (0.984)
  waiting for transfers between devices: 32.2 us -> 20.5 us
  blocking collectives: 0 us -> 11 us
  local copies, waits for them, and re-layouts: 5.37 us -> 3.36 us
  starting transfers between devices: 59 us -> 60.3 us
    ppermute x6, waiting for transfers between devices: 30.5 us -> 17.2 us  [shift(): lax.ppermute(block, axis, [(i, (i + by) % size) for i in range(size)])]
    all_to_all x0 -> x1, blocking collectives: none -> 11 us  [local(): pieces = lax.all_to_all(mine.reshape(16, 16, SIZE_K), OUTER, 0, 0)]
    ppermute x6, starting transfers between devices: 20.6 us -> 28.6 us  [shift(): lax.ppermute(block, axis, [(i, (i + by) % size) for i in range(size)])]
    all_to_all x1 -> x0, starting transfers between devices: 7.54 us -> none  [local(): pieces = lax.all_to_all(mine.reshape(32, 8, SIZE_K), OUTER, 0, 0)]
    unnamed x16 -> x10, local copies, waits for them, and re-layouts: 3.84 us -> 1.65 us
    ppermute x3, starting transfers between devices: 13.5 us -> 15.1 us  [swap(): return lax.ppermute(block, 'core', SWAP)]
    ppermute x3, waiting for transfers between devices: 1.65 us -> 3.24 us  [swap(): return lax.ppermute(block, 'core', SWAP)]
    dot_general x3 -> x2, matrix products: 6.81 us -> 6.9 us  [dot(): lax.dot_general(a, b, (contract, ((), ())), precision=precision, preferre...]
  transfers between devices with their start and end apart: 13 -> 12, of which waited for: 5 -> 8; matrix products, arithmetic and copies ran while one was open for 3% -> 4% of each run, Pallas kernels for 2% -> 1%
where the time goes in v8:
time: 121 us; the launch traced here: 120 us
  starting transfers between devices  60.3 us (50%)
  waiting for transfers between devices  20.5 us (17%)
  between operations  13.7 us (11%)
  blocking collectives  11 us (9%)
  matrix products  6.9 us (6%)
  local copies, waits for them, and re-layouts  3.36 us (3%)
  Pallas kernels  3.12 us (3%)
  other arithmetic  1.58 us (1%)
    ppermute x6, starting transfers between devices, shift(): lax.ppermute(block, axis, [(i, (i + by) % size) for i in range(size)])  28.6 us
    ppermute x6, waiting for transfers between devices, shift(): lax.ppermute(block, axis, [(i, (i + by) % size) for i in range(size)])  17.2 us
    all_to_all x2, starting transfers between devices, gather(): return lax.all_to_all(copies, axis, 0, 0)  16.6 us
    ppermute x3, starting transfers between devices, swap(): return lax.ppermute(block, 'core', SWAP)  15.1 us
    all_to_all x1, blocking collectives, local(): pieces = lax.all_to_all(mine.reshape(16, 16, SIZE_K), OUTER, 0, 0)  11 us
    dot_general x2, matrix products, dot(): lax.dot_general(a, b, (contract, ((), ())), precision=precision, preferre...  6.9 us
    ppermute x3, waiting for transfers between devices, swap(): return lax.ppermute(block, 'core', SWAP)  3.24 us
  transfers between devices with their start and end apart: 12, of which 8 were waited for; matrix products, arithmetic and copies ran while one was open for 4% of the time, Pallas kernels for 1%

profile of v8, /device:TPU:1, one launch (start us, length us, event | category | flops | bytes accessed | tf_op | source)
XLA Modules:
  0.0 120.4 jit_solution(2058886127459813853)
XLA Ops:
  6.5 1.8 %pack.1 = (f32[48,1024]{1,0:T(8,128)}, f32[16,1024]{1,0:T(8,128)}, f32[64,1024]{1,0:T(8,128)}) custom-call(f32[16,512]{1,0:T(8,128)} %left.1, f32[16,512]{1,0:T(8,128)} %left_cot.1, f32[48,512]{1,0:T(8,128)} %right.1, f32[48,512]{1,0:T(8,128)} %right_cot.1), custom_call_target="tpu_custom_call" | custom-call | bytes 1048576 | tf_op jit(solution)/shard_map/pack/pallas_call | solution.py:71
  8.4 8.7 %collective-permute-start.7 = (f32[64,1024]{1,0:T(8,128)}, f32[64,1024]{1,0:T(8,128)S(1)}, u32[]{:S(2)}, u32[]{:S(2)}) collective-permute-start(f32[64,1024]{1,0:T(8,128)} %get-tuple-element.9.own), channel_id=1, source_target_pairs={{0,1},{1,0},{2,3},{3,2},{4,5},{5,4},{6,7},{7,6},{8,9},{9,8},{10,11... | collective-permute-start | bytes 786440 | tf_op jit(solution)/shard_map/ppermute | solution.py:39
  17.1 1.3 %collective-permute-done.7.got = f32[64,1024]{1,0:T(8,128)S(1)} collective-permute-done((f32[64,1024]{1,0:T(8,128)}, f32[64,1024]{1,0:T(8,128)S(1)}, u32[]{:S(2)}, u32[]{:S(2)}) %collective-permute-start.7) | collective-permute-done | bytes 262176 | tf_op jit(solution)/shard_map/ppermute | solution.py:39
  18.5 0.7 copy-done
  19.1 0.9 copy-done.2
  20.1 1.1 half_core.1
  21.2 11.0 %all_to_all.15 = f32[16,16,512]{2,1,0:T(8,128)S(1)} all-to-all(f32[16,16,512]{2,1,0:T(8,128)S(1)} %bitcast.26), channel_id=1, replica_groups=mesh['x'=4,'yh'=4,'zh'=4,'zl'=2,'yl'=2,'core'=2] {'x','zl','yl'}, dimensions={0} | all-to-all | bytes 1048576 | tf_op jit(solution)/shard_map/all_to_all | solution.py:180
  32.2 0.9 broadcast_in_dim.31
  33.1 12.4 %all-to-all-start.1 = ((f32[16,16,512]{2,1,0:T(8,128)}), f32[16,16,512]{2,1,0:T(8,128)S(1)}, u32[]{:S(2)}, u32[]{:S(2)}) async-start(f32[16,16,512]{2,1,0:T(8,128)} %broadcast_in_dim.31), calls=%async_computation.1 | async-start | bytes 1048576 | tf_op jit(solution)/shard_map/all_to_all | solution.py:31
  45.5 3.7 %collective-permute-start = (f32[16,1024]{1,0:T(8,128)S(1)}, f32[16,1024]{1,0:T(8,128)S(1)}, u32[]{:S(2)}, u32[]{:S(2)}) collective-permute-start(f32[16,1024]{1,0:T(8,128)S(1)} %copy-done.3), channel_id=1, source_target_pairs={{0,2},{2,0},{1,3},{3,1},{4,6},{6,4},{5,7},{7,5},{8,10},{10,8},{9,1... | collective-permute-start | bytes 196616 | tf_op jit(solution)/shard_map/ppermute | solution.py:35
  49.2 11.0 %collective-permute-done = f32[16,1024]{1,0:T(8,128)S(1)} collective-permute-done((f32[16,1024]{1,0:T(8,128)S(1)}, f32[16,1024]{1,0:T(8,128)S(1)}, u32[]{:S(2)}, u32[]{:S(2)}) %collective-permute-start) | collective-permute-done | bytes 65568 | tf_op jit(solution)/shard_map/ppermute | solution.py:35
  60.2 5.6 %collective-permute-start.1 = (f32[2,16,1024]{2,1,0:T(8,128)S(1)}, f32[2,16,1024]{2,1,0:T(8,128)S(1)}, u32[]{:S(2)}, u32[]{:S(2)}) collective-permute-start(f32[2,16,1024]{2,1,0:T(8,128)S(1)} %get-tuple-element.16.own), channel_id=1, source_target_pairs={{0,4},{4,8},{8,12},{12,16},{16,20},{20,24},{24,28},{28,0},{1,5},{5... | collective-permute-start | bytes 393224 | tf_op jit(solution)/shard_map/ppermute | solution.py:35
  65.8 3.9 %collective-permute-start.2 = (f32[2,16,1024]{2,1,0:T(8,128)S(1)}, f32[2,16,1024]{2,1,0:T(8,128)S(1)}, u32[]{:S(2)}, u32[]{:S(2)}) collective-permute-start(f32[2,16,1024]{2,1,0:T(8,128)S(1)} %get-tuple-element.16.own), channel_id=1, source_target_pairs={{0,28},{4,0},{8,4},{12,8},{16,12},{20,16},{24,20},{28,24},{1,29},{... | collective-permute-start | bytes 393224 | tf_op jit(solution)/shard_map/ppermute | solution.py:35
  69.7 1.0 collective-permute-done.1.below
  70.7 1.2 collective-permute-done.2.above
  72.0 5.1 %collective-permute-start.4 = (f32[2,2,16,1024]{3,2,1,0:T(8,128)S(1)}, f32[2,2,16,1024]{3,2,1,0:T(8,128)S(1)}, u32[]{:S(2)}, u32[]{:S(2)}) collective-permute-start(f32[2,2,16,1024]{3,2,1,0:T(8,128)S(1)} %get-tuple-element.13), channel_id=1, source_target_pairs={{0,24},{4,28},{8,0},{12,4},{16,8},{20,12},{24,16},{28,20},{1,25},{... | collective-permute-start | bytes 786440 | tf_op jit(solution)/shard_map/ppermute | solution.py:35
  77.1 1.9 %collective-permute-start.3 = (f32[2,2,16,1024]{3,2,1,0:T(8,128)S(1)}, f32[2,2,16,1024]{3,2,1,0:T(8,128)S(1)}, u32[]{:S(2)}, u32[]{:S(2)}) collective-permute-start(f32[2,2,16,1024]{3,2,1,0:T(8,128)S(1)} %get-tuple-element.14), channel_id=1, source_target_pairs={{0,8},{4,12},{8,16},{12,20},{16,24},{20,28},{24,0},{28,4},{1,9},{5... | collective-permute-start | bytes 786440 | tf_op jit(solution)/shard_map/ppermute | solution.py:35
  79.1 0.9 broadcast_in_dim.32
  79.9 4.2 %all-to-all-start.2 = ((f32[16,16,512]{2,1,0:T(8,128)}), f32[16,16,512]{2,1,0:T(8,128)}, u32[]{:S(2)}, u32[]{:S(2)}) async-start(f32[16,16,512]{2,1,0:T(8,128)} %broadcast_in_dim.32), calls=%async_computation.2 | async-start | bytes 1048576 | tf_op jit(solution)/shard_map/all_to_all | solution.py:31
  84.2 0.1 collective-permute-done.4.mid_above
  84.3 8.3 %collective-permute-start.5 = (f32[2,16,1024]{2,1,0:T(8,128)S(1)}, f32[2,16,1024]{2,1,0:T(8,128)S(1)}, u32[]{:S(2)}, u32[]{:S(2)}) collective-permute-start(f32[2,16,1024]{2,1,0:T(8,128)S(1)} %slice_bitcast_fusion), channel_id=1, source_target_pairs={{0,28},{4,0},{8,4},{12,8},{16,12},{20,16},{24,20},{28,24},{1,29},{... | collective-permute-start | bytes 393224 | tf_op jit(solution)/shard_map/ppermute | solution.py:35
  92.7 4.0 %collective-permute-done.5.last_above = f32[2,16,1024]{2,1,0:T(8,128)S(1)} collective-permute-done((f32[2,16,1024]{2,1,0:T(8,128)S(1)}, f32[2,16,1024]{2,1,0:T(8,128)S(1)}, u32[]{:S(2)}, u32[]{:S(2)}) %collective-permute-start.5) | collective-permute-done | bytes 131104 | tf_op jit(solution)/shard_map/ppermute | solution.py:35
  96.6 0.1 shard_map.64
  96.7 4.5 %collective-permute-start.6 = (f32[16,16,1024]{2,1,0:T(8,128)S(1)}, f32[16,16,1024]{2,1,0:T(8,128)S(1)}, u32[]{:S(2)}, u32[]{:S(2)}) collective-permute-start(f32[16,16,1024]{2,1,0:T(8,128)S(1)} %bitcast.22), channel_id=1, source_target_pairs={{0,1},{1,0},{2,3},{3,2},{4,5},{5,4},{6,7},{7,6},{8,9},{9,8},{10,11... | collective-permute-start | bytes 3145736 | tf_op jit(solution)/shard_map/ppermute | solution.py:39
  101.2 1.9 %collective-permute-start.8 = (f32[256,512]{1,0:T(8,128)}, f32[256,512]{1,0:T(8,128)}, u32[]{:S(2)}, u32[]{:S(2)}) collective-permute-start(f32[256,512]{1,0:T(8,128)} %bitcast.12), channel_id=1, source_target_pairs={{0,1},{1,0},{2,3},{3,2},{4,5},{5,4},{6,7},{7,6},{8,9},{9,8},{10,11... | collective-permute-start | bytes 1572872 | tf_op jit(solution)/shard_map/ppermute | solution.py:39
  103.2 0.3 collective-permute-done.6.theirs
  103.5 0.1 shard_map.65
  103.6 0.1 slice_multiply_fusion.1
  103.7 1.6 %collective-permute-done.8 = f32[256,512]{1,0:T(8,128)} collective-permute-done((f32[256,512]{1,0:T(8,128)}, f32[256,512]{1,0:T(8,128)}, u32[]{:S(2)}, u32[]{:S(2)}) %collective-permute-start.8) | collective-permute-done | bytes 524320 | tf_op jit(solution)/shard_map/ppermute | solution.py:39
  105.3 1.3 %broadcast_select_fusion.1 = (f32[256,512]{1,0:T(8,128)S(1)}, f32[256,512]{1,0:T(8,128)S(1)}) fusion(f32[256,512]{1,0:T(8,128)} %collective-permute-done.8, pred[]{:T(512)S(6)} %eq.11, f32[16,16,512]{2,1,0:T(8,128)} %all-to-all-done.2), kind=kLoop, calls=%fused_computation.18 | loop fusion | flops 262144 | bytes 2097153 | tf_op jit(solution)/shard_map/jit(_where)/select_n | solution.py:200
  106.7 1.1 convolution_add_fusion
  107.8 5.8 %fusion = f32[512,768]{1,0:T(8,128)} fusion(f32[768,1024]{1,0:T(8,128)} %all-gather.2.cloned.1.call-done, f32[512,512]{1,0:T(8,128)S(1)} %convolution_add_fusion, f32[512,512]{1,0:T(8,128)S(1)} %slice_multiply_fusion.1), kind=kOutput, calls=%fused_computation | convolution fusion | flops 2416443392 | bytes 6815744 | tf_op jit(solution)/shard_map/dot_general | solution.py:24
  (21 shorter events, 0.2 us)
Async XLA Ops:
  6.5 101.3 %all-gather.2.cloned.1.call-start = ((), (), s32[]{:S(2)}) async-start(), calls=%async_computation.3 | async-start | bytes 3342336 | tf_op jit(solution)/shard_map/all_gather | solution.py:176
  8.4 10.1 %collective-permute-start.7 = (f32[64,1024]{1,0:T(8,128)}, f32[64,1024]{1,0:T(8,128)S(1)}, u32[]{:S(2)}, u32[]{:S(2)}) collective-permute-start(f32[64,1024]{1,0:T(8,128)} %get-tuple-element.9.own), channel_id=1, source_target_pairs={{0,1},{1,0},{2,3},{3,2},{4,5},{5,4},{6,7},{7,6},{8,9},{9,8},{10,11... | collective-permute-start | bytes 786440 | tf_op jit(solution)/shard_map/ppermute | solution.py:39
  18.5 0.7 copy-start
  19.1 0.9 copy-start.2
  21.2 24.2 %copy-start.3 = (f32[16,1024]{1,0:T(8,128)S(1)}, f32[16,1024]{1,0:T(8,128)}, u32[]{:S(2)}) copy-start(f32[16,1024]{1,0:T(8,128)} %get-tuple-element.8) | copy-start | bytes 196612
  33.1 45.9 %all-to-all-start.1 = ((f32[16,16,512]{2,1,0:T(8,128)}), f32[16,16,512]{2,1,0:T(8,128)S(1)}, u32[]{:S(2)}, u32[]{:S(2)}) async-start(f32[16,16,512]{2,1,0:T(8,128)} %broadcast_in_dim.31), calls=%async_computation.1 | async-start | bytes 1048576 | tf_op jit(solution)/shard_map/all_to_all | solution.py:31
  45.5 14.7 %collective-permute-start = (f32[16,1024]{1,0:T(8,128)S(1)}, f32[16,1024]{1,0:T(8,128)S(1)}, u32[]{:S(2)}, u32[]{:S(2)}) collective-permute-start(f32[16,1024]{1,0:T(8,128)S(1)} %copy-done.3), channel_id=1, source_target_pairs={{0,2},{2,0},{1,3},{3,1},{4,6},{6,4},{5,7},{7,5},{8,10},{10,8},{9,1... | collective-permute-start | bytes 196616 | tf_op jit(solution)/shard_map/ppermute | solution.py:35
  60.2 10.5 %collective-permute-start.1 = (f32[2,16,1024]{2,1,0:T(8,128)S(1)}, f32[2,16,1024]{2,1,0:T(8,128)S(1)}, u32[]{:S(2)}, u32[]{:S(2)}) collective-permute-start(f32[2,16,1024]{2,1,0:T(8,128)S(1)} %get-tuple-element.16.own), channel_id=1, source_target_pairs={{0,4},{4,8},{8,12},{12,16},{16,20},{20,24},{24,28},{28,0},{1,5},{5... | collective-permute-start | bytes 393224 | tf_op jit(solution)/shard_map/ppermute | solution.py:35
  65.8 6.1 %collective-permute-start.2 = (f32[2,16,1024]{2,1,0:T(8,128)S(1)}, f32[2,16,1024]{2,1,0:T(8,128)S(1)}, u32[]{:S(2)}, u32[]{:S(2)}) collective-permute-start(f32[2,16,1024]{2,1,0:T(8,128)S(1)} %get-tuple-element.16.own), channel_id=1, source_target_pairs={{0,28},{4,0},{8,4},{12,8},{16,12},{20,16},{24,20},{28,24},{1,29},{... | collective-permute-start | bytes 393224 | tf_op jit(solution)/shard_map/ppermute | solution.py:35
  72.0 12.3 %collective-permute-start.4 = (f32[2,2,16,1024]{3,2,1,0:T(8,128)S(1)}, f32[2,2,16,1024]{3,2,1,0:T(8,128)S(1)}, u32[]{:S(2)}, u32[]{:S(2)}) collective-permute-start(f32[2,2,16,1024]{3,2,1,0:T(8,128)S(1)} %get-tuple-element.13), channel_id=1, source_target_pairs={{0,24},{4,28},{8,0},{12,4},{16,8},{20,12},{24,16},{28,20},{1,25},{... | collective-permute-start | bytes 786440 | tf_op jit(solution)/shard_map/ppermute | solution.py:35
  77.1 15.6 %collective-permute-start.3 = (f32[2,2,16,1024]{3,2,1,0:T(8,128)S(1)}, f32[2,2,16,1024]{3,2,1,0:T(8,128)S(1)}, u32[]{:S(2)}, u32[]{:S(2)}) collective-permute-start(f32[2,2,16,1024]{3,2,1,0:T(8,128)S(1)} %get-tuple-element.14), channel_id=1, source_target_pairs={{0,8},{4,12},{8,16},{12,20},{16,24},{20,28},{24,0},{28,4},{1,9},{5... | collective-permute-start | bytes 786440 | tf_op jit(solution)/shard_map/ppermute | solution.py:35
  79.1 24.1 %copy-start.1 = (f32[512]{0:T(512)S(1)}, f32[512]{0:T(512)}, u32[]{:S(2)}) copy-start(f32[512]{0:T(512)} %param.10) | copy-start | bytes 6148
  79.9 21.3 %all-to-all-start.2 = ((f32[16,16,512]{2,1,0:T(8,128)}), f32[16,16,512]{2,1,0:T(8,128)}, u32[]{:S(2)}, u32[]{:S(2)}) async-start(f32[16,16,512]{2,1,0:T(8,128)} %broadcast_in_dim.32), calls=%async_computation.2 | async-start | bytes 1048576 | tf_op jit(solution)/shard_map/all_to_all | solution.py:31
  84.3 12.3 %collective-permute-start.5 = (f32[2,16,1024]{2,1,0:T(8,128)S(1)}, f32[2,16,1024]{2,1,0:T(8,128)S(1)}, u32[]{:S(2)}, u32[]{:S(2)}) collective-permute-start(f32[2,16,1024]{2,1,0:T(8,128)S(1)} %slice_bitcast_fusion), channel_id=1, source_target_pairs={{0,28},{4,0},{8,4},{12,8},{16,12},{20,16},{24,20},{28,24},{1,29},{... | collective-permute-start | bytes 393224 | tf_op jit(solution)/shard_map/ppermute | solution.py:35
  96.7 6.7 %collective-permute-start.6 = (f32[16,16,1024]{2,1,0:T(8,128)S(1)}, f32[16,16,1024]{2,1,0:T(8,128)S(1)}, u32[]{:S(2)}, u32[]{:S(2)}) collective-permute-start(f32[16,16,1024]{2,1,0:T(8,128)S(1)} %bitcast.22), channel_id=1, source_target_pairs={{0,1},{1,0},{2,3},{3,2},{4,5},{5,4},{6,7},{7,6},{8,9},{9,8},{10,11... | collective-permute-start | bytes 3145736 | tf_op jit(solution)/shard_map/ppermute | solution.py:39
  101.2 4.1 %collective-permute-start.8 = (f32[256,512]{1,0:T(8,128)}, f32[256,512]{1,0:T(8,128)}, u32[]{:S(2)}, u32[]{:S(2)}) collective-permute-start(f32[256,512]{1,0:T(8,128)} %bitcast.12), channel_id=1, source_target_pairs={{0,1},{1,0},{2,3},{3,2},{4,5},{5,4},{6,7},{7,6},{8,9},{9,8},{10,11... | collective-permute-start | bytes 1572872 | tf_op jit(solution)/shard_map/ppermute | solution.py:39
  103.6 3.1 %copy-start.4 = (f32[512]{0:T(512)S(1)}, f32[512]{0:T(512)}, u32[]{:S(2)}) copy-start(f32[512]{0:T(512)} %param.11) | copy-start | bytes 6148
Sparse Core Ops, SparseCore 0:
  10.4 80.2 all-gather.1

commit v9 on v8

--- a/solution.py
+++ b/solution.py
@@ -11,7 +11,6 @@
 ALL = ROW + COL
 Z = ("zh", "zl")
 OUTER = ("x", "zl", "yl")
-INNER = ("yh", "zh")
 SIZES = (4, 4, 4, 2, 2, 2)
 SIZE_K = 512
 HALF = 256
@@ -169,7 +168,6 @@
 
 def local(left, left_cot, right, right_cot, singular, singular_cot):
     core_index = lax.axis_index("core")
-    first = core_index == 0
     at_low = lax.axis_index("yl") == 0
 
     right_pair, left_pair, stacked = pack(left, left_cot, right, right_cot)
@@ -184,7 +182,8 @@
 
     mid_below = shift(jnp.stack([below, own]), Z, 8, 2)
     mid_above = shift(jnp.stack([own, above]), Z, 8, -2)
-    pieces = gather(jnp.sum(pieces, axis=0), INNER, 16)
+    pieces = gather(jnp.sum(pieces, axis=0), "yh", 4)
+    pieces = gather(jnp.sum(pieces, axis=0), "zh", 4)
     last_above = shift(mid_above[1], Z, 8, -1)
     blocks = (below, own, above, mid_below, mid_above, last_above)
     line = assemble(place_kernel, (8, 2, 16, 1024), lax.axis_index(Z), *blocks)
@@ -196,13 +195,14 @@
         merge_kernel, (16, 2, 16, 1024), core_index, line, other_line
     ).reshape(-1, 1024)
     other_half = swap(own_half)
-    core = jnp.concatenate(
-        [jnp.where(first, own_half, other_half), jnp.where(first, other_half, own_half)], axis=0
-    ) + jnp.diag(singular_cot)
+    halves = (own_half[None], other_half[None])
+    core = assemble(merge_kernel, (1, 2, HALF, SIZE_K), core_index, *halves)
+    core = core.reshape(SIZE_K, SIZE_K)
 
     inverse = (1.0 / singular)[None, :]
     factor = lefts[:, :SIZE_K]
-    panel = dot(factor, core, ((1,), (0,)), HIGH) + lefts[:, SIZE_K:] * inverse
+    panel = dot(factor, core, ((1,), (0,)), HIGH) + factor * singular_cot[None, :]
+    panel = panel + lefts[:, SIZE_K:] * inverse
     both = jnp.concatenate([factor * inverse, panel], axis=1)
     return dot(both, rights, ((1,), (1,)), HIGH)
 

time: 121 us -> 115 us (0.950)
  blocking collectives: 11 us -> 0 us
  starting transfers between devices: 60.3 us -> 66.9 us
  waiting for transfers between devices: 20.5 us -> 19 us
  other arithmetic: 1.58 us -> 0.27 us
    all_to_all x1 -> x0, blocking collectives: 11 us -> none  [local(): pieces = lax.all_to_all(mine.reshape(16, 16, SIZE_K), OUTER, 0, 0)]
    ppermute x3, starting transfers between devices: 15.1 us -> 23.6 us  [swap(): return lax.ppermute(block, 'core', SWAP)]
    ppermute x6, waiting for transfers between devices: 17.2 us -> 9.27 us  [shift(): lax.ppermute(block, axis, [(i, (i + by) % size) for i in range(size)])]
    all_to_all x2 -> x3, waiting for transfers between devices: 0.01 us -> 6.77 us  [gather(): return lax.all_to_all(copies, axis, 0, 0)]
    all_to_all x0 -> x1, starting transfers between devices: none -> 3.57 us  [local(): pieces = lax.all_to_all(mine.reshape(16, 16, SIZE_K), OUTER, 0, 0)]
    ppermute x6, starting transfers between devices: 28.6 us -> 25.5 us  [shift(): lax.ppermute(block, axis, [(i, (i + by) % size) for i in range(size)])]
    all_to_all x2 -> x3, starting transfers between devices: 16.6 us -> 14.3 us  [gather(): return lax.all_to_all(copies, axis, 0, 0)]
    select_n x1 -> x0, other arithmetic: 1.29 us -> none  [local(): jnp.where(first, own_half, other_half)]
  transfers between devices with their start and end apart: 12 -> 14, of which waited for: 8 -> 7; matrix products, arithmetic and copies ran while one was open for 4% -> 3% of each run, Pallas kernels for 1% -> 2%
where the time goes in v9:
time: 115 us
  starting transfers between devices  66.9 us (58%)
  waiting for transfers between devices  19 us (17%)
  between operations  13.7 us (12%)
  matrix products  6.93 us (6%)
  Pallas kernels  3.98 us (3%)
  local copies, waits for them, and re-layouts  3.84 us (3%)
    ppermute x6, starting transfers between devices, shift(): lax.ppermute(block, axis, [(i, (i + by) % size) for i in range(size)])  25.5 us
    ppermute x3, starting transfers between devices, swap(): return lax.ppermute(block, 'core', SWAP)  23.6 us
    all_to_all x3, starting transfers between devices, gather(): return lax.all_to_all(copies, axis, 0, 0)  14.3 us
    ppermute x6, waiting for transfers between devices, shift(): lax.ppermute(block, axis, [(i, (i + by) % size) for i in range(size)])  9.27 us
    dot_general x2, matrix products, dot(): lax.dot_general(a, b, (contract, ((), ())), precision=precision, preferre...  6.93 us
    all_to_all x3, waiting for transfers between devices, gather(): return lax.all_to_all(copies, axis, 0, 0)  6.77 us
    all_to_all x1, starting transfers between devices, local(): pieces = lax.all_to_all(mine.reshape(16, 16, SIZE_K), OUTER, 0, 0)  3.57 us
    ppermute x3, waiting for transfers between devices, swap(): return lax.ppermute(block, 'core', SWAP)  2.91 us
  transfers between devices with their start and end apart: 14, of which 7 were waited for; matrix products, arithmetic and copies ran while one was open for 3% of the time, Pallas kernels for 2%

profile of v9, /device:TPU:1, one launch (start us, length us, event | category | flops | bytes accessed | tf_op | source)
XLA Modules:
  0.0 114.5 jit_solution(18348176771794584452)
XLA Ops:
  6.5 1.8 %pack.1 = (f32[48,1024]{1,0:T(8,128)}, f32[16,1024]{1,0:T(8,128)}, f32[64,1024]{1,0:T(8,128)}) custom-call(f32[16,512]{1,0:T(8,128)} %left.1, f32[16,512]{1,0:T(8,128)} %left_cot.1, f32[48,512]{1,0:T(8,128)} %right.1, f32[48,512]{1,0:T(8,128)} %right_cot.1), custom_call_target="tpu_custom_call" | custom-call | bytes 1048576 | tf_op jit(solution)/shard_map/pack/pallas_call | solution.py:70
  8.4 8.7 %collective-permute-start.7 = (f32[64,1024]{1,0:T(8,128)}, f32[64,1024]{1,0:T(8,128)S(1)}, u32[]{:S(2)}, u32[]{:S(2)}) collective-permute-start(f32[64,1024]{1,0:T(8,128)} %get-tuple-element.9.own), channel_id=1, source_target_pairs={{0,1},{1,0},{2,3},{3,2},{4,5},{5,4},{6,7},{7,6},{8,9},{9,8},{10,11... | collective-permute-start | bytes 786440 | tf_op jit(solution)/shard_map/ppermute | solution.py:38
  17.1 1.3 %collective-permute-done.7.got = f32[64,1024]{1,0:T(8,128)S(1)} collective-permute-done((f32[64,1024]{1,0:T(8,128)}, f32[64,1024]{1,0:T(8,128)S(1)}, u32[]{:S(2)}, u32[]{:S(2)}) %collective-permute-start.7) | collective-permute-done | bytes 262176 | tf_op jit(solution)/shard_map/ppermute | solution.py:38
  18.5 0.7 copy-done
  19.1 0.9 copy-done.2
  20.1 1.9 %half_core.1 = f32[256,512]{1,0:T(8,128)} custom-call(s32[1]{0:T(128)} %bitcast.index.core_index, f32[64,1024]{1,0:T(8,128)S(1)} %copy-done.2, f32[64,1024]{1,0:T(8,128)S(1)} %collective-permute-done.7.got, f32[1,512]{1,0:T(1,128)S(1)} %bitcast.32), custom_call_target="tpu_custom_call" | custom-call | flops 603979776 | bytes 1048576 | tf_op jit(solution)/shard_map/half_core/pallas_call | solution.py:126
  22.0 3.6 %all-to-all-start = ((f32[16,16,512]{2,1,0:T(8,128)}), f32[16,16,512]{2,1,0:T(8,128)S(1)}, u32[]{:S(2)}, u32[]{:S(2)}) async-start(f32[16,16,512]{2,1,0:T(8,128)} %bitcast.11), calls=%async_computation | async-start | bytes 1048576 | tf_op jit(solution)/shard_map/all_to_all | solution.py:178
  25.6 3.1 %collective-permute-start = (f32[16,1024]{1,0:T(8,128)S(1)}, f32[16,1024]{1,0:T(8,128)S(1)}, u32[]{:S(2)}, u32[]{:S(2)}) collective-permute-start(f32[16,1024]{1,0:T(8,128)S(1)} %copy-done.3), channel_id=1, source_target_pairs={{0,2},{2,0},{1,3},{3,1},{4,6},{6,4},{5,7},{7,5},{8,10},{10,8},{9,1... | collective-permute-start | bytes 196616 | tf_op jit(solution)/shard_map/ppermute | solution.py:34
  28.8 5.8 %collective-permute-done = f32[16,1024]{1,0:T(8,128)S(1)} collective-permute-done((f32[16,1024]{1,0:T(8,128)S(1)}, f32[16,1024]{1,0:T(8,128)S(1)}, u32[]{:S(2)}, u32[]{:S(2)}) %collective-permute-start) | collective-permute-done | bytes 65568 | tf_op jit(solution)/shard_map/ppermute | solution.py:34
  34.7 3.0 %collective-permute-start.1 = (f32[2,16,1024]{2,1,0:T(8,128)S(1)}, f32[2,16,1024]{2,1,0:T(8,128)S(1)}, u32[]{:S(2)}, u32[]{:S(2)}) collective-permute-start(f32[2,16,1024]{2,1,0:T(8,128)S(1)} %get-tuple-element.14.own), channel_id=1, source_target_pairs={{0,4},{4,8},{8,12},{12,16},{16,20},{20,24},{24,28},{28,0},{1,5},{5... | collective-permute-start | bytes 393224 | tf_op jit(solution)/shard_map/ppermute | solution.py:34
  37.7 8.6 %collective-permute-start.2 = (f32[2,16,1024]{2,1,0:T(8,128)S(1)}, f32[2,16,1024]{2,1,0:T(8,128)S(1)}, u32[]{:S(2)}, u32[]{:S(2)}) collective-permute-start(f32[2,16,1024]{2,1,0:T(8,128)S(1)} %get-tuple-element.14.own), channel_id=1, source_target_pairs={{0,28},{4,0},{8,4},{12,8},{16,12},{20,16},{24,20},{28,24},{1,29},{... | collective-permute-start | bytes 393224 | tf_op jit(solution)/shard_map/ppermute | solution.py:34
  46.4 0.7 broadcast_in_dim.8
  47.0 5.8 %all-to-all-start.1 = ((f32[4,16,512]{2,1,0:T(8,128)}), f32[4,16,512]{2,1,0:T(8,128)S(1)}, u32[]{:S(2)}, u32[]{:S(2)}) async-start(f32[4,16,512]{2,1,0:T(8,128)} %broadcast_in_dim.8), calls=%async_computation.1 | async-start | bytes 262144 | tf_op jit(solution)/shard_map/all_to_all | solution.py:30
  52.9 3.5 %collective-permute-start.4 = (f32[2,2,16,1024]{3,2,1,0:T(8,128)S(1)}, f32[2,2,16,1024]{3,2,1,0:T(8,128)S(1)}, u32[]{:S(2)}, u32[]{:S(2)}) collective-permute-start(f32[2,2,16,1024]{3,2,1,0:T(8,128)S(1)} %get-tuple-element.11), channel_id=1, source_target_pairs={{0,24},{4,28},{8,0},{12,4},{16,8},{20,12},{24,16},{28,20},{1,25},{... | collective-permute-start | bytes 786440 | tf_op jit(solution)/shard_map/ppermute | solution.py:34
  56.4 3.7 %all-to-all-done.1 = f32[4,16,512]{2,1,0:T(8,128)S(1)} async-done(((f32[4,16,512]{2,1,0:T(8,128)}), f32[4,16,512]{2,1,0:T(8,128)S(1)}, u32[]{:S(2)}, u32[]{:S(2)}) %all-to-all-start.1) | async-done | bytes 131104 | tf_op jit(solution)/shard_map/all_to_all | solution.py:30
  60.1 0.7 broadcast_in_dim.9
  60.8 3.5 %all-to-all-start.2 = ((f32[4,16,512]{2,1,0:T(8,128)}), f32[4,16,512]{2,1,0:T(8,128)S(1)}, u32[]{:S(2)}, u32[]{:S(2)}) async-start(f32[4,16,512]{2,1,0:T(8,128)} %broadcast_in_dim.9), calls=%async_computation.2 | async-start | bytes 262144 | tf_op jit(solution)/shard_map/all_to_all | solution.py:30
  64.3 4.4 %collective-permute-start.3 = (f32[2,2,16,1024]{3,2,1,0:T(8,128)S(1)}, f32[2,2,16,1024]{3,2,1,0:T(8,128)S(1)}, u32[]{:S(2)}, u32[]{:S(2)}) collective-permute-start(f32[2,2,16,1024]{3,2,1,0:T(8,128)S(1)} %get-tuple-element.12), channel_id=1, source_target_pairs={{0,8},{4,12},{8,16},{12,20},{16,24},{20,28},{24,0},{28,4},{1,9},{5... | collective-permute-start | bytes 786440 | tf_op jit(solution)/shard_map/ppermute | solution.py:34
  68.7 3.0 %all-to-all-done.2 = f32[4,16,512]{2,1,0:T(8,128)S(1)} async-done(((f32[4,16,512]{2,1,0:T(8,128)}), f32[4,16,512]{2,1,0:T(8,128)S(1)}, u32[]{:S(2)}, u32[]{:S(2)}) %all-to-all-start.2) | async-done | bytes 131104 | tf_op jit(solution)/shard_map/all_to_all | solution.py:30
  71.7 0.9 broadcast_in_dim.10
  72.6 5.0 %all-to-all-start.3 = ((f32[16,16,512]{2,1,0:T(8,128)}), f32[16,16,512]{2,1,0:T(8,128)S(1)}, u32[]{:S(2)}, u32[]{:S(2)}) async-start(f32[16,16,512]{2,1,0:T(8,128)} %broadcast_in_dim.10), calls=%async_computation.3 | async-start | bytes 1048576 | tf_op jit(solution)/shard_map/all_to_all | solution.py:30
  77.6 2.8 %collective-permute-start.5 = (f32[2,16,1024]{2,1,0:T(8,128)S(1)}, f32[2,16,1024]{2,1,0:T(8,128)S(1)}, u32[]{:S(2)}, u32[]{:S(2)}) collective-permute-start(f32[2,16,1024]{2,1,0:T(8,128)S(1)} %slice_bitcast_fusion), channel_id=1, source_target_pairs={{0,28},{4,0},{8,4},{12,8},{16,12},{20,16},{24,20},{28,24},{1,29},{... | collective-permute-start | bytes 393224 | tf_op jit(solution)/shard_map/ppermute | solution.py:34
  80.4 3.4 %collective-permute-done.5.last_above = f32[2,16,1024]{2,1,0:T(8,128)S(1)} collective-permute-done((f32[2,16,1024]{2,1,0:T(8,128)S(1)}, f32[2,16,1024]{2,1,0:T(8,128)S(1)}, u32[]{:S(2)}, u32[]{:S(2)}) %collective-permute-start.5) | collective-permute-done | bytes 131104 | tf_op jit(solution)/shard_map/ppermute | solution.py:34
  83.9 0.1 shard_map.64
  83.9 12.9 %collective-permute-start.6 = (f32[16,16,1024]{2,1,0:T(8,128)S(1)}, f32[16,16,1024]{2,1,0:T(8,128)S(1)}, u32[]{:S(2)}, u32[]{:S(2)}) collective-permute-start(f32[16,16,1024]{2,1,0:T(8,128)S(1)} %bitcast.24), channel_id=1, source_target_pairs={{0,1},{1,0},{2,3},{3,2},{4,5},{5,4},{6,7},{7,6},{8,9},{9,8},{10,11... | collective-permute-start | bytes 3145736 | tf_op jit(solution)/shard_map/ppermute | solution.py:38
  96.9 1.9 %collective-permute-start.8 = (f32[256,512]{1,0:T(8,128)S(1)}, f32[256,512]{1,0:T(8,128)S(1)}, u32[]{:S(2)}, u32[]{:S(2)}) collective-permute-start(f32[256,512]{1,0:T(8,128)S(1)} %bitcast.27), channel_id=1, source_target_pairs={{0,1},{1,0},{2,3},{3,2},{4,5},{5,4},{6,7},{7,6},{8,9},{9,8},{10,11... | collective-permute-start | bytes 1572872 | tf_op jit(solution)/shard_map/ppermute | solution.py:38
  98.8 0.3 collective-permute-done.6.theirs
  99.1 0.1 shard_map.65
  99.3 0.1 slice_multiply_fusion.1
  99.4 1.3 %collective-permute-done.8 = f32[256,512]{1,0:T(8,128)S(1)} collective-permute-done((f32[256,512]{1,0:T(8,128)S(1)}, f32[256,512]{1,0:T(8,128)S(1)}, u32[]{:S(2)}, u32[]{:S(2)}) %collective-permute-start.8) | collective-permute-done | bytes 524320 | tf_op jit(solution)/shard_map/ppermute | solution.py:38
  100.7 1.2 %fusion.4 = f32[512,512]{1,0:T(8,128)S(1)} fusion(f32[512,512]{1,0:T(8,128)S(1)} %bitcast.26, f32[512,1024]{1,0:T(8,128)S(1)} %bitcast.23, f32[512]{0:T(512)S(1)} %copy-done.4, f32[512]{0:T(512)S(1)} %broadcast_divide_fusion), kind=kOutput, calls=%fused_computation.5 | convolution fusion | flops 806354944 | bytes 5246976 | tf_op jit(solution)/shard_map/dot_general | solution.py:23
  102.0 5.8 %fusion = f32[512,768]{1,0:T(8,128)} fusion(f32[768,1024]{1,0:T(8,128)} %all-gather.2.cloned.1.call-done, f32[512,512]{1,0:T(8,128)S(1)} %fusion.4, f32[512,512]{1,0:T(8,128)S(1)} %slice_multiply_fusion.1), kind=kOutput, calls=%fused_computation | convolution fusion | flops 2416443392 | bytes 6815744 | tf_op jit(solution)/shard_map/dot_general | solution.py:23
  (26 shorter events, 0.3 us)
Async XLA Ops:
  6.5 95.4 %all-gather.2.cloned.1.call-start = ((), (), s32[]{:S(2)}) async-start(), calls=%async_computation.4 | async-start | bytes 3342336 | tf_op jit(solution)/shard_map/all_gather | solution.py:174
  8.3 17.3 %copy-start.3 = (f32[16,1024]{1,0:T(8,128)S(1)}, f32[16,1024]{1,0:T(8,128)}, u32[]{:S(2)}) copy-start(f32[16,1024]{1,0:T(8,128)} %get-tuple-element.8) | copy-start | bytes 196612
  8.4 10.1 %collective-permute-start.7 = (f32[64,1024]{1,0:T(8,128)}, f32[64,1024]{1,0:T(8,128)S(1)}, u32[]{:S(2)}, u32[]{:S(2)}) collective-permute-start(f32[64,1024]{1,0:T(8,128)} %get-tuple-element.9.own), channel_id=1, source_target_pairs={{0,1},{1,0},{2,3},{3,2},{4,5},{5,4},{6,7},{7,6},{8,9},{9,8},{10,11... | collective-permute-start | bytes 786440 | tf_op jit(solution)/shard_map/ppermute | solution.py:38
  18.5 0.7 copy-start
  19.1 0.9 copy-start.2
  22.0 24.3 %all-to-all-start = ((f32[16,16,512]{2,1,0:T(8,128)}), f32[16,16,512]{2,1,0:T(8,128)S(1)}, u32[]{:S(2)}, u32[]{:S(2)}) async-start(f32[16,16,512]{2,1,0:T(8,128)} %bitcast.11), calls=%async_computation | async-start | bytes 1048576 | tf_op jit(solution)/shard_map/all_to_all | solution.py:178
  25.6 9.0 %collective-permute-start = (f32[16,1024]{1,0:T(8,128)S(1)}, f32[16,1024]{1,0:T(8,128)S(1)}, u32[]{:S(2)}, u32[]{:S(2)}) collective-permute-start(f32[16,1024]{1,0:T(8,128)S(1)} %copy-done.3), channel_id=1, source_target_pairs={{0,2},{2,0},{1,3},{3,1},{4,6},{6,4},{5,7},{7,5},{8,10},{10,8},{9,1... | collective-permute-start | bytes 196616 | tf_op jit(solution)/shard_map/ppermute | solution.py:34
  34.7 18.2 %collective-permute-start.1 = (f32[2,16,1024]{2,1,0:T(8,128)S(1)}, f32[2,16,1024]{2,1,0:T(8,128)S(1)}, u32[]{:S(2)}, u32[]{:S(2)}) collective-permute-start(f32[2,16,1024]{2,1,0:T(8,128)S(1)} %get-tuple-element.14.own), channel_id=1, source_target_pairs={{0,4},{4,8},{8,12},{12,16},{16,20},{20,24},{24,28},{28,0},{1,5},{5... | collective-permute-start | bytes 393224 | tf_op jit(solution)/shard_map/ppermute | solution.py:34
  37.7 15.2 %collective-permute-start.2 = (f32[2,16,1024]{2,1,0:T(8,128)S(1)}, f32[2,16,1024]{2,1,0:T(8,128)S(1)}, u32[]{:S(2)}, u32[]{:S(2)}) collective-permute-start(f32[2,16,1024]{2,1,0:T(8,128)S(1)} %get-tuple-element.14.own), channel_id=1, source_target_pairs={{0,28},{4,0},{8,4},{12,8},{16,12},{20,16},{24,20},{28,24},{1,29},{... | collective-permute-start | bytes 393224 | tf_op jit(solution)/shard_map/ppermute | solution.py:34
  47.0 13.1 %all-to-all-start.1 = ((f32[4,16,512]{2,1,0:T(8,128)}), f32[4,16,512]{2,1,0:T(8,128)S(1)}, u32[]{:S(2)}, u32[]{:S(2)}) async-start(f32[4,16,512]{2,1,0:T(8,128)} %broadcast_in_dim.8), calls=%async_computation.1 | async-start | bytes 262144 | tf_op jit(solution)/shard_map/all_to_all | solution.py:30
  52.9 24.7 %collective-permute-start.4 = (f32[2,2,16,1024]{3,2,1,0:T(8,128)S(1)}, f32[2,2,16,1024]{3,2,1,0:T(8,128)S(1)}, u32[]{:S(2)}, u32[]{:S(2)}) collective-permute-start(f32[2,2,16,1024]{3,2,1,0:T(8,128)S(1)} %get-tuple-element.11), channel_id=1, source_target_pairs={{0,24},{4,28},{8,0},{12,4},{16,8},{20,12},{24,16},{28,20},{1,25},{... | collective-permute-start | bytes 786440 | tf_op jit(solution)/shard_map/ppermute | solution.py:34
  60.8 10.9 %all-to-all-start.2 = ((f32[4,16,512]{2,1,0:T(8,128)}), f32[4,16,512]{2,1,0:T(8,128)S(1)}, u32[]{:S(2)}, u32[]{:S(2)}) async-start(f32[4,16,512]{2,1,0:T(8,128)} %broadcast_in_dim.9), calls=%async_computation.2 | async-start | bytes 262144 | tf_op jit(solution)/shard_map/all_to_all | solution.py:30
  64.3 34.5 %copy-start.1 = (f32[512]{0:T(512)S(1)}, f32[512]{0:T(512)}, u32[]{:S(2)}) copy-start(f32[512]{0:T(512)} %param.10) | copy-start | bytes 6148
  64.3 16.1 %collective-permute-start.3 = (f32[2,2,16,1024]{3,2,1,0:T(8,128)S(1)}, f32[2,2,16,1024]{3,2,1,0:T(8,128)S(1)}, u32[]{:S(2)}, u32[]{:S(2)}) collective-permute-start(f32[2,2,16,1024]{3,2,1,0:T(8,128)S(1)} %get-tuple-element.12), channel_id=1, source_target_pairs={{0,8},{4,12},{8,16},{12,20},{16,24},{20,28},{24,0},{28,4},{1,9},{5... | collective-permute-start | bytes 786440 | tf_op jit(solution)/shard_map/ppermute | solution.py:34
  72.6 24.3 %all-to-all-start.3 = ((f32[16,16,512]{2,1,0:T(8,128)}), f32[16,16,512]{2,1,0:T(8,128)S(1)}, u32[]{:S(2)}, u32[]{:S(2)}) async-start(f32[16,16,512]{2,1,0:T(8,128)} %broadcast_in_dim.10), calls=%async_computation.3 | async-start | bytes 1048576 | tf_op jit(solution)/shard_map/all_to_all | solution.py:30
  77.6 6.3 %collective-permute-start.5 = (f32[2,16,1024]{2,1,0:T(8,128)S(1)}, f32[2,16,1024]{2,1,0:T(8,128)S(1)}, u32[]{:S(2)}, u32[]{:S(2)}) collective-permute-start(f32[2,16,1024]{2,1,0:T(8,128)S(1)} %slice_bitcast_fusion), channel_id=1, source_target_pairs={{0,28},{4,0},{8,4},{12,8},{16,12},{20,16},{24,20},{28,24},{1,29},{... | collective-permute-start | bytes 393224 | tf_op jit(solution)/shard_map/ppermute | solution.py:34
  83.9 15.2 %collective-permute-start.6 = (f32[16,16,1024]{2,1,0:T(8,128)S(1)}, f32[16,16,1024]{2,1,0:T(8,128)S(1)}, u32[]{:S(2)}, u32[]{:S(2)}) collective-permute-start(f32[16,16,1024]{2,1,0:T(8,128)S(1)} %bitcast.24), channel_id=1, source_target_pairs={{0,1},{1,0},{2,3},{3,2},{4,5},{5,4},{6,7},{7,6},{8,9},{9,8},{10,11... | collective-permute-start | bytes 3145736 | tf_op jit(solution)/shard_map/ppermute | solution.py:38
  96.9 3.8 %collective-permute-start.8 = (f32[256,512]{1,0:T(8,128)S(1)}, f32[256,512]{1,0:T(8,128)S(1)}, u32[]{:S(2)}, u32[]{:S(2)}) collective-permute-start(f32[256,512]{1,0:T(8,128)S(1)} %bitcast.27), channel_id=1, source_target_pairs={{0,1},{1,0},{2,3},{3,2},{4,5},{5,4},{6,7},{7,6},{8,9},{9,8},{10,11... | collective-permute-start | bytes 1572872 | tf_op jit(solution)/shard_map/ppermute | solution.py:38
  99.2 1.5 %copy-start.4 = (f32[512]{0:T(512)S(1)}, f32[512]{0:T(512)}, u32[]{:S(2)}) copy-start(f32[512]{0:T(512)} %param.11) | copy-start | bytes 6148
Sparse Core Ops, SparseCore 0:
  10.4 80.0 all-gather.1

commit v10 on v9

--- a/solution.py
+++ b/solution.py
@@ -28,10 +28,6 @@
 def gather(block, axis, size):
     copies = jnp.broadcast_to(block[None], (size,) + block.shape)
     return lax.all_to_all(copies, axis, 0, 0)
-
-
-def shift(block, axis, size, by):
-    return lax.ppermute(block, axis, [(i, (i + by) % size) for i in range(size)])
 
 
 def swap(block):
@@ -142,13 +138,6 @@
     )(core_index.reshape(1), own, got, singular.reshape(1, -1))
 
 
-def place_kernel(z, below, own, above, mid_below, mid_above, last_above, out):
-    blocks = [own[...], above[...], mid_above[0], mid_above[1], last_above[...]]
-    blocks = blocks + [mid_below[0], mid_below[1], below[...]]
-    for i, block in enumerate(blocks):
-        out[lax.rem(z[0] + i, 8)] = block
-
-
 def merge_kernel(index, mine, theirs, out):
     out[:, index[0]] = mine[...]
     out[:, 1 - index[0]] = theirs[...]
@@ -168,31 +157,24 @@
 
 def local(left, left_cot, right, right_cot, singular, singular_cot):
     core_index = lax.axis_index("core")
-    at_low = lax.axis_index("yl") == 0
 
     right_pair, left_pair, stacked = pack(left, left_cot, right, right_cot)
     rights = lax.all_gather(right_pair, ROW, axis=0, tiled=True)
-    other = shift(left_pair, "yl", 2, 1)
+    line = gather(left_pair, Z, 8)
     got = swap(stacked)
     mine = half_core(core_index, stacked, got, singular)
     pieces = lax.all_to_all(mine.reshape(16, 16, SIZE_K), OUTER, 0, 0)
-
-    own = jnp.stack([jnp.where(at_low, left_pair, other), jnp.where(at_low, other, left_pair)])
-    below, above = shift(own, Z, 8, 1), shift(own, Z, 8, -1)
-
-    mid_below = shift(jnp.stack([below, own]), Z, 8, 2)
-    mid_above = shift(jnp.stack([own, above]), Z, 8, -2)
+    other_line = lax.ppermute(line, "yl", SWAP)
+    pieces = gather(jnp.sum(pieces, axis=0), "zh", 4)
     pieces = gather(jnp.sum(pieces, axis=0), "yh", 4)
-    pieces = gather(jnp.sum(pieces, axis=0), "zh", 4)
-    last_above = shift(mid_above[1], Z, 8, -1)
-    blocks = (below, own, above, mid_below, mid_above, last_above)
-    line = assemble(place_kernel, (8, 2, 16, 1024), lax.axis_index(Z), *blocks)
-    line = line.reshape(16, 16, 1024)
+    plane = assemble(
+        merge_kernel, (8, 2, 16, 1024), lax.axis_index("yl"), line, other_line
+    ).reshape(16, 16, 1024)
+    other_plane = swap(plane)
     rows = jnp.sum(pieces, axis=0)
     own_half = gather(rows, OUTER, 16).reshape(HALF, SIZE_K)
-    other_line = swap(line)
     lefts = assemble(
-        merge_kernel, (16, 2, 16, 1024), core_index, line, other_line
+        merge_kernel, (16, 2, 16, 1024), core_index, plane, other_plane
     ).reshape(-1, 1024)
     other_half = swap(own_half)
     halves = (own_half[None], other_half[None])

time: 115 us -> 138 us (1.20)
  blocking collectives: 0 us -> 45.6 us
  starting transfers between devices: 66.9 us -> 39.2 us
  waiting for transfers between devices: 19 us -> 24.6 us
    all_to_all x0 -> x2, blocking collectives: none -> 45.6 us  [the longest x1 34.7 us: gather(): return lax.all_to_all(copies, axis, 0, 0)]
    ppermute x6 -> x1, starting transfers between devices: 25.5 us -> 4.43 us  [local(): other_line = lax.ppermute(line, 'yl', SWAP)]
    all_to_all x3, waiting for transfers between devices: 6.77 us -> 22 us  [gather(): return lax.all_to_all(copies, axis, 0, 0)]
    ppermute x6 -> x1, waiting for transfers between devices: 9.27 us -> 0.01 us  [local(): other_line = lax.ppermute(line, 'yl', SWAP)]
    ppermute x3, starting transfers between devices: 23.6 us -> 18.1 us  [swap(): return lax.ppermute(block, 'core', SWAP)]
    all_to_all x1 -> x0, starting transfers between devices: 3.57 us -> none  [local(): pieces = lax.all_to_all(mine.reshape(16, 16, SIZE_K), OUTER, 0, 0)]
    all_to_all x3, starting transfers between devices: 14.3 us -> 16.7 us  [gather(): return lax.all_to_all(copies, axis, 0, 0)]
  transfers between devices with their start and end apart: 14 -> 8, of which waited for: 7 -> 5; matrix products, arithmetic and copies ran while one was open for 3% -> 3% of each run, Pallas kernels for 2% -> 1%
where the time goes in v10:
time: 138 us; the launch traced here: 137 us
  blocking collectives  45.6 us (33%)
  starting transfers between devices  39.2 us (28%)
  waiting for transfers between devices  24.6 us (18%)
  between operations  13.6 us (10%)
  matrix products  6.93 us (5%)
  local copies, waits for them, and re-layouts  4.02 us (3%)
  Pallas kernels  3.19 us (2%)
    all_to_all x1, blocking collectives, gather(): return lax.all_to_all(copies, axis, 0, 0)  34.7 us
    all_to_all x3, waiting for transfers between devices, gather(): return lax.all_to_all(copies, axis, 0, 0)  22 us
    ppermute x3, starting transfers between devices, swap(): return lax.ppermute(block, 'core', SWAP)  18.1 us
    all_to_all x3, starting transfers between devices, gather(): return lax.all_to_all(copies, axis, 0, 0)  16.7 us
    all_to_all x1, blocking collectives, local(): pieces = lax.all_to_all(mine.reshape(16, 16, SIZE_K), OUTER, 0, 0)  10.8 us
    dot_general x2, matrix products, dot(): lax.dot_general(a, b, (contract, ((), ())), precision=precision, preferre...  6.93 us
    ppermute x1, starting transfers between devices, local(): other_line = lax.ppermute(line, 'yl', SWAP)  4.43 us
  transfers between devices with their start and end apart: 8, of which 5 were waited for; matrix products, arithmetic and copies ran while one was open for 3% of the time, Pallas kernels for 1%

profile of v10, /device:TPU:1, one launch (start us, length us, event | category | flops | bytes accessed | tf_op | source)
XLA Modules:
  0.0 137.3 jit_solution(644907488004594079)
XLA Ops:
  6.5 1.8 %pack.1 = (f32[48,1024]{1,0:T(8,128)}, f32[16,1024]{1,0:T(8,128)}, f32[64,1024]{1,0:T(8,128)}) custom-call(f32[16,512]{1,0:T(8,128)} %left.1, f32[16,512]{1,0:T(8,128)} %left_cot.1, f32[48,512]{1,0:T(8,128)} %right.1, f32[48,512]{1,0:T(8,128)} %right_cot.1), custom_call_target="tpu_custom_call" | custom-call | bytes 1048576 | tf_op jit(solution)/shard_map/pack/pallas_call | solution.py:66
  8.3 0.0 all-gather.2.cloned.1.call-update
  8.4 8.7 %collective-permute-start.2 = (f32[64,1024]{1,0:T(8,128)}, f32[64,1024]{1,0:T(8,128)S(1)}, u32[]{:S(2)}, u32[]{:S(2)}) collective-permute-start(f32[64,1024]{1,0:T(8,128)} %get-tuple-element.9.own), channel_id=1, source_target_pairs={{0,1},{1,0},{2,3},{3,2},{4,5},{5,4},{6,7},{7,6},{8,9},{9,8},{10,11... | collective-permute-start | bytes 786440 | tf_op jit(solution)/shard_map/ppermute | solution.py:34
  17.1 1.3 collective-permute-done.2.got
  18.5 0.7 copy-done
  19.1 0.9 copy-done.2
  20.1 1.1 half_core.1
  21.2 10.8 %all_to_all.25 = f32[16,16,512]{2,1,0:T(8,128)S(1)} all-to-all(f32[16,16,512]{2,1,0:T(8,128)S(1)} %bitcast.20), channel_id=1, replica_groups=mesh['x'=4,'yh'=4,'zh'=4,'zl'=2,'yl'=2,'core'=2] {'x','zl','yl'}, dimensions={0} | all-to-all | bytes 1048576 | tf_op jit(solution)/shard_map/all_to_all | solution.py:166
  32.1 0.8 broadcast_in_dim.10
  32.9 9.4 %all-to-all-start = ((f32[8,16,1024]{2,1,0:T(8,128)}), f32[8,16,1024]{2,1,0:T(8,128)S(1)}, u32[]{:S(2)}, u32[]{:S(2)}) async-start(f32[8,16,1024]{2,1,0:T(8,128)} %broadcast_in_dim.10), calls=%async_computation | async-start | bytes 1048576 | tf_op jit(solution)/shard_map/all_to_all | solution.py:30
  42.4 15.7 %all-to-all-done.mine = f32[8,16,1024]{2,1,0:T(8,128)S(1)} async-done(((f32[8,16,1024]{2,1,0:T(8,128)}), f32[8,16,1024]{2,1,0:T(8,128)S(1)}, u32[]{:S(2)}, u32[]{:S(2)}) %all-to-all-start) | async-done | bytes 524320 | tf_op jit(solution)/shard_map/all_to_all | solution.py:30
  58.1 0.7 broadcast_in_dim.11
  58.8 3.3 %all-to-all-start.2 = ((f32[4,16,512]{2,1,0:T(8,128)}), f32[4,16,512]{2,1,0:T(8,128)S(1)}, u32[]{:S(2)}, u32[]{:S(2)}) async-start(f32[4,16,512]{2,1,0:T(8,128)} %broadcast_in_dim.11), calls=%async_computation.2 | async-start | bytes 262144 | tf_op jit(solution)/shard_map/all_to_all | solution.py:30
  62.1 4.4 %collective-permute-start = (f32[8,16,1024]{2,1,0:T(8,128)S(1)}, f32[8,16,1024]{2,1,0:T(8,128)S(1)}, u32[]{:S(2)}, u32[]{:S(2)}) collective-permute-start(f32[8,16,1024]{2,1,0:T(8,128)S(1)} %all-to-all-done.mine), channel_id=1, source_target_pairs={{0,2},{2,0},{1,3},{3,1},{4,6},{6,4},{5,7},{7,5},{8,10},{10,8},{9,1... | collective-permute-start | bytes 1572872 | tf_op jit(solution)/shard_map/ppermute | solution.py:167
  66.5 2.9 %all-to-all-done.2 = f32[4,16,512]{2,1,0:T(8,128)S(1)} async-done(((f32[4,16,512]{2,1,0:T(8,128)}), f32[4,16,512]{2,1,0:T(8,128)S(1)}, u32[]{:S(2)}, u32[]{:S(2)}) %all-to-all-start.2) | async-done | bytes 131104 | tf_op jit(solution)/shard_map/all_to_all | solution.py:30
  69.5 0.0 copy-start.1
  69.5 34.7 %all_to_all.26 = f32[4,16,512]{2,1,0:T(8,128)S(1)} all-to-all(f32[4,16,512]{2,1,0:T(8,128)S(1)} %broadcast_in_dim.12), channel_id=1, replica_groups=mesh['x'=4,'yh'=4,'zh'=4,'zl'=2,'yl'=2,'core'=2] {'yh'}, dimensions={0} | all-to-all | bytes 262144 | tf_op jit(solution)/shard_map/all_to_all | solution.py:30
  104.3 0.9 broadcast_in_dim.13
  105.1 4.0 %all-to-all-start.4 = ((f32[16,16,512]{2,1,0:T(8,128)}), f32[16,16,512]{2,1,0:T(8,128)S(1)}, u32[]{:S(2)}, u32[]{:S(2)}) async-start(f32[16,16,512]{2,1,0:T(8,128)} %broadcast_in_dim.13), calls=%async_computation.4 | async-start | bytes 1048576 | tf_op jit(solution)/shard_map/all_to_all | solution.py:30
  109.1 0.0 collective-permute-done.theirs
  109.1 0.1 shard_map.64
  109.2 3.9 %collective-permute-start.1 = (f32[16,16,1024]{2,1,0:T(8,128)S(1)}, f32[16,16,1024]{2,1,0:T(8,128)S(1)}, u32[]{:S(2)}, u32[]{:S(2)}) collective-permute-start(f32[16,16,1024]{2,1,0:T(8,128)S(1)} %bitcast.14), channel_id=1, source_target_pairs={{0,1},{1,0},{2,3},{3,2},{4,5},{5,4},{6,7},{7,6},{8,9},{9,8},{10,11... | collective-permute-start | bytes 3145736 | tf_op jit(solution)/shard_map/ppermute | solution.py:34
  113.1 3.3 %all-to-all-done.4 = f32[16,16,512]{2,1,0:T(8,128)S(1)} async-done(((f32[16,16,512]{2,1,0:T(8,128)}), f32[16,16,512]{2,1,0:T(8,128)S(1)}, u32[]{:S(2)}, u32[]{:S(2)}) %all-to-all-start.4) | async-done | bytes 524320 | tf_op jit(solution)/shard_map/all_to_all | solution.py:30
  116.4 5.5 %collective-permute-start.3 = (f32[256,512]{1,0:T(8,128)S(1)}, f32[256,512]{1,0:T(8,128)S(1)}, u32[]{:S(2)}, u32[]{:S(2)}) collective-permute-start(f32[256,512]{1,0:T(8,128)S(1)} %bitcast.17), channel_id=1, source_target_pairs={{0,1},{1,0},{2,3},{3,2},{4,5},{5,4},{6,7},{7,6},{8,9},{9,8},{10,11... | collective-permute-start | bytes 1572872 | tf_op jit(solution)/shard_map/ppermute | solution.py:34
  121.9 0.1 shard_map.65
  122.0 0.0 copy-start.4
  122.0 0.1 slice_multiply_fusion.1
  122.2 1.2 collective-permute-done.3
  123.4 0.1 shard_map.66
  123.4 1.2 fusion.4
  124.6 0.0 all-gather.2.cloned.1.call-done
  124.7 5.8 %fusion = f32[512,768]{1,0:T(8,128)} fusion(f32[768,1024]{1,0:T(8,128)} %all-gather.2.cloned.1.call-done, f32[512,512]{1,0:T(8,128)S(1)} %fusion.4, f32[512,512]{1,0:T(8,128)S(1)} %slice_multiply_fusion.1), kind=kOutput, calls=%fused_computation | convolution fusion | flops 2416443392 | bytes 6815744 | tf_op jit(solution)/shard_map/dot_general | solution.py:23
  (13 shorter events, 0.1 us)
Async XLA Ops:
  6.5 118.1 %all-gather.2.cloned.1.call-start = ((), (), s32[]{:S(2)}) async-start(), calls=%async_computation.5 | async-start | bytes 3342336 | tf_op jit(solution)/shard_map/all_gather | solution.py:162
  8.3 23.8 %copy-start.3 = (f32[16,1024]{1,0:T(8,128)S(1)}, f32[16,1024]{1,0:T(8,128)}, u32[]{:S(2)}) copy-start(f32[16,1024]{1,0:T(8,128)} %get-tuple-element.8) | copy-start | bytes 196612
  8.4 10.1 %collective-permute-start.2 = (f32[64,1024]{1,0:T(8,128)}, f32[64,1024]{1,0:T(8,128)S(1)}, u32[]{:S(2)}, u32[]{:S(2)}) collective-permute-start(f32[64,1024]{1,0:T(8,128)} %get-tuple-element.9.own), channel_id=1, source_target_pairs={{0,1},{1,0},{2,3},{3,2},{4,5},{5,4},{6,7},{7,6},{8,9},{9,8},{10,11... | collective-permute-start | bytes 786440 | tf_op jit(solution)/shard_map/ppermute | solution.py:34
  18.5 0.7 copy-start
  19.1 0.9 copy-start.2
  32.9 25.2 %all-to-all-start = ((f32[8,16,1024]{2,1,0:T(8,128)}), f32[8,16,1024]{2,1,0:T(8,128)S(1)}, u32[]{:S(2)}, u32[]{:S(2)}) async-start(f32[8,16,1024]{2,1,0:T(8,128)} %broadcast_in_dim.10), calls=%async_computation | async-start | bytes 1048576 | tf_op jit(solution)/shard_map/all_to_all | solution.py:30
  58.8 10.7 %all-to-all-start.2 = ((f32[4,16,512]{2,1,0:T(8,128)}), f32[4,16,512]{2,1,0:T(8,128)S(1)}, u32[]{:S(2)}, u32[]{:S(2)}) async-start(f32[4,16,512]{2,1,0:T(8,128)} %broadcast_in_dim.11), calls=%async_computation.2 | async-start | bytes 262144 | tf_op jit(solution)/shard_map/all_to_all | solution.py:30
  62.1 47.0 %collective-permute-start = (f32[8,16,1024]{2,1,0:T(8,128)S(1)}, f32[8,16,1024]{2,1,0:T(8,128)S(1)}, u32[]{:S(2)}, u32[]{:S(2)}) collective-permute-start(f32[8,16,1024]{2,1,0:T(8,128)S(1)} %all-to-all-done.mine), channel_id=1, source_target_pairs={{0,2},{2,0},{1,3},{3,1},{4,6},{6,4},{5,7},{7,5},{8,10},{10,8},{9,1... | collective-permute-start | bytes 1572872 | tf_op jit(solution)/shard_map/ppermute | solution.py:167
  69.5 52.3 %copy-start.1 = (f32[512]{0:T(512)S(1)}, f32[512]{0:T(512)}, u32[]{:S(2)}) copy-start(f32[512]{0:T(512)} %param.10) | copy-start | bytes 6148
  105.1 11.3 %all-to-all-start.4 = ((f32[16,16,512]{2,1,0:T(8,128)}), f32[16,16,512]{2,1,0:T(8,128)S(1)}, u32[]{:S(2)}, u32[]{:S(2)}) async-start(f32[16,16,512]{2,1,0:T(8,128)} %broadcast_in_dim.13), calls=%async_computation.4 | async-start | bytes 1048576 | tf_op jit(solution)/shard_map/all_to_all | solution.py:30
  109.2 12.7 %collective-permute-start.1 = (f32[16,16,1024]{2,1,0:T(8,128)S(1)}, f32[16,16,1024]{2,1,0:T(8,128)S(1)}, u32[]{:S(2)}, u32[]{:S(2)}) collective-permute-start(f32[16,16,1024]{2,1,0:T(8,128)S(1)} %bitcast.14), channel_id=1, source_target_pairs={{0,1},{1,0},{2,3},{3,2},{4,5},{5,4},{6,7},{7,6},{8,9},{9,8},{10,11... | collective-permute-start | bytes 3145736 | tf_op jit(solution)/shard_map/ppermute | solution.py:34
  116.4 7.0 %collective-permute-start.3 = (f32[256,512]{1,0:T(8,128)S(1)}, f32[256,512]{1,0:T(8,128)S(1)}, u32[]{:S(2)}, u32[]{:S(2)}) collective-permute-start(f32[256,512]{1,0:T(8,128)S(1)} %bitcast.17), channel_id=1, source_target_pairs={{0,1},{1,0},{2,3},{3,2},{4,5},{5,4},{6,7},{7,6},{8,9},{9,8},{10,11... | collective-permute-start | bytes 1572872 | tf_op jit(solution)/shard_map/ppermute | solution.py:34
  122.0 1.4 %copy-start.4 = (f32[512]{0:T(512)S(1)}, f32[512]{0:T(512)}, u32[]{:S(2)}) copy-start(f32[512]{0:T(512)} %param.11) | copy-start | bytes 6148
Sparse Core Ops, SparseCore 0:
  10.4 85.6 all-gather.1
